TPU v7x, 32 devices: a whole 2x2x4 slice. The times are simulated.
32 devices in a mesh: rep: 4 (over y, x), seq: 8 (over z, core).
Axes of the slice: x: 2, y: 2, z: 4, core: 2. Of those that a mesh axis runs over, the one named last changes fastest.
Arguments:
- inputs: bfloat16 [4, 2048, 1536], P('rep', 'seq'), may hold values from -13 to 13
- segment_ids: int32 [4, 2048], P('rep'), may hold values from 0 to 7, as said below
- valid_mask: int32 [4, 2048], P('rep'), may hold values from 0 to 1, as said below
- input_weight: bfloat16 [1536, 4608], P('seq'), may hold values from -0.15625 to 0.15625
- output_weight: bfloat16 [1536, 1536], P('seq'), may hold values from -0.15625 to 0.15625
- conv_kernel: float32 [16, 6, 11], replicated, may hold values from -1.2 to 1.2
- head_mix: float32 [8, 2, 2], replicated, may hold values from 0.2 to 1
- first_gain: float32 [1536], replicated, may hold values from 0.5 to 1.5
- second_gain: float32 [1536], replicated, may hold values from 0.5 to 1.5
- group_gain: float32 [1536], replicated, may hold values from 0.5 to 1.5
- gate_weight: bfloat16 [1536, 4096], P(None, 'seq'), may hold values from -0.15625 to 0.15625
- up_weight: bfloat16 [1536, 4096], P(None, 'seq'), may hold values from -0.15625 to 0.15625
- down_weight: bfloat16 [4096, 1536], P('seq'), may hold values from -0.09375 to 0.09375
- cotangent: bfloat16 [4, 2048, 1536], P('rep', 'seq'), may hold values from -17 to 17
Outputs:
- output: bfloat16 [4, 2048, 1536], P('rep', 'seq')
- grad_inputs: bfloat16 [4, 2048, 1536], P('rep', 'seq')
- grad_input_weight: float32 [1536, 4608], P('seq')
- grad_output_weight: float32 [1536, 1536], P('seq')
- grad_kernel: float32 [16, 6, 11], replicated
- grad_mix: float32 [8, 2, 2], replicated
- grad_first_gain: float32 [1536], replicated
- grad_second_gain: float32 [1536], replicated
- grad_group_gain: float32 [1536], replicated
- grad_gate: float32 [1536, 4096], P(None, 'seq')
- grad_up: float32 [1536, 4096], P(None, 'seq')
- grad_down: float32 [4096, 1536], P('seq')
Inputs may be any that keep to these rules, and one draw needn't show every extreme that they name: `segment_ids`: segment ids never fall along a sequence and start at 0. The positions k * 1024 to (k + 1) * 1024 - 1 form frame k; every document lies inside one frame, a frame holds one to four documents, the first frame of the first sequence is a single document of exactly 1024 positions, and every frame of the last sequence holds four documents. `valid_mask`: in each frame the positions with 0 form its tail, at most 256 of them; the first frame of the first sequence has none.
All inputs are finite; a program needn't handle non-finite values.
Results may differ from a plain program's by a relative error of at most 0.02.
Values may be sent and summed in bfloat16 or wider, within the bound.
A program may use at most 384 MiB of HBM per device.

v0:
```python
import jax
import jax.numpy as jnp
from jax import lax
from jax.sharding import PartitionSpec as P

REACH = 4


EPS = 1e-06
HIGHEST = lax.Precision.HIGHEST


def from_behind(x, axis, by):
    count = lax.axis_size(axis)
    pairs = [(i, i + by) for i in range(count) if 0 <= i + by < count]
    return lax.ppermute(x, axis, pairs)


def convolve(logits, kernel, rows, columns):
    rim_rows = kernel.shape[1] - 1
    key_span = kernel.shape[2] - 1
    result = jnp.zeros((logits.shape[0], rows, columns), jnp.float32)
    for row_tap in range(kernel.shape[1]):
        for col_tap in range(kernel.shape[2]):
            weight = kernel[:, row_tap, col_tap][:, None, None]
            result = (
                result
                + weight
                * logits[
                    :,
                    rim_rows - row_tap : rim_rows - row_tap + rows,
                    key_span - col_tap : key_span - col_tap + columns,
                ]
            )
    return result


def convolve_back(grads, kernel):
    rim_rows = kernel.shape[1] - 1
    key_span = kernel.shape[2] - 1
    rows = grads.shape[1] + rim_rows
    columns = grads.shape[2] + key_span
    padded = jnp.pad(grads, ((0, 0), (rim_rows, rim_rows), (key_span, key_span)))
    result = jnp.zeros((grads.shape[0], rows, columns), jnp.float32)
    for row_tap in range(kernel.shape[1]):
        for col_tap in range(kernel.shape[2]):
            weight = kernel[:, row_tap, col_tap][:, None, None]
            result = (
                result + weight * padded[:, row_tap : row_tap + rows, col_tap : col_tap + columns]
            )
    return result


def kernel_grads(grads, logits, taps_rows, taps_cols):
    rim_rows = taps_rows - 1
    key_span = taps_cols - 1
    rows = grads.shape[1]
    columns = grads.shape[2]
    entries = []
    for row_tap in range(taps_rows):
        line_sums = []
        for col_tap in range(taps_cols):
            window_part = logits[
                :,
                rim_rows - row_tap : rim_rows - row_tap + rows,
                key_span - col_tap : key_span - col_tap + columns,
            ]
            line_sums.append(jnp.sum(grads * window_part, axis=(1, 2)))
        entries.append(jnp.stack(line_sums, axis=-1))
    return jnp.stack(entries, axis=1)


def attend_group(operands, mask_ext, mask_own, row_valid, score_scale):
    query_g, key_g, value_g, kernel_g, mixing_g = operands
    rows = mask_own.shape[0]
    columns = mask_own.shape[1]
    raw = jnp.einsum("qhd,khd->hqk", query_g, key_g, preferred_element_type=jnp.float32)
    logits = raw * score_scale * mask_ext
    conv = convolve(logits, kernel_g, rows, columns)
    allowed = mask_own > 0
    peak = jnp.max(jnp.where(allowed, conv, -1e30), axis=-1, keepdims=True)
    peak = jnp.where(row_valid > 0, peak, 0.0)
    expo = jnp.where(allowed, jnp.exp(conv - peak), 0.0)
    denom = jnp.sum(expo, axis=-1, keepdims=True) + 1.0 - row_valid
    prob = expo / denom
    mixed = (
        mixing_g[:, 0][:, None, None] * prob[0][None]
        + mixing_g[:, 1][:, None, None] * prob[1][None]
    )
    mixed_low = mixed.astype(jnp.bfloat16)
    result = jnp.einsum("hqk,khd->qhd", mixed_low, value_g, preferred_element_type=jnp.float32)
    return (result, peak + jnp.log(denom))


def attend_group_back(operands, mask_ext, mask_own, score_scale):
    query_g, key_g, value_g, kernel_g, mixing_g, dresult_g, lse_g = operands
    rows = mask_own.shape[0]
    columns = mask_own.shape[1]
    raw = jnp.einsum("qhd,khd->hqk", query_g, key_g, preferred_element_type=jnp.float32)
    logits = raw * score_scale * mask_ext
    conv = convolve(logits, kernel_g, rows, columns)
    allowed = mask_own > 0
    prob = jnp.where(allowed, jnp.exp(conv - lse_g), 0.0)
    mixed = (
        mixing_g[:, 0][:, None, None] * prob[0][None]
        + mixing_g[:, 1][:, None, None] * prob[1][None]
    )
    mixed_low = mixed.astype(jnp.bfloat16)
    dmixed = jnp.einsum("qhd,khd->hqk", dresult_g, value_g, preferred_element_type=jnp.float32)
    dvalue = jnp.einsum("hqk,qhd->khd", mixed_low, dresult_g, preferred_element_type=jnp.float32)
    dmixing = jnp.stack(
        [
            jnp.sum(dmixed * prob[0][None], axis=(1, 2)),
            jnp.sum(dmixed * prob[1][None], axis=(1, 2)),
        ],
        axis=-1,
    )
    dprob = (
        mixing_g[0][:, None, None] * dmixed[0][None] + mixing_g[1][:, None, None] * dmixed[1][None]
    )
    dconv = prob * (dprob - jnp.sum(prob * dprob, axis=-1, keepdims=True))
    dkernel = kernel_grads(dconv, logits, kernel_g.shape[1], kernel_g.shape[2])
    dlogits = convolve_back(dconv, kernel_g) * mask_ext * score_scale
    dquery = jnp.einsum(
        "hqk,khd->qhd",
        dlogits,
        key_g.astype(jnp.float32),
        precision=HIGHEST,
        preferred_element_type=jnp.float32,
    )
    dkey = jnp.einsum(
        "hqk,qhd->khd",
        dlogits,
        query_g.astype(jnp.float32),
        precision=HIGHEST,
        preferred_element_type=jnp.float32,
    )
    return (dquery, dkey, dvalue, dkernel, dmixing)


def rms_scale(values):
    return lax.rsqrt(jnp.mean(values * values, axis=-1, keepdims=True) + EPS)


def norm_back(grad_out, values, inv_scale, gain):
    scaled_grad = grad_out * gain
    inner = jnp.mean(scaled_grad * values, axis=-1, keepdims=True)
    return inv_scale * scaled_grad - values * inv_scale**3 * inner


def on_device(
    inputs,
    segment_ids,
    valid_mask,
    input_weight,
    output_weight,
    conv_kernel,
    head_mix,
    first_gain,
    second_gain,
    group_gain,
    gate_weight,
    up_weight,
    down_weight,
    cotangent,
):
    tokens = inputs.shape[1]
    model_width = inputs.shape[2]
    head_count = conv_kernel.shape[0]
    head_dim = model_width // head_count
    groups = head_mix.shape[0]
    rim_rows = conv_kernel.shape[1] - 1
    half_span = conv_kernel.shape[2] // 2
    window = REACH * tokens
    score_scale = head_dim ** (-0.5)
    seq_rank = lax.axis_index("seq")
    row_start = seq_rank * tokens
    window_start = row_start - (REACH - 1) * tokens
    resid_in = inputs[0].astype(jnp.float32)
    grad_out = cotangent[0].astype(jnp.float32)
    offset = window + half_span
    segment_pad = jnp.concatenate(
        [jnp.full((offset,), -1, jnp.int32), segment_ids[0], jnp.full((half_span,), -1, jnp.int32)]
    )
    valid_pad = jnp.concatenate(
        [jnp.zeros((offset,), jnp.int32), valid_mask[0], jnp.zeros((half_span,), jnp.int32)]
    )
    query_pos = row_start - rim_rows + jnp.arange(tokens + rim_rows, dtype=jnp.int32)
    key_pos = window_start - half_span + jnp.arange(window + 2 * half_span, dtype=jnp.int32)
    query_seg = lax.dynamic_slice_in_dim(
        segment_pad, row_start - rim_rows + offset, tokens + rim_rows
    )
    key_seg = lax.dynamic_slice_in_dim(
        segment_pad, window_start - half_span + offset, window + 2 * half_span
    )
    query_live = lax.dynamic_slice_in_dim(
        valid_pad, row_start - rim_rows + offset, tokens + rim_rows
    )
    key_live = lax.dynamic_slice_in_dim(
        valid_pad, window_start - half_span + offset, window + 2 * half_span
    )
    mask_ext = (
        (query_seg[:, None] == key_seg[None, :])
        & (key_pos[None, :] <= query_pos[:, None])
        & (query_live[:, None] > 0)
        & (key_live[None, :] > 0)
    ).astype(jnp.float32)
    mask_own = mask_ext[rim_rows:, half_span : half_span + window]
    row_valid = query_live[rim_rows:].astype(jnp.float32)[:, None]
    full_input, full_output = (
        lax.all_gather(input_weight, "seq", axis=0, tiled=True),
        lax.all_gather(output_weight, "seq", axis=0, tiled=True),
    )
    first_scale = rms_scale(resid_in)
    normed_in = (resid_in * first_scale * first_gain).astype(jnp.bfloat16)
    projected = jnp.dot(normed_in, full_input, preferred_element_type=jnp.float32).astype(
        jnp.bfloat16
    )
    query = projected[:, :model_width]
    keys_values = projected[:, model_width:]
    query_rim = from_behind(query[tokens - rim_rows :], "seq", 1)
    query_ext = jnp.concatenate([query_rim, query], axis=0)
    pieces = [keys_values]
    for distance in range(1, REACH):
        pieces.append(from_behind(keys_values, "seq", distance))
    window_rows = jnp.concatenate(pieces[::-1], axis=0)
    key_ext = jnp.pad(window_rows[:, :model_width], ((half_span, half_span), (0, 0)))
    value_window = window_rows[:, model_width:]

    def split_heads(values):
        return values.reshape(values.shape[0], groups, 2, head_dim).transpose(1, 0, 2, 3)

    def merge_heads(values):
        return values.transpose(1, 0, 2, 3).reshape(values.shape[1], model_width)

    query_groups = split_heads(query_ext)
    key_groups = split_heads(key_ext)
    value_groups = split_heads(value_window)
    kernel_groups = conv_kernel.reshape(groups, 2, conv_kernel.shape[1], conv_kernel.shape[2])
    result_groups, lse_groups = lax.map(
        lambda operands: attend_group(operands, mask_ext, mask_own, row_valid, score_scale),
        (query_groups, key_groups, value_groups, kernel_groups, head_mix),
    )
    attended = merge_heads(result_groups)
    shaped = attended.reshape(tokens, head_count, head_dim)
    centred = shaped - jnp.mean(shaped, axis=-1, keepdims=True)
    inv_std = lax.rsqrt(jnp.mean(centred * centred, axis=-1, keepdims=True) + EPS)
    unit_heads = centred * inv_std
    unit = unit_heads.reshape(tokens, model_width)
    normed = (unit * group_gain).astype(jnp.bfloat16)
    branch = jnp.dot(normed, full_output, preferred_element_type=jnp.float32)
    resid = resid_in + row_valid * branch
    second_scale = rms_scale(resid)
    normed_mid = (resid * second_scale * second_gain).astype(jnp.bfloat16)
    dmlp = (row_valid * grad_out).astype(jnp.bfloat16)
    contract_rows = (((0,), (0,)), ((), ()))
    inputs_all = lax.all_gather(normed_mid, "seq", axis=0, tiled=True)
    gate = jnp.dot(inputs_all, gate_weight, preferred_element_type=jnp.float32)
    up_proj = jnp.dot(inputs_all, up_weight, preferred_element_type=jnp.float32)
    hidden = (jax.nn.silu(gate) * up_proj).astype(jnp.bfloat16)
    mlp = lax.psum_scatter(
        jnp.dot(hidden, down_weight, preferred_element_type=jnp.float32).astype(jnp.bfloat16),
        "seq",
        scatter_dimension=0,
        tiled=True,
    ).astype(jnp.float32)
    result = resid + row_valid * mlp
    dmlp_all = lax.all_gather(dmlp, "seq", axis=0, tiled=True)
    dhidden = jnp.dot(dmlp_all, down_weight.T, preferred_element_type=jnp.float32)
    sigmoid_gate = jax.nn.sigmoid(gate)
    gate_grad = (dhidden * up_proj * sigmoid_gate * (1.0 + gate * (1.0 - sigmoid_gate))).astype(
        jnp.bfloat16
    )
    up_grad = (dhidden * gate * sigmoid_gate).astype(jnp.bfloat16)
    grad_down = lax.dot_general(hidden, dmlp_all, contract_rows, preferred_element_type=jnp.float32)
    grad_gate = lax.dot_general(
        inputs_all, gate_grad, contract_rows, preferred_element_type=jnp.float32
    )
    grad_up = lax.dot_general(
        inputs_all, up_grad, contract_rows, preferred_element_type=jnp.float32
    )
    dmid = lax.psum_scatter(
        (
            jnp.dot(gate_grad, gate_weight.T, preferred_element_type=jnp.float32)
            + jnp.dot(up_grad, up_weight.T, preferred_element_type=jnp.float32)
        ).astype(jnp.bfloat16),
        "seq",
        scatter_dimension=0,
        tiled=True,
    ).astype(jnp.float32)
    second_part = jnp.sum(dmid * resid * second_scale, axis=0)
    dresid = grad_out + norm_back(dmid, resid, second_scale, second_gain)
    dbranch = (row_valid * dresid).astype(jnp.bfloat16)
    whole_output_grad = lax.dot_general(
        normed, dbranch, contract_rows, preferred_element_type=jnp.float32
    )
    dnormed = jnp.dot(dbranch, full_output.T, preferred_element_type=jnp.float32)
    group_part = jnp.sum(dnormed * unit, axis=0)
    dunit = (dnormed * group_gain).reshape(tokens, head_count, head_dim)
    dshaped = inv_std * (
        dunit
        - jnp.mean(dunit, axis=-1, keepdims=True)
        - unit_heads * jnp.mean(dunit * unit_heads, axis=-1, keepdims=True)
    )
    dattended = dshaped.reshape(tokens, model_width).astype(jnp.bfloat16)
    dquery_g, dkey_g, dvalue_g, dkernel_g, dmixing = lax.map(
        lambda operands: attend_group_back(operands, mask_ext, mask_own, score_scale),
        (
            query_groups,
            key_groups,
            value_groups,
            kernel_groups,
            head_mix,
            split_heads(dattended),
            lse_groups,
        ),
    )
    dquery_ext = merge_heads(dquery_g)
    dkey_window = merge_heads(dkey_g)[half_span : half_span + window]
    dvalue_window = merge_heads(dvalue_g)
    dpair_window = jnp.concatenate([dkey_window, dvalue_window], axis=1)
    dpair = dpair_window[(REACH - 1) * tokens :]
    for distance in range(1, REACH):
        block_first = (REACH - 1 - distance) * tokens
        dpair = dpair + from_behind(
            dpair_window[block_first : block_first + tokens].astype(jnp.bfloat16), "seq", -distance
        ).astype(jnp.float32)
    rim_grad = from_behind(dquery_ext[:rim_rows], "seq", -1)
    dquery_own = dquery_ext[rim_rows:]
    dquery_own = jnp.concatenate(
        [dquery_own[: tokens - rim_rows], dquery_own[tokens - rim_rows :] + rim_grad], axis=0
    )
    dprojected = jnp.concatenate([dquery_own, dpair], axis=1).astype(jnp.bfloat16)
    whole_input_grad = lax.dot_general(
        normed_in, dprojected, contract_rows, preferred_element_type=jnp.float32
    )
    dnormin = jnp.dot(dprojected, full_input.T, preferred_element_type=jnp.float32)
    first_part = jnp.sum(dnormin * resid_in * first_scale, axis=0)
    grad_in = dresid + norm_back(dnormin, resid_in, first_scale, first_gain)
    input_shard, output_shard = (
        lax.psum_scatter(
            whole_input_grad.astype(jnp.bfloat16), "seq", scatter_dimension=0, tiled=True
        ).astype(jnp.float32),
        lax.psum_scatter(
            whole_output_grad.astype(jnp.bfloat16), "seq", scatter_dimension=0, tiled=True
        ).astype(jnp.float32),
    )
    kernel_part = dkernel_g.reshape(head_count, conv_kernel.shape[1], conv_kernel.shape[2])
    grad_kernel, grad_mix, grad_first, grad_second, grad_group = lax.psum(
        (kernel_part, dmixing, first_part, second_part, group_part), ("rep", "seq")
    )
    grad_input_w, grad_output_w, grad_gate, grad_up, grad_down = (
        lax.psum(input_shard.astype(jnp.bfloat16), "rep").astype(jnp.float32),
        lax.psum(output_shard.astype(jnp.bfloat16), "rep").astype(jnp.float32),
        lax.psum(grad_gate.astype(jnp.bfloat16), "rep").astype(jnp.float32),
        lax.psum(grad_up.astype(jnp.bfloat16), "rep").astype(jnp.float32),
        lax.psum(grad_down.astype(jnp.bfloat16), "rep").astype(jnp.float32),
    )
    return (
        result.astype(jnp.bfloat16)[None],
        grad_in.astype(jnp.bfloat16)[None],
        grad_input_w,
        grad_output_w,
        grad_kernel,
        grad_mix,
        grad_first,
        grad_second,
        grad_group,
        grad_gate,
        grad_up,
        grad_down,
    )


def solution(mesh):
    in_specs = (
        P("rep", "seq", None),
        P("rep", None),
        P("rep", None),
        P("seq", None),
        P("seq", None),
        P(),
        P(),
        P(),
        P(),
        P(),
        P(None, "seq"),
        P(None, "seq"),
        P("seq", None),
        P("rep", "seq", None),
    )
    out_specs = (
        P("rep", "seq", None),
        P("rep", "seq", None),
        P("seq", None),
        P("seq", None),
        P(),
        P(),
        P(),
        P(),
        P(),
        P(None, "seq"),
        P(None, "seq"),
        P("seq", None),
    )
    return jax.shard_map(
        on_device, mesh=mesh, in_specs=in_specs, out_specs=out_specs, check_vma=False
    )
```

profile of v0, /device:TPU:25, one launch (start us, length us, event | category | flops | bytes accessed | tf_op | source)
XLA Modules:
  0.0 4014.8 jit_solution(8021908718773649853)
XLA Ops:
  9.3 128.4 %all-gather.5.cloned.1.call-done = bf16[1536,4608]{1,0:T(8,128)(2,1)} async-done(((bf16[192,4608]{1,0:T(8,128)(2,1)}), bf16[1536,4608]{1,0:T(8,128)(2,1)}) %all-gather.5.cloned.1.call-update) | async-done | bytes 14155792 | tf_op jit(solution)/shard_map/all_gather | solution.py:211
  169.0 88.0 %collective-permute-done.1 = bf16[256,3072]{1,0:T(8,128)(2,1)} collective-permute-done((bf16[256,3072]{1,0:T(8,128)(2,1)}, bf16[256,3072]{1,0:T(8,128)(2,1)}, u32[]{:S(2)}, u32[]{:S(2)}) %collective-permute-start.1) | collective-permute-done | bytes 1572896 | tf_op jit(solution)/shard_map/ppermute | solution.py:16
  282.5 341.3 %while.34 = (s32[]{:T(128)}, f32[8,256,2,96]{1,3,2,0:T(8,128)S(1)}, f32[8,2,256,1]{2,1,3,0:T(2,128)}, bf16[8,1024,2,96]{1,3,2,0:T(8,128)(2,1)}, f32[8,2,2]{2,1,0...) while((s32[]{:T(128)}, f32[8,256,2,96]{1,3,2,0:T(8,128)S(1)}, ...), condition=%wide.region_4.5_spmd.clone, body=%wide.region_1.4_spmd.clone.sunk | while | flops 281692032 | bytes 160720624 | solution.py:240
  647.7 102.5 %all-gather.9.cloned.1.call-done = bf16[2048,1536]{1,0:T(8,128)(2,1)} async-done(((bf16[256,1536]{1,0:T(8,128)(2,1)}), bf16[2048,1536]{1,0:T(8,128)(2,1)}) %all-gather.9.cloned.1.call-update) | async-done | bytes 6291472 | tf_op jit(solution)/shard_map/all_gather | solution.py:257
  763.9 51.8 %all-gather.11.cloned.1.call-done = bf16[2048,1536]{1,0:T(8,128)(2,1)} async-done(((bf16[256,1536]{1,0:T(8,128)(2,1)}), bf16[2048,1536]{1,0:T(8,128)(2,1)}) %all-gather.11.cloned.1.call-update) | async-done | bytes 6291472 | tf_op jit(solution)/shard_map/all_gather | solution.py:268
  844.9 60.5 %reduce-scatter.7.cloned.1.call-done = bf16[256,1536]{1,0:T(8,128)(2,1)} async-done(((bf16[2048,1536]{1,0:T(8,128)(2,1)}), bf16[256,1536]{1,0:T(8,128)(2,1)}) %reduce-scatter.7.cloned.1.call-update) | async-done | bytes 786448 | tf_op jit(solution)/shard_map/reduce_scatter | solution.py:282
  907.6 68.2 %reduce-scatter.5.cloned.1.call-done = bf16[256,1536]{1,0:T(8,128)(2,1)} async-done(((bf16[2048,1536]{1,0:T(8,128)(2,1)}), bf16[256,1536]{1,0:T(8,128)(2,1)}) %reduce-scatter.5.cloned.1.call-update) | async-done | bytes 786448 | tf_op jit(solution)/shard_map/reduce_scatter | solution.py:261
  1003.6 2550.7 %while.35 = (s32[]{:T(128)}, f32[8,261,2,96]{3,1,2,0:T(8,128)}, f32[8,1034,2,96]{1,3,2,0:T(8,128)}, f32[8,1024,2,96]{1,3,2,0:T(8,128)}, f32[8,2,6,11]{3,1,0,2:T(...) while((s32[]{:T(128)}, f32[8,261,2,96]{3,1,2,0:T(8,128)}, ...), condition=%wide.region_83.84_spmd.clone, body=%wide.region_13.83_spmd.clone.sunk | while | flops 1772737280 | bytes 370601792 | solution.py:306
  1036.8 36.7 multiply_reduce_fusion.77
  1158.8 124.6 %multiply_multiply_fusion.4 = f32[2,261,1034]{2,1,0:T(8,128)S(1)} fusion(f32[2,256,1024]{2,1,0:T(8,128)} %get-tuple-element.1464, f32[261,1034]{1,0:T(8,128)} %fusion.360, f32[2]{0:T(128)} %get-tuple-element.1396, f32[2]{0:T(128)} %get-tuple-element.1397, f32[2]{0:T(128)} %get-tuple-element.1398, f32[2]{0:T(128)} %get-tuple-element.1399, ...), kind=kLoop, calls=%fused_computation.436.clone.1 | loop fusion | flops 71786448 | bytes 5336168 | tf_op jit(solution)/shard_map/while/body/eval_jaxpr/mul | solution.py:123
  1352.0 36.7 multiply_reduce_fusion.77
  1474.1 124.6 %multiply_multiply_fusion.4 = f32[2,261,1034]{2,1,0:T(8,128)S(1)} fusion(f32[2,256,1024]{2,1,0:T(8,128)} %get-tuple-element.1464, f32[261,1034]{1,0:T(8,128)} %fusion.360, f32[2]{0:T(128)} %get-tuple-element.1396, f32[2]{0:T(128)} %get-tuple-element.1397, f32[2]{0:T(128)} %get-tuple-element.1398, f32[2]{0:T(128)} %get-tuple-element.1399, ...), kind=kLoop, calls=%fused_computation.436.clone.1 | loop fusion | flops 71786448 | bytes 5336168 | tf_op jit(solution)/shard_map/while/body/eval_jaxpr/mul | solution.py:123
  1667.3 36.7 multiply_reduce_fusion.77
  1789.3 124.6 %multiply_multiply_fusion.4 = f32[2,261,1034]{2,1,0:T(8,128)S(1)} fusion(f32[2,256,1024]{2,1,0:T(8,128)} %get-tuple-element.1464, f32[261,1034]{1,0:T(8,128)} %fusion.360, f32[2]{0:T(128)} %get-tuple-element.1396, f32[2]{0:T(128)} %get-tuple-element.1397, f32[2]{0:T(128)} %get-tuple-element.1398, f32[2]{0:T(128)} %get-tuple-element.1399, ...), kind=kLoop, calls=%fused_computation.436.clone.1 | loop fusion | flops 71786448 | bytes 5336168 | tf_op jit(solution)/shard_map/while/body/eval_jaxpr/mul | solution.py:123
  1982.6 36.7 multiply_reduce_fusion.77
  2104.6 124.6 %multiply_multiply_fusion.4 = f32[2,261,1034]{2,1,0:T(8,128)S(1)} fusion(f32[2,256,1024]{2,1,0:T(8,128)} %get-tuple-element.1464, f32[261,1034]{1,0:T(8,128)} %fusion.360, f32[2]{0:T(128)} %get-tuple-element.1396, f32[2]{0:T(128)} %get-tuple-element.1397, f32[2]{0:T(128)} %get-tuple-element.1398, f32[2]{0:T(128)} %get-tuple-element.1399, ...), kind=kLoop, calls=%fused_computation.436.clone.1 | loop fusion | flops 71786448 | bytes 5336168 | tf_op jit(solution)/shard_map/while/body/eval_jaxpr/mul | solution.py:123
  2297.8 36.7 multiply_reduce_fusion.77
  2419.8 124.6 %multiply_multiply_fusion.4 = f32[2,261,1034]{2,1,0:T(8,128)S(1)} fusion(f32[2,256,1024]{2,1,0:T(8,128)} %get-tuple-element.1464, f32[261,1034]{1,0:T(8,128)} %fusion.360, f32[2]{0:T(128)} %get-tuple-element.1396, f32[2]{0:T(128)} %get-tuple-element.1397, f32[2]{0:T(128)} %get-tuple-element.1398, f32[2]{0:T(128)} %get-tuple-element.1399, ...), kind=kLoop, calls=%fused_computation.436.clone.1 | loop fusion | flops 71786448 | bytes 5336168 | tf_op jit(solution)/shard_map/while/body/eval_jaxpr/mul | solution.py:123
  2735.1 124.6 %multiply_multiply_fusion.4 = f32[2,261,1034]{2,1,0:T(8,128)S(1)} fusion(f32[2,256,1024]{2,1,0:T(8,128)} %get-tuple-element.1464, f32[261,1034]{1,0:T(8,128)} %fusion.360, f32[2]{0:T(128)} %get-tuple-element.1396, f32[2]{0:T(128)} %get-tuple-element.1397, f32[2]{0:T(128)} %get-tuple-element.1398, f32[2]{0:T(128)} %get-tuple-element.1399, ...), kind=kLoop, calls=%fused_computation.436.clone.1 | loop fusion | flops 71786448 | bytes 5336168 | tf_op jit(solution)/shard_map/while/body/eval_jaxpr/mul | solution.py:123
  3050.4 124.6 %multiply_multiply_fusion.4 = f32[2,261,1034]{2,1,0:T(8,128)S(1)} fusion(f32[2,256,1024]{2,1,0:T(8,128)} %get-tuple-element.1464, f32[261,1034]{1,0:T(8,128)} %fusion.360, f32[2]{0:T(128)} %get-tuple-element.1396, f32[2]{0:T(128)} %get-tuple-element.1397, f32[2]{0:T(128)} %get-tuple-element.1398, f32[2]{0:T(128)} %get-tuple-element.1399, ...), kind=kLoop, calls=%fused_computation.436.clone.1 | loop fusion | flops 71786448 | bytes 5336168 | tf_op jit(solution)/shard_map/while/body/eval_jaxpr/mul | solution.py:123
  3365.6 124.6 %multiply_multiply_fusion.4 = f32[2,261,1034]{2,1,0:T(8,128)S(1)} fusion(f32[2,256,1024]{2,1,0:T(8,128)} %get-tuple-element.1464, f32[261,1034]{1,0:T(8,128)} %fusion.360, f32[2]{0:T(128)} %get-tuple-element.1396, f32[2]{0:T(128)} %get-tuple-element.1397, f32[2]{0:T(128)} %get-tuple-element.1398, f32[2]{0:T(128)} %get-tuple-element.1399, ...), kind=kLoop, calls=%fused_computation.436.clone.1 | loop fusion | flops 71786448 | bytes 5336168 | tf_op jit(solution)/shard_map/while/body/eval_jaxpr/mul | solution.py:123
  3682.7 153.6 %reduce-scatter.9.cloned.1.call-done = bf16[192,4608]{1,0:T(8,128)(2,1)} async-done(((bf16[1536,4608]{1,0:T(8,128)(2,1)}), bf16[192,4608]{1,0:T(8,128)(2,1)}) %reduce-scatter.9.cloned.1.call-update) | async-done | bytes 1769488 | tf_op jit(solution)/shard_map/reduce_scatter | solution.py:341
  3849.2 41.8 %all-reduce.2 = (f32[16,6,11]{2,0,1:T(8,128)S(1)}, f32[8,2,2]{0,2,1:T(2,128)}, f32[1536]{0:T(1024)}, f32[1536]{0:T(1024)}, f32[1536]{0:T(1024)}) all-reduce(f32[16,6,11]{2,0,1:T(8,128)} %bitcast.783, f32[8,2,2]{0,2,1:T(2,128)} %copy.255, f32[1536]{0:T(1024)} %get-tuple-element.619, ...), channel_id=1, replica_groups=mesh['rep'=4,'seq'=8] {'rep','seq'}, use_global_device_ids=true, to_apply=%region_89.90 | all-reduce | flops 5696 | bytes 45568 | tf_op jit(solution)/shard_map/psum | solution.py:349
  3895.1 102.1 %all-reduce.6.cloned.1.call-done = (bf16[192,4608]{1,0:T(8,128)(2,1)}, bf16[192,1536]{1,0:T(8,128)(2,1)}, bf16[1536,512]{1,0:T(8,128)(2,1)}, bf16[1536,512]{1,0:T(8,128)(2,1)}, bf16[512,1536]{1,0:T(8,128)(2,1)}) async-done(((bf16[192,4608]{1,0:T(8,128)(2,1)}, bf16[192,1536]{1,0:T(8,128)(2,1)}, bf16[1536,512]{1,0:T(8,128)(2,1)}, bf16[1536,512]{1,0:T(8,128)(2,1)}, bf16[512,1536]{1,0:T(8,128)(2,1)}), ...) | async-done | bytes 7077904 | tf_op jit(solution)/shard_map/psum | solution.py:353
  (1999 shorter events, 1987.9 us)
Async XLA Ops:
  7.2 808.5 %copy-start = (bf16[512,1536]{1,0:T(8,128)(2,1)S(1)}, bf16[512,1536]{1,0:T(8,128)(2,1)}, u32[]{:S(2)}) copy-start(bf16[512,1536]{1,0:T(8,128)(2,1)} %param.30) | copy-start | bytes 4718596
  7.2 130.5 %copy-start.64 = (f32[1536]{0:T(1024)S(1)}, f32[1536]{0:T(1024)}, u32[]{:S(2)}) copy-start(f32[1536]{0:T(1024)} %param.25) | copy-start | bytes 18436
  7.2 130.5 %all-gather.5.cloned.1.call-start = ((), (), s32[]{:S(2)}) async-start(), calls=%async_computation.4 | async-start | bytes 15925248 | tf_op jit(solution)/shard_map/all_gather | solution.py:211
  8.0 630.4 %all-gather.7.cloned.1.call-start = ((), (), s32[]{:S(2)}) async-start(), calls=%async_computation.5 | async-start | bytes 5308416 | tf_op jit(solution)/shard_map/all_gather | solution.py:212
  9.3 137.7 %copy-start.72 = (f32[256]{0:T(256)}, f32[256]{0:T(256)S(1)}, u32[]{:S(2)}) copy-start(f32[256]{0:T(256)S(1)} %get-tuple-element.869) | copy-start | bytes 3076
  149.7 19.3 collective-permute-start.2
  151.0 106.0 %collective-permute-start.1 = (bf16[256,3072]{1,0:T(8,128)(2,1)}, bf16[256,3072]{1,0:T(8,128)(2,1)}, u32[]{:S(2)}, u32[]{:S(2)}) collective-permute-start(bf16[256,3072]{1,0:T(8,128)(2,1)} %slice.2477), channel_id=1, source_target_pairs={{0,2},{1,3},{2,4},{3,5},{4,6},{5,7},{8,10},{9,11},{10,12},{11,13},... | collective-permute-start | bytes 4718600 | tf_op jit(solution)/shard_map/ppermute | solution.py:16
  152.3 108.7 %collective-permute-start = (bf16[256,3072]{1,0:T(8,128)(2,1)}, bf16[256,3072]{1,0:T(8,128)(2,1)}, u32[]{:S(2)}, u32[]{:S(2)}) collective-permute-start(bf16[256,3072]{1,0:T(8,128)(2,1)} %slice.2477), channel_id=1, source_target_pairs={{0,3},{1,4},{2,5},{3,6},{4,7},{8,11},{9,12},{10,13},{11,14},{12,15... | collective-permute-start | bytes 4718600 | tf_op jit(solution)/shard_map/ppermute | solution.py:16
  153.6 596.6 %all-gather.9.cloned.1.call-start = ((), (), s32[]{:S(2)}) async-start(), calls=%async_computation.6 | async-start | bytes 7077888 | tf_op jit(solution)/shard_map/all_gather | solution.py:257
  156.7 3.7 collective-permute-start.3
  645.1 170.6 %all-gather.11.cloned.1.call-start = ((), (), s32[]{:S(2)}) async-start(), calls=%async_computation.8 | async-start | bytes 7077888 | tf_op jit(solution)/shard_map/all_gather | solution.py:268
  647.4 258.0 %reduce-scatter.7.cloned.1.call-start = ((), (), s32[]{:S(2)}) async-start(), calls=%async_computation.9 | async-start | bytes 7077888 | tf_op jit(solution)/shard_map/reduce_scatter | solution.py:282
  837.4 138.3 %reduce-scatter.5.cloned.1.call-start = ((), (), s32[]{:S(2)}) async-start(), calls=%async_computation.7 | async-start | bytes 7077888 | tf_op jit(solution)/shard_map/reduce_scatter | solution.py:261
  844.4 61.0 %copy-start.12 = (f32[256,1536]{1,0:T(8,128)S(1)}, f32[256,1536]{1,0:T(8,128)}, u32[]{:S(2)}) copy-start(f32[256,1536]{1,0:T(8,128)} %copy-done.11) | copy-start | bytes 4718596
  844.5 2838.2 %reduce-scatter.11.cloned.1.call-start = ((), (), s32[]{:S(2)}) async-start(), calls=%async_computation.11 | async-start | bytes 5308416 | tf_op jit(solution)/shard_map/reduce_scatter | solution.py:344
  1003.6 2832.7 %reduce-scatter.9.cloned.1.call-start = ((), (), s32[]{:S(2)}) async-start(), calls=%async_computation.10 | async-start | bytes 15925248 | tf_op jit(solution)/shard_map/reduce_scatter | solution.py:341
  3574.6 19.9 collective-permute-start.5
  3578.6 36.5 collective-permute-start.7
  3581.8 67.1 %collective-permute-start.6 = (bf16[256,3072]{0,1:T(8,128)(2,1)}, bf16[256,3072]{0,1:T(8,128)(2,1)}, u32[]{:S(2)}, u32[]{:S(2)}) collective-permute-start(bf16[256,3072]{0,1:T(8,128)(2,1)} %get-tuple-element.859), channel_id=1, source_target_pairs={{2,0},{3,1},{4,2},{5,3},{6,4},{7,5},{10,8},{11,9},{12,10},{13,11},... | collective-permute-start | bytes 4718600 | tf_op jit(solution)/shard_map/ppermute | solution.py:16
  3589.1 5.1 collective-permute-start.4
  3594.5 58.4 %copy-start.15 = (bf16[1,256,1536]{2,1,0:T(8,128)(2,1)S(1)}, bf16[1,256,1536]{2,1,0:T(8,128)(2,1)}, u32[]{:S(2)}) copy-start(bf16[1,256,1536]{2,1,0:T(8,128)(2,1)} %param.18) | copy-start | bytes 2359300
  3594.5 58.4 %copy-start.20 = (bf16[251,8,2,96]{0,3,2,1:T(8,128)(2,1)S(1)}, bf16[251,8,2,96]{0,3,2,1:T(8,128)(2,1)}, u32[]{:S(2)}) copy-start(bf16[251,8,2,96]{0,3,2,1:T(8,128)(2,1)} %slice.3701) | copy-start | bytes 2313220
  3594.5 58.4 %copy-start.65 = (f32[1536]{0:T(1024)S(1)}, f32[1536]{0:T(1024)}, u32[]{:S(2)}) copy-start(f32[1536]{0:T(1024)} %param.25) | copy-start | bytes 18436
  3662.1 335.1 %all-reduce.6.cloned.1.call-start = ((), (), s32[]{:S(2)}) async-start(), calls=%async_computation.12 | async-start | bytes 14155776 | tf_op jit(solution)/shard_map/psum | solution.py:353
  (417 other events, 4079.7 us)
Sparse Core Ops, SparseCore 0:
  9.7 127.9 all-gather.4
  153.8 73.6 all-gather.6
  645.3 104.8 all-gather.8
  752.3 63.3 all-gather.10
  837.5 67.8 reduce-scatter.6
  907.6 68.1 reduce-scatter.4
  1003.7 53.3 reduce-scatter.10
  3662.2 174.0 reduce-scatter.8
  3841.7 155.4 all-reduce.5
where the time goes:
time: 4040 us; the launch traced here: 4010 us
  other arithmetic  2010 us (50%)
  local copies, waits for them, and re-layouts  852 us (21%)
  waiting for transfers between devices  815 us (20%)
  matrix products  225 us (6%)
  blocking collectives  41.8 us (1%)
    mul x8, other arithmetic, attend_group_back(): dlogits = convolve_back(dconv, kernel_g) * mask_ext * score_scale  997 us
    another operation x576, local copies, waits for them, and re-layouts, kernel_grads(): entries.append(jnp.stack(line_sums, axis=-1))  678 us
    reduce_sum x32, other arithmetic, kernel_grads(): line_sums.append(jnp.sum(grads * window_part, axis=(1, 2)))  334 us
    reduce_sum x8, other arithmetic, attend_group_back(): dconv = prob * (dprob - jnp.sum(prob * dprob, axis=-1, keepdims=True))  294 us
    reduce_max x8, other arithmetic, attend_group(): peak = jnp.max(jnp.where(allowed, conv, -1e+30), axis=-1, keepdims=True)  277 us
    reduce_scatter x1, waiting for transfers between devices, on_device(): lax.psum_scatter(whole_input_grad.astype(jnp.bfloat16), 'seq', scatter_di...  154 us
    ppermute x8, waiting for transfers between devices, from_behind(): return lax.ppermute(x, axis, pairs)  147 us
    all_gather x1, waiting for transfers between devices, on_device(): lax.all_gather(input_weight, 'seq', axis=0, tiled=True)  128 us
  transfers between devices with their start and end apart: 17, of which 12 were waited for; matrix products, arithmetic and copies ran while one was open for 74% of the time, Pallas kernels for 0%

commit v1 on v0

v1 whole, which is shorter than its diff:
```python
import functools
import jax
import jax.numpy as jnp
from jax import lax
from jax.experimental import pallas as pl
from jax.experimental.pallas import tpu as pltpu
from jax.sharding import PartitionSpec as P

FRAME = 1024


EPS = 1e-06
LANES = 128
ROWS = 256
EDGE = 64
HEADER = 16
NEG = -1e30
PROB = jnp.float32

NT = (((1,), (1,)), ((), ()))
NN = (((1,), (0,)), ((), ()))


def dot(a, b, dims=NN):
    return lax.dot_general(a, b, dims, preferred_element_type=jnp.float32)


def toeplitz(kernel, scale):
    heads, taps, span = kernel.shape
    shape = (heads, 2 * LANES, taps * LANES)
    lane = lax.broadcasted_iota(jnp.int32, shape, 2)
    tap = lax.broadcasted_iota(jnp.int32, shape, 1)
    diff = lane % LANES + EDGE + span // 2 - tap
    total = jnp.zeros(shape, jnp.float32)
    for b in range(span):
        weight = jnp.repeat(kernel[:, :, b] * scale, LANES, axis=1)[:, None, :]
        total = total + jnp.where(diff == b, weight, 0.0)
    return total


def split_toeplitz(full):
    kept = lax.reduce_precision(full, exponent_bits=8, mantissa_bits=7)
    high = kept.astype(jnp.bfloat16)
    low = (full - kept).astype(jnp.bfloat16)
    return high, jnp.concatenate([high, high, low], axis=1)


def toeplitz_grad(grads, taps, span, scale):
    heads = grads.shape[0]
    shape = grads.shape
    lane = lax.broadcasted_iota(jnp.int32, shape, 2)
    tap = lax.broadcasted_iota(jnp.int32, shape, 1)
    diff = lane % LANES + EDGE + span // 2 - tap
    cols = []
    for b in range(span):
        part = jnp.sum(jnp.where(diff == b, grads, 0.0), axis=1)
        cols.append(jnp.sum(part.reshape(heads, taps, LANES), axis=-1) * scale)
    return jnp.stack(cols, axis=-1)


def lane_mask(dim):
    return lax.broadcasted_iota(jnp.int32, (ROWS, LANES), 1) < dim


def group_stats(att, dim):
    mean = jnp.sum(att, axis=-1, keepdims=True) / dim
    centred = jnp.where(lane_mask(dim), att - mean, 0.0)
    var = jnp.sum(centred * centred, axis=-1, keepdims=True) / dim
    inv = lax.rsqrt(var + EPS)
    return centred * inv, inv


def forward_kernel(
    dim, taps, q_ref, k_ref, v_ref, t_ref, rowc_ref, colp_ref, colc_ref, gain_ref, mix_ref,
    normed_ref, att_ref, prob_ref, lm_ref, lo_ref, p_ref, cv_ref, mx_ref, sm_ref, acc_ref,
):
    step = pl.program_id(1)
    first = step * ROWS
    top = pl.multiple_of(first + EDGE - HEADER, 16)
    tall = ROWS + HEADER
    codes = rowc_ref[pl.ds(top, tall), :]
    ipos = first - HEADER + lax.broadcasted_iota(jnp.int32, (tall, LANES), 0)
    lane = lax.broadcasted_iota(jnp.int32, (tall, LANES), 1)
    live = codes[HEADER:] >= 0

    def logits(c, carry):
        at = pl.multiple_of(c * LANES, LANES)
        keep = (codes == colp_ref[:, pl.ds(at, LANES)]) & (at - EDGE + lane <= ipos)
        for h in range(2):
            cols = slice(h * LANES, (h + 1) * LANES)
            raw = dot(q_ref[pl.ds(top, tall), cols], k_ref[pl.ds(at, LANES), cols], NT)
            raw = jnp.where(keep, raw, 0.0)
            high = raw.astype(jnp.bfloat16)
            lm_ref[h, :, pl.ds(at, LANES)] = high
            lo_ref[h, :, pl.ds(at, LANES)] = (raw - high.astype(jnp.float32)).astype(jnp.bfloat16)
        return carry

    lax.fori_loop(0, 2 * step + 3, logits, 0)
    mx_ref[...] = jnp.full(mx_ref.shape, NEG, jnp.float32)
    blocks = 2 * step + 2

    def convolve(c, carry):
        at = pl.multiple_of(c * LANES, LANES)
        keep = (codes[HEADER:] == colc_ref[:, pl.ds(at, LANES)]) & (at + lane[HEADER:] <= ipos[HEADER:])
        for h in range(2):
            high = lm_ref[h, :, pl.ds(at, 2 * LANES)]
            p_ref[h] = dot(jnp.concatenate([high, lo_ref[h, :, pl.ds(at, 2 * LANES)], high], axis=1), t_ref[h])
            conv = p_ref[h, HEADER:, :LANES]
            for a in range(1, taps):
                conv = conv + p_ref[h, HEADER - a : tall - a, a * LANES : (a + 1) * LANES]
            conv = jnp.where(keep, conv, NEG)
            cv_ref[h, :, pl.ds(at, LANES)] = conv
            mx_ref[h] = jnp.maximum(mx_ref[h], conv)
        return carry

    lax.fori_loop(0, blocks, convolve, 0)
    sm_ref[...] = jnp.zeros(sm_ref.shape, jnp.float32)
    for h in range(2):
        peak = jnp.max(mx_ref[h], axis=-1, keepdims=True)
        mx_ref[h] = jnp.where(live, jnp.broadcast_to(peak, (ROWS, LANES)), 0.0)

    def exponents(c, carry):
        at = pl.multiple_of(c * LANES, LANES)
        for h in range(2):
            value = jnp.exp(cv_ref[h, :, pl.ds(at, LANES)] - mx_ref[h])
            cv_ref[h, :, pl.ds(at, LANES)] = value
            sm_ref[h] = sm_ref[h] + value
        return carry

    lax.fori_loop(0, blocks, exponents, 0)
    for h in range(2):
        total = jnp.sum(sm_ref[h], axis=-1, keepdims=True)
        total = jnp.where(live, jnp.broadcast_to(total, (ROWS, LANES)), 1.0)
        sm_ref[h] = 1.0 / total
    acc_ref[...] = jnp.zeros(acc_ref.shape, jnp.float32)
    pair = pl.program_id(0)
    mix = [[mix_ref[pair, 2 * g + h] for h in range(2)] for g in range(2)]

    def mixing(c, carry):
        at = pl.multiple_of(c * LANES, LANES)
        prob = [cv_ref[h, :, pl.ds(at, LANES)] * sm_ref[h] for h in range(2)]
        for g in range(2):
            cols = slice(g * LANES, (g + 1) * LANES)
            prob_ref[g, :, pl.ds(at, LANES)] = prob[g].astype(prob_ref.dtype)
            mixed = (mix[g][0] * prob[0] + mix[g][1] * prob[1]).astype(jnp.bfloat16)
            acc_ref[g] += dot(mixed, v_ref[pl.ds(at + EDGE, LANES), cols])
        return carry

    lax.fori_loop(0, blocks, mixing, 0)
    for g in range(2):
        att = acc_ref[g]
        att_ref[:, g * LANES : (g + 1) * LANES] = att
        unit, _ = group_stats(att, dim)
        normed = unit * gain_ref[0:1, g * LANES : (g + 1) * LANES]
        normed_ref[:, g * LANES : (g + 1) * LANES] = normed.astype(jnp.bfloat16)


def backward_kernel(
    dim, taps, q_ref, k_ref, v_ref, t_ref, rowc_ref, colp_ref, colt_ref, rowt_ref, prob_ref, att_ref, dn_ref,
    gain_ref, mix_ref, dq_ref, dk_ref, dv_ref, g_ref, dmix_ref, dgain_ref,
    dp_ref, dc_ref, dl_ref, lt_ref, dkt_ref, dvt_ref, datt_ref, dattt_ref, qt_ref, rs_ref, dqa_ref, dm_ref, ahead_ref,
):
    pair = pl.program_id(0)
    turn = pl.program_id(1)
    step = pl.num_programs(1) - 1 - turn
    first = pl.multiple_of(step * ROWS, ROWS)
    own = pl.multiple_of(first + EDGE, 16)
    codes = rowc_ref[pl.ds(own, ROWS), :]
    ipos = first + lax.broadcasted_iota(jnp.int32, (ROWS, LANES), 0)
    lane = lax.broadcasted_iota(jnp.int32, (ROWS, LANES), 1)
    blocks = 2 * step + 2
    mix = [[mix_ref[pair, 2 * g + h] for h in range(2)] for g in range(2)]

    @pl.when(turn == 0)
    def _():
        dc_ref[...] = jnp.zeros(dc_ref.shape, jnp.float32)
        dkt_ref[...] = jnp.zeros(dkt_ref.shape, jnp.float32)
        dvt_ref[...] = jnp.zeros(dvt_ref.shape, jnp.float32)
        g_ref[...] = jnp.zeros(g_ref.shape, jnp.float32)
        dmix_ref[...] = jnp.zeros(dmix_ref.shape, jnp.float32)
        dgain_ref[...] = jnp.zeros(dgain_ref.shape, jnp.float32)
        for ref in (dq_ref, dv_ref):
            ref[:EDGE, :] = jnp.zeros((EDGE, 2 * LANES), jnp.bfloat16)
            ref[ref.shape[0] - EDGE :, :] = jnp.zeros((EDGE, 2 * LANES), jnp.bfloat16)

    @pl.when(turn > 0)
    def _():
        for h in range(2):
            dc_ref[h, ROWS:, :] = dc_ref[h, :8, :]

    for g in range(2):
        cols = slice(g * LANES, (g + 1) * LANES)
        unit, inv = group_stats(att_ref[:, cols], dim)
        grad = dn_ref[:, cols]
        dgain_ref[0:1, cols] += jnp.sum(grad * unit, axis=0, keepdims=True)
        scaled = grad * gain_ref[0:1, cols]
        mean = jnp.sum(scaled, axis=-1, keepdims=True) / dim
        inner = jnp.sum(scaled * unit, axis=-1, keepdims=True) / dim
        datt = inv * (scaled - mean - unit * inner)
        datt = jnp.where(lane_mask(dim), datt, 0.0)
        high = datt.astype(jnp.bfloat16)
        datt_ref[g, :, :LANES] = high
        datt_ref[g, :, LANES:] = (datt - high.astype(jnp.float32)).astype(jnp.bfloat16)
        dattt_ref[g] = datt.T.astype(jnp.bfloat16)
        qt_ref[g] = q_ref[pl.ds(own, ROWS), cols].astype(jnp.float32).T.astype(jnp.bfloat16)
    rs_ref[...] = jnp.zeros(rs_ref.shape, jnp.float32)
    dm_ref[...] = jnp.zeros(dm_ref.shape, jnp.float32)

    def probs(c, carry):
        at = pl.multiple_of(c * LANES, LANES)
        prob = [prob_ref[h, :, pl.ds(at, LANES)].astype(jnp.float32) for h in range(2)]
        dmixed = []
        for g in range(2):
            cols = slice(g * LANES, (g + 1) * LANES)
            value = v_ref[pl.ds(at + EDGE, LANES), cols]
            dmixed.append(dot(datt_ref[g], jnp.concatenate([value, value], axis=1), NT))
            mixed = (mix[g][0] * prob[0] + mix[g][1] * prob[1]).astype(jnp.bfloat16)
            dvt_ref[g, :, pl.ds(at, LANES)] += dot(dattt_ref[g], mixed)
            for h in range(2):
                dm_ref[2 * g + h] += dmixed[g] * prob[h]
        for h in range(2):
            dprob = mix[0][h] * dmixed[0] + mix[1][h] * dmixed[1]
            dp_ref[h, :, pl.ds(at, LANES)] = dprob
            rs_ref[h] += prob[h] * dprob
        return carry

    lax.fori_loop(0, blocks, probs, 0)
    for h in range(2):
        rs_ref[h] = jnp.broadcast_to(jnp.sum(rs_ref[h], axis=-1, keepdims=True), (ROWS, LANES))
    for n in range(4):
        dmix_ref[0, n : n + 1, :] += jnp.sum(dm_ref[n], axis=0, keepdims=True)

    tlane = lax.broadcasted_iota(jnp.int32, (LANES, ROWS), 1)
    trow = lax.broadcasted_iota(jnp.int32, (LANES, ROWS), 0)

    def transposed_logits(c, carry):
        at = pl.multiple_of(c * LANES, LANES)
        wide = jnp.concatenate([colt_ref[pl.ds(at, LANES), :]] * 2, axis=1)
        keep = (wide == rowt_ref[:, pl.ds(first, ROWS)]) & (at - EDGE + trow <= first + tlane)
        for h in range(2):
            cols = slice(h * LANES, (h + 1) * LANES)
            raw = dot(k_ref[pl.ds(at, LANES), cols], q_ref[pl.ds(own, ROWS), cols], NT)
            lt_ref[h, pl.ds(at, LANES), :] = jnp.where(keep, raw, 0.0).astype(jnp.bfloat16)
            dl_ref[h, :, pl.ds(at, LANES)] = jnp.zeros((ROWS, LANES), jnp.float32)
        return carry

    lax.fori_loop(0, blocks + 1, transposed_logits, 0)

    def convolve(c, carry):
        at = pl.multiple_of(c * LANES, LANES)
        for h in range(2):
            prob = prob_ref[h, :, pl.ds(at, LANES)].astype(jnp.float32)
            dc_ref[h, :ROWS, pl.ds(at, LANES)] = prob * (dp_ref[h, :, pl.ds(at, LANES)] - rs_ref[h])
            shifted = jnp.concatenate(
                [dc_ref[h, a : a + ROWS, pl.ds(at, LANES)].astype(jnp.bfloat16) for a in range(taps)], axis=1
            )
            g_ref[h] += dot(lt_ref[h, pl.ds(at, 2 * LANES), :], shifted)
            dl_ref[h, :, pl.ds(at, 2 * LANES)] += dot(shifted, t_ref[h], NT)
        return carry

    lax.fori_loop(0, blocks, convolve, 0)
    dqa_ref[...] = jnp.zeros(dqa_ref.shape, jnp.float32)

    def logits(c, carry):
        at = pl.multiple_of(c * LANES, LANES)
        keep = (codes == colp_ref[:, pl.ds(at, LANES)]) & (at - EDGE + lane <= ipos)
        for h in range(2):
            cols = slice(h * LANES, (h + 1) * LANES)
            dl = jnp.where(keep, dl_ref[h, :, pl.ds(at, LANES)], 0.0).astype(jnp.bfloat16)
            dqa_ref[h] += dot(dl, k_ref[pl.ds(at, LANES), cols])
            dkt_ref[h, :, pl.ds(at, LANES)] += dot(qt_ref[h], dl)
        return carry

    lax.fori_loop(0, blocks + 1, logits, 0)
    for h in range(2):
        dq_ref[pl.ds(own, ROWS), h * LANES : (h + 1) * LANES] = dqa_ref[h].astype(jnp.bfloat16)

    @pl.when(step == 0)
    def _():
        head = slice(EDGE - HEADER, EDGE)
        wide = (HEADER, 2 * LANES)
        keep = jnp.concatenate([rowc_ref[head, :]] * 2, axis=1) == colp_ref[:, : 2 * LANES]
        keep = keep & (
            lax.broadcasted_iota(jnp.int32, wide, 1) - EDGE <= lax.broadcasted_iota(jnp.int32, wide, 0) - HEADER
        )
        for h in range(2):
            cols = slice(h * LANES, (h + 1) * LANES)
            ahead_ref[:HEADER, :] = jnp.zeros((HEADER, LANES), jnp.float32)
            ahead_ref[HEADER:, :] = dc_ref[h, :HEADER, :LANES]
            shifted = jnp.concatenate(
                [ahead_ref[a : a + HEADER, :].astype(jnp.bfloat16) for a in range(taps)], axis=1
            )
            near = k_ref[: 2 * LANES, cols]
            query = q_ref[head, cols]
            raw = jnp.where(keep, dot(query, near, NT), 0.0)
            g_ref[h] += dot(raw.T.astype(jnp.bfloat16), shifted)
            dl = jnp.where(keep, dot(shifted, t_ref[h], NT), 0.0).astype(jnp.bfloat16)
            dq_ref[head, cols] = dot(dl, near).astype(jnp.bfloat16)
            dkt_ref[h, :, : 2 * LANES] += dot(query.astype(jnp.float32).T.astype(jnp.bfloat16), dl)
            dk_ref[:, cols] = dkt_ref[h].T.astype(jnp.bfloat16)
            dv_ref[pl.ds(EDGE, dvt_ref.shape[2]), cols] = dvt_ref[h].T.astype(jnp.bfloat16)


def attention_forward(proj, toep, codes, gain, mix, dim, taps):
    tall = proj.shape[0]
    frame = tall - 2 * EDGE
    pairs = mix.shape[0]
    steps = frame // ROWS
    whole = lambda off: pl.BlockSpec((tall, 2 * LANES), lambda p, r: (0, off * pairs + p))
    wide = pairs * 2 * LANES
    return pl.pallas_call(
        functools.partial(forward_kernel, dim, taps),
        grid=(pairs, steps),
        in_specs=[
            whole(0), whole(1), whole(2),
            pl.BlockSpec((2, 6 * LANES, taps * LANES), lambda p, r: (p, 0, 0)),
            pl.BlockSpec((tall, LANES), lambda p, r: (0, 0)),
            pl.BlockSpec((1, tall), lambda p, r: (0, 0)),
            pl.BlockSpec((1, frame), lambda p, r: (0, 0)),
            pl.BlockSpec((1, 2 * LANES), lambda p, r: (0, p)),
            pl.BlockSpec(memory_space=pltpu.SMEM),
        ],
        out_specs=[
            pl.BlockSpec((ROWS, 2 * LANES), lambda p, r: (r, p)),
            pl.BlockSpec((ROWS, 2 * LANES), lambda p, r: (r, p)),
            pl.BlockSpec((2, ROWS, frame), lambda p, r: (p, r, 0)),
        ],
        out_shape=[
            jax.ShapeDtypeStruct((frame, wide), jnp.bfloat16),
            jax.ShapeDtypeStruct((frame, wide), jnp.float32),
            jax.ShapeDtypeStruct((2 * pairs, frame, frame), PROB),
        ],
        scratch_shapes=[
            pltpu.VMEM((2, ROWS + HEADER, tall), jnp.bfloat16),
            pltpu.VMEM((2, ROWS + HEADER, tall), jnp.bfloat16),
            pltpu.VMEM((2, ROWS + HEADER, taps * LANES), jnp.float32),
            pltpu.VMEM((2, ROWS, frame), jnp.float32),
            pltpu.VMEM((2, ROWS, LANES), jnp.float32),
            pltpu.VMEM((2, ROWS, LANES), jnp.float32),
            pltpu.VMEM((2, ROWS, LANES), jnp.float32),
        ],
        cost_estimate=pl.CostEstimate(flops=60_000_000_000, bytes_accessed=40_000_000, transcendentals=0),
        compiler_params=pltpu.CompilerParams(vmem_limit_bytes=48 << 20),
        name="attend",
    )(proj, proj, proj, toep, codes["row"], codes["colp"], codes["col"], gain, mix)


def attention_backward(proj, toep, codes, prob, att, dnormed, gain, mix, dim, taps):
    tall = proj.shape[0]
    frame = tall - 2 * EDGE
    pairs = mix.shape[0]
    steps = frame // ROWS
    whole = lambda off: pl.BlockSpec((tall, 2 * LANES), lambda p, r: (0, off * pairs + p))
    wide = pairs * 2 * LANES
    back = lambda r: steps - 1 - r
    return pl.pallas_call(
        functools.partial(backward_kernel, dim, taps),
        grid=(pairs, steps),
        in_specs=[
            whole(0), whole(1), whole(2),
            pl.BlockSpec((2, 2 * LANES, taps * LANES), lambda p, r: (p, 0, 0)),
            pl.BlockSpec((tall, LANES), lambda p, r: (0, 0)),
            pl.BlockSpec((1, tall), lambda p, r: (0, 0)),
            pl.BlockSpec((tall, LANES), lambda p, r: (0, 0)),
            pl.BlockSpec((1, frame), lambda p, r: (0, 0)),
            pl.BlockSpec((2, ROWS, frame), lambda p, r: (p, back(r), 0)),
            pl.BlockSpec((ROWS, 2 * LANES), lambda p, r: (back(r), p)),
            pl.BlockSpec((ROWS, 2 * LANES), lambda p, r: (back(r), p)),
            pl.BlockSpec((1, 2 * LANES), lambda p, r: (0, p)),
            pl.BlockSpec(memory_space=pltpu.SMEM),
        ],
        out_specs=[
            pl.BlockSpec((tall, 2 * LANES), lambda p, r: (0, p)),
            pl.BlockSpec((tall, 2 * LANES), lambda p, r: (0, p)),
            pl.BlockSpec((tall, 2 * LANES), lambda p, r: (0, p)),
            pl.BlockSpec((2, 2 * LANES, taps * LANES), lambda p, r: (p, 0, 0)),
            pl.BlockSpec((1, 8, LANES), lambda p, r: (p, 0, 0)),
            pl.BlockSpec((1, 2 * LANES), lambda p, r: (0, p)),
        ],
        out_shape=[
            jax.ShapeDtypeStruct((tall, wide), jnp.bfloat16),
            jax.ShapeDtypeStruct((tall, wide), jnp.bfloat16),
            jax.ShapeDtypeStruct((tall, wide), jnp.bfloat16),
            jax.ShapeDtypeStruct((2 * pairs, 2 * LANES, taps * LANES), jnp.float32),
            jax.ShapeDtypeStruct((pairs, 8, LANES), jnp.float32),
            jax.ShapeDtypeStruct((1, wide), jnp.float32),
        ],
        scratch_shapes=[
            pltpu.VMEM((2, ROWS, frame), jnp.float32),
            pltpu.VMEM((2, ROWS + 8, frame), jnp.float32),
            pltpu.VMEM((2, ROWS, tall), jnp.float32),
            pltpu.VMEM((2, tall, ROWS), jnp.bfloat16),
            pltpu.VMEM((2, LANES, tall), jnp.float32),
            pltpu.VMEM((2, LANES, frame), jnp.float32),
            pltpu.VMEM((2, ROWS, 2 * LANES), jnp.bfloat16),
            pltpu.VMEM((2, LANES, ROWS), jnp.bfloat16),
            pltpu.VMEM((2, LANES, ROWS), jnp.bfloat16),
            pltpu.VMEM((2, ROWS, LANES), jnp.float32),
            pltpu.VMEM((2, ROWS, LANES), jnp.float32),
            pltpu.VMEM((4, ROWS, LANES), jnp.float32),
            pltpu.VMEM((2 * HEADER, LANES), jnp.float32),
        ],
        cost_estimate=pl.CostEstimate(flops=70_000_000_000, bytes_accessed=40_000_000, transcendentals=0),
        compiler_params=pltpu.CompilerParams(vmem_limit_bytes=48 << 20),
        name="attend_back",
    )(proj, proj, proj, toep, codes["row"], codes["colp"], codes["colt"], codes["rowt"], prob, att, dnormed, gain, mix)


def make_codes(segment, valid):
    row = jnp.where(valid > 0, segment, -1)
    col = jnp.where(valid > 0, segment, -2)
    rowp = jnp.pad(row, (EDGE - HEADER, EDGE), constant_values=-1)
    colp = jnp.pad(col, (EDGE - HEADER, EDGE), constant_values=-2)
    tall = rowp.shape[0]
    return {
        "row": jnp.broadcast_to(rowp[:, None], (tall, LANES)),
        "colt": jnp.broadcast_to(colp[:, None], (tall, LANES)),
        "colp": colp[None],
        "col": col[None, HEADER:],
        "rowt": row[None, HEADER:],
    }


MESH = pl.DeviceIdType.MESH


def meet(peers):
    barrier = pltpu.get_barrier_semaphore()
    for peer in peers:
        pl.semaphore_signal(barrier, inc=1, device_id=peer, device_id_type=MESH)
    pl.semaphore_wait(barrier, len(peers))


def send(src, dst, send_sem, recv_sem, peer):
    return pltpu.make_async_remote_copy(
        src_ref=src, dst_ref=dst, send_sem=send_sem, recv_sem=recv_sem, device_id=peer, device_id_type=MESH
    )


def gather_kernel(
    reps, count, w_ref, x_ref, z_ref, wc_ref, f_ref, own_sem, side_send, side_recv, far_send, far_recv, rep_send, rep_recv,
    tok_send, tok_recv, head_send, head_recv,
):
    rep = lax.axis_index("rep")
    me = lax.axis_index("seq")
    chips = count // 2
    chip, core = me // 2, me % 2
    rows = w_ref.shape[0]
    part = rows // reps
    full = w_ref.shape[1] // 3
    cols = wc_ref.shape[1] // 3
    tokens = x_ref.shape[0]
    place = me % 4
    sibling = chip * 2 + 1 - core
    far_ids = [((chip + k) % chips) * 2 + e for k in range(1, chips) for e in range(2)]
    rep_ids = [(rep + k) % reps for k in range(1, reps)]
    at = lambda r, s: (r, s)
    meet([at(rep, s) for s in far_ids + [sibling]] + [at(r, me) for r in rep_ids])

    def source(first, size, who, t):
        left = pl.multiple_of(t * full + (who % 4) * cols, LANES)
        return w_ref.at[pl.ds(first, size), pl.ds(left, cols)]

    def target(first, size, t):
        return wc_ref.at[pl.ds(first, size), pl.ds(t * cols, cols)]

    def spot(who, r):
        return pl.multiple_of(who * rows + r * part, 16)

    def token_rows(who, half):
        return f_ref.at[pl.ds(pl.multiple_of(EDGE + (who % 4) * tokens + half * (tokens // 2), 16), tokens // 2), :]

    waits = []
    quarter = pl.multiple_of(rep * part, 16)
    for n, who in enumerate(far_ids):
        for t in range(3):
            copy = send(
                source(quarter, part, who, t), target(spot(me, rep), part, t), far_send.at[n, t], far_recv.at[me, t],
                at(rep, who),
            )
            copy.start()
            waits.append(copy)
    for t in range(3):
        copy = send(
            source(0, rows, sibling, t), target(spot(me, 0), rows, t), side_send.at[t], side_recv.at[t], at(rep, sibling)
        )
        copy.start()
        waits.append(copy)
    partner = (chip ^ 1) * 2 + core
    for half in range(2):
        mine = x_ref.at[pl.ds(half * (tokens // 2), tokens // 2), :]
        copy = send(mine, token_rows(me, half), tok_send.at[0, half], tok_recv.at[0, half], at(rep, partner))
        copy.start()
        waits.append(copy)
        copy = send(mine, token_rows(me, half), tok_send.at[1, half], tok_recv.at[1, half], at(rep, sibling))
        copy.start()
        waits.append(copy)
    local = [
        pltpu.make_async_copy(source(0, rows, me, t), target(spot(me, 0), rows, t), own_sem.at[t]) for t in range(3)
    ]
    lead = EDGE - HEADER
    local.append(pltpu.make_async_copy(z_ref.at[pl.ds(0, lead), :], f_ref.at[pl.ds(0, lead), :], own_sem.at[4]))
    local.append(
        pltpu.make_async_copy(z_ref, f_ref.at[pl.ds(f_ref.shape[0] - EDGE, EDGE), :], own_sem.at[5])
    )
    local.append(pltpu.make_async_copy(
        x_ref, f_ref.at[pl.ds(pl.multiple_of(EDGE + place * tokens, 16), tokens), :], own_sem.at[3]
    ))
    for copy in local:
        copy.start()
    head = f_ref.at[pl.ds(lead, HEADER), :]
    fill = pltpu.make_async_copy(z_ref.at[pl.ds(0, HEADER), :], head, own_sem.at[6])
    sends_on = (place == 3) & (me < count - 4)
    after = [
        send(x_ref.at[pl.ds(tokens - HEADER, HEADER), :], head, head_send.at[v], head_recv.at[0],
             at(rep, lax.rem(me + 1 + v, count)))
        for v in range(4)
    ]

    @pl.when(sends_on)
    def _():
        for copy in after:
            copy.start()

    @pl.when(me < 4)
    def _():
        fill.start()

    for n, who in enumerate(far_ids):
        for t in range(3):
            got = target(spot(who, rep), part, t)
            send(got, got, far_send.at[n, t], far_recv.at[who, t], at(rep, who)).wait_recv()
        block = wc_ref.at[pl.ds(spot(who, rep), part), :]
        for m, r in enumerate(rep_ids):
            copy = send(block, block, rep_send.at[n, m], rep_recv.at[n, m], at(r, me))
            copy.start()
            waits.append(copy)
    for half in range(2):
        got = token_rows(partner, half)
        send(got, got, tok_send.at[0, half], tok_recv.at[0, half], at(rep, partner)).wait_recv()
        copy = send(got, got, tok_send.at[2, half], tok_recv.at[2, half], at(rep, sibling))
        copy.start()
        waits.append(copy)
    for copy in local:
        copy.wait()

    @pl.when(me < 4)
    def _():
        fill.wait()

    @pl.when(me >= 4)
    def _():
        after[0].wait_recv()

    @pl.when(sends_on)
    def _():
        for copy in after:
            copy.wait_send()

    for t in range(3):
        got = target(spot(sibling, 0), rows, t)
        send(got, got, side_send.at[t], side_recv.at[t], at(rep, sibling)).wait_recv()
    for half in range(2):
        for kind, who in ((1, sibling), (2, partner ^ 1)):
            got = token_rows(who, half)
            send(got, got, tok_send.at[kind, half], tok_recv.at[kind, half], at(rep, sibling)).wait_recv()
    for n, who in enumerate(far_ids):
        for m in range(reps - 1):
            block = wc_ref.at[pl.ds(spot(who, (rep + reps - 1 - m) % reps), part), :]
            send(block, block, rep_send.at[n, m], rep_recv.at[n, m], at(rep_ids[m], me)).wait_recv()
    for copy in waits:
        copy.wait_send()


def gather_weight(weight, tokens, reps, count):
    rows, full = weight.shape
    own = full // 4
    far = count - 2
    dma = pltpu.SemaphoreType.DMA
    return pl.pallas_call(
        functools.partial(gather_kernel, reps, count),
        in_specs=[pl.BlockSpec(memory_space=pl.ANY)] * 3,
        out_specs=[pl.BlockSpec(memory_space=pl.ANY)] * 2,
        out_shape=[
            jax.ShapeDtypeStruct((rows * count, own), weight.dtype),
            jax.ShapeDtypeStruct((tokens.shape[0] * 4 + 2 * EDGE, tokens.shape[1]), tokens.dtype),
        ],
        scratch_shapes=[
            dma((7,)), dma((3,)), dma((3,)), dma((far, 3)), dma((count, 3)), dma((far, reps - 1)), dma((far, reps - 1)),
            dma((3, 2)), dma((3, 2)), dma((4,)), dma((1,)),
        ],
        cost_estimate=pl.CostEstimate(flops=40_000_000_000, bytes_accessed=20_000_000, transcendentals=0),
        compiler_params=pltpu.CompilerParams(collective_id=1, has_side_effects=True),
        name="gather_weight",
    )(weight, tokens, jnp.zeros((EDGE, tokens.shape[1]), tokens.dtype))


def frame_gather_kernel(x_ref, f_ref, own_sem, send_sem, recv_sem):
    rep = lax.axis_index("rep")
    me = lax.axis_index("seq")
    chip, core = me // 2, me % 2
    half_rows = x_ref.shape[0] // 2
    sibling = (rep, chip * 2 + 1 - core)
    partner = (rep, (chip ^ 1) * 2 + core)
    meet([sibling, partner])

    def rows(who, half):
        return f_ref.at[pl.ds(pl.multiple_of((who % 4) * 2 * half_rows + half * half_rows, 16), half_rows), :]

    waits = []

    def push(src, dst, kind, half, peer):
        copy = send(src, dst, send_sem.at[kind, half], recv_sem.at[kind, half], peer)
        copy.start()
        waits.append(copy)

    for half in range(2):
        push(x_ref.at[pl.ds(half * half_rows, half_rows), :], rows(me, half), 0, half, partner)
    for half in range(2):
        push(x_ref.at[pl.ds(half * half_rows, half_rows), :], rows(me, half), 1, half, sibling)
    local = pltpu.make_async_copy(
        x_ref, f_ref.at[pl.ds(pl.multiple_of((me % 4) * 2 * half_rows, 16), 2 * half_rows), :], own_sem.at[0]
    )
    local.start()

    def arrived(kind, half, who):
        got = rows(who, half)
        send(got, got, send_sem.at[kind, half], recv_sem.at[kind, half], sibling).wait_recv()
        return got

    for half in range(2):
        got = arrived(0, half, partner[1])
        push(got, got, 2, half, sibling)
    local.wait()
    for half in range(2):
        arrived(1, half, sibling[1])
        arrived(2, half, partner[1] ^ 1)
    for copy in waits:
        copy.wait_send()


def frame_gather(values):
    dma = pltpu.SemaphoreType.DMA
    return pl.pallas_call(
        frame_gather_kernel,
        in_specs=[pl.BlockSpec(memory_space=pl.ANY)],
        out_specs=pl.BlockSpec(memory_space=pl.ANY),
        out_shape=jax.ShapeDtypeStruct((values.shape[0] * 4, values.shape[1]), values.dtype),
        scratch_shapes=[dma((1,)), dma((3, 2)), dma((3, 2))],
        cost_estimate=pl.CostEstimate(flops=20_000_000_000, bytes_accessed=8_000_000, transcendentals=0),
        compiler_params=pltpu.CompilerParams(collective_id=2, has_side_effects=True),
        name="frame_gather",
    )(values)


def frame_swap_kernel(h_ref, r_ref, own_sem, send_sem, recv_sem):
    rep = lax.axis_index("rep")
    me = lax.axis_index("seq")
    base, place = me // 4 * 4, me % 4
    rows = r_ref.shape[0]
    cols = h_ref.shape[1]
    peers = [base + (place ^ n) for n in (2, 3, 1)]
    meet([(rep, who) for who in peers])

    def block(who):
        return h_ref.at[pl.ds(pl.multiple_of((who % 4) * rows, 16), rows), :]

    def spot(who):
        return r_ref.at[:, pl.ds(pl.multiple_of((who % 4) * cols, LANES), cols)]

    copies = [
        send(block(who), spot(me), send_sem.at[n], recv_sem.at[n], (rep, who)) for n, who in enumerate(peers)
    ]
    for copy in copies:
        copy.start()
    local = pltpu.make_async_copy(block(me), spot(me), own_sem.at[0])
    local.start()
    local.wait()
    for n, who in enumerate(peers):
        send(block(who), spot(who), send_sem.at[n], recv_sem.at[n], (rep, who)).wait_recv()
    for copy in copies:
        copy.wait_send()


def frame_swap(values):
    dma = pltpu.SemaphoreType.DMA
    return pl.pallas_call(
        frame_swap_kernel,
        in_specs=[pl.BlockSpec(memory_space=pl.ANY)],
        out_specs=pl.BlockSpec(memory_space=pl.ANY),
        out_shape=jax.ShapeDtypeStruct((values.shape[0] // 4, values.shape[1] * 4), values.dtype),
        scratch_shapes=[dma((1,)), dma((3,)), dma((3,))],
        cost_estimate=pl.CostEstimate(flops=10_000_000_000, bytes_accessed=2_000_000, transcendentals=0),
        compiler_params=pltpu.CompilerParams(collective_id=3, has_side_effects=True),
        name="frame_swap",
    )(values)


def small_sum_kernel(reps, count, v_ref, o_ref, one_ref, two_ref, sum_ref, send1, recv1, send2, recv2):
    rep = lax.axis_index("rep")
    me = lax.axis_index("seq")
    rep_ids = [(rep + k) % reps for k in range(1, reps)]
    seq_ids = [(me + k) % count for k in range(1, count)]
    meet([(r, me) for r in rep_ids] + [(rep, s) for s in seq_ids])
    waits = []
    for m, r in enumerate(rep_ids):
        copy = send(v_ref, one_ref.at[rep], send1.at[m], recv1.at[rep], (r, me))
        copy.start()
        waits.append(copy)
    one_ref[rep] = v_ref[...]
    for m, r in enumerate(rep_ids):
        send(v_ref, one_ref.at[r], send1.at[m], recv1.at[r], (r, me)).wait_recv()
    total = one_ref[0]
    for r in range(1, reps):
        total = total + one_ref[r]
    sum_ref[...] = total
    for m, s in enumerate(seq_ids):
        copy = send(sum_ref, two_ref.at[me], send2.at[m], recv2.at[me], (rep, s))
        copy.start()
        waits.append(copy)
    two_ref[me] = total
    for m, s in enumerate(seq_ids):
        send(sum_ref, two_ref.at[s], send2.at[m], recv2.at[s], (rep, s)).wait_recv()
    total = two_ref[0]
    for s in range(1, count):
        total = total + two_ref[s]
    o_ref[...] = total
    for copy in waits:
        copy.wait_send()


def small_sum(values, reps, count):
    size = values.shape[0]
    rows = -(-size // (8 * LANES)) * 8
    shaped = jnp.pad(values, (0, rows * LANES - size)).reshape(rows, LANES)
    dma = pltpu.SemaphoreType.DMA
    vmem = pl.BlockSpec(memory_space=pltpu.VMEM)
    out = pl.pallas_call(
        functools.partial(small_sum_kernel, reps, count),
        in_specs=[vmem],
        out_specs=vmem,
        out_shape=jax.ShapeDtypeStruct(shaped.shape, jnp.float32),
        scratch_shapes=[
            pltpu.VMEM((reps, rows, LANES), jnp.float32), pltpu.VMEM((count, rows, LANES), jnp.float32),
            pltpu.VMEM((rows, LANES), jnp.float32),
            dma((reps - 1,)), dma((reps,)), dma((count - 1,)), dma((count,)),
        ],
        compiler_params=pltpu.CompilerParams(collective_id=4, has_side_effects=True),
        name="small_sum",
    )(shaped)
    return out.reshape(-1)[:size]


def reduce_kernel(
    reps, count, gi_ref, go_ref, dn_ref, oi_ref, oo_ref, od_ref,
    li_ref, ri_ref, zi_ref, qi_ref, lo_ref, ro_ref, zo_ref, qo_ref, ld_ref, bd_ref, hd_ref,
    load_sem, one_send, one_recv, two_send, two_recv, three_send, three_recv, tok_send, tok_recv,
    head_send, head_recv,
):
    rep = lax.axis_index("rep")
    me = lax.axis_index("seq")
    chip, core = me // 2, me % 2
    base, place = me // 4 * 4, me % 4
    sibling = chip * 2 + 1 - core
    partner = (chip ^ 1) * 2 + core
    rep_ids = [(rep + k) % reps for k in range(1, reps)]
    seq_ids = [(me + k) % count for k in range(1, count)]
    part = li_ref.shape[1]
    rows = part * reps
    halves = lo_ref.shape[0]
    cols = gi_ref.shape[1] // 3
    width = cols * 4
    tokens = od_ref.shape[0]
    meet([(r, me) for r in rep_ids] + [(rep, s) for s in seq_ids])
    waits = []

    def push(src, dst, send_sem, recv_sem, peer):
        copy = send(src, dst, send_sem, recv_sem, peer)
        copy.start()
        waits.append(copy)

    def arrived(dst, send_sem, recv_sem):
        send(dst, dst, send_sem, recv_sem, (rep, sibling)).wait_recv()

    def quarter(ref, who, r):
        return ref.at[pl.ds(pl.multiple_of(who * rows + r * part, 16), part), :]

    def token_rows(who):
        return dn_ref.at[pl.ds(pl.multiple_of(EDGE + (who % 4) * tokens, 16), tokens), :]

    ahead = send(
        dn_ref.at[pl.ds(EDGE - HEADER, HEADER), :], hd_ref.at[place], head_send.at[0], head_recv.at[place],
        (rep, lax.rem(base + count - 1, count)),
    )

    @pl.when(me >= 4)
    def _():
        ahead.start()

    push(token_rows(partner ^ 1), bd_ref.at[0], tok_send.at[0], tok_recv.at[0], (rep, sibling))
    push(token_rows(sibling), bd_ref.at[1], tok_send.at[1], tok_recv.at[1], (rep, sibling))
    loads = [
        pltpu.make_async_copy(token_rows(partner), ld_ref.at[0], load_sem.at[0]),
        pltpu.make_async_copy(token_rows(me), ld_ref.at[1], load_sem.at[1]),
    ]
    for copy in loads:
        copy.start()
    order = seq_ids + [me]
    for h in range(halves):
        for m, r in enumerate(rep_ids):
            push(quarter(go_ref, h, r), ro_ref.at[m, h], one_send.at[count + h, m], one_recv.at[count + h, m], (r, me))
    for n, who in enumerate(order):
        for m, r in enumerate(rep_ids):
            push(quarter(gi_ref, who, r), ri_ref.at[m, n], one_send.at[n, m], one_recv.at[n, m], (r, me))
    own = [pltpu.make_async_copy(quarter(gi_ref, who, rep), li_ref.at[n], load_sem.at[2 + n]) for n, who in enumerate(order)]
    own += [
        pltpu.make_async_copy(quarter(go_ref, h, rep), lo_ref.at[h], load_sem.at[2 + count + h]) for h in range(halves)
    ]
    for copy in own:
        copy.start()

    loads[0].wait()
    arrived(bd_ref.at[0], tok_send.at[0], tok_recv.at[0])
    wide = jnp.float32
    ld_ref[0] = (ld_ref[0].astype(wide) + bd_ref[0].astype(wide)).astype(jnp.bfloat16)
    push(ld_ref.at[0], bd_ref.at[2], tok_send.at[2], tok_recv.at[2], (rep, partner))

    def over_reps(local_ref, rest_ref, n, sems):
        total = local_ref[n].astype(wide)
        for m in range(reps - 1):
            arrived(rest_ref.at[m, n], one_send.at[sems, m], one_recv.at[sems, m])
            total = total + rest_ref[m, n].astype(wide)
        local_ref[n] = total.astype(jnp.bfloat16)

    frames = count // 4
    for h in range(halves):
        own[count + h].wait()
        over_reps(lo_ref, ro_ref, h, count + h)
        owner = place * halves + h

        @pl.when(owner == me)
        def _():
            zo_ref[me // 4] = lo_ref[h]

        @pl.when(owner != me)
        def _():
            send(lo_ref.at[h], zo_ref.at[me // 4], two_send.at[count + h], two_recv.at[count + me // 4], (rep, owner)).start()

    for n, who in enumerate(order):
        own[n].wait()
        over_reps(li_ref, ri_ref, n, n)
        if n < count - 1:
            push(li_ref.at[n], zi_ref.at[me], two_send.at[n], two_recv.at[me], (rep, who))
        else:
            zi_ref[me] = li_ref[n]

    loads[1].wait()
    arrived(bd_ref.at[1], tok_send.at[1], tok_recv.at[1])
    arrived(bd_ref.at[2], tok_send.at[2], tok_recv.at[2])
    od_ref[...] = ld_ref[1].astype(wide) + bd_ref[1].astype(wide) + bd_ref[2].astype(wide)

    @pl.when((place == 3) & (me < count - 4))
    def _():
        total = od_ref[tokens - HEADER :, :]
        for v in range(4):
            arrived(hd_ref.at[v], head_send.at[0], head_recv.at[v])
            total = total + hd_ref[v].astype(wide)
        od_ref[tokens - HEADER :, :] = total

    @pl.when(me >= 4)
    def _():
        ahead.wait_send()

    for f in range(frames):
        source = f * 4 + me // halves

        @pl.when(source != me)
        def _():
            arrived(zo_ref.at[f], two_send.at[count], two_recv.at[count + f])

    total = zo_ref[0].astype(wide)
    for f in range(1, frames):
        total = total + zo_ref[f].astype(wide)
    qo_ref[...] = total.astype(jnp.bfloat16)
    for m, r in enumerate(rep_ids):
        push(qo_ref, oo_ref.at[pl.ds(pl.multiple_of(rep * part, 16), part), :], three_send.at[0, m], three_recv.at[0, m], (r, me))
    for n, who in enumerate(seq_ids):
        arrived(zi_ref.at[who], two_send.at[n], two_recv.at[who])
    for u in range(4):
        total = zi_ref[u].astype(wide)
        for f in range(1, frames):
            total = total + zi_ref[f * 4 + u].astype(wide)
        for t in range(3):
            qi_ref[:, t * width + u * cols : t * width + (u + 1) * cols] = total[:, t * cols : (t + 1) * cols].astype(
                jnp.bfloat16
            )
    for m, r in enumerate(rep_ids):
        push(qi_ref, oi_ref.at[pl.ds(pl.multiple_of(rep * part, 16), part), :], three_send.at[1, m], three_recv.at[1, m], (r, me))
    final = [
        pltpu.make_async_copy(qo_ref, oo_ref.at[pl.ds(pl.multiple_of(rep * part, 16), part), :], load_sem.at[0]),
        pltpu.make_async_copy(qi_ref, oi_ref.at[pl.ds(pl.multiple_of(rep * part, 16), part), :], load_sem.at[1]),
    ]
    for copy in final:
        copy.start()
    for h in range(halves):
        owner = place * halves + h

        @pl.when(owner != me)
        def _():
            send(lo_ref.at[h], zo_ref.at[me // 4], two_send.at[count + h], two_recv.at[count + me // 4], (rep, owner)).wait_send()

    for copy in final:
        copy.wait()
    for m in range(reps - 1):
        r = (rep + reps - 1 - m) % reps
        for n, ref in ((0, oo_ref), (1, oi_ref)):
            arrived(ref.at[pl.ds(pl.multiple_of(r * part, 16), part), :], three_send.at[n, m], three_recv.at[n, m])
    for copy in waits:
        copy.wait_send()


def reduce_weights(grad_in, grad_out, tokens, reps, count):
    width = grad_out.shape[1]
    own = grad_in.shape[1]
    rows = width // count
    part = rows // reps
    halves = grad_out.shape[0] // rows
    frames = count // 4
    each = (tokens.shape[0] - 2 * EDGE) // 4
    dma = pltpu.SemaphoreType.DMA
    low = jnp.bfloat16
    hbm = pl.BlockSpec(memory_space=pl.ANY)
    return pl.pallas_call(
        functools.partial(reduce_kernel, reps, count),
        in_specs=[hbm] * 3,
        out_specs=[hbm, hbm, pl.BlockSpec(memory_space=pltpu.VMEM)],
        out_shape=[
            jax.ShapeDtypeStruct((rows, 3 * width), low),
            jax.ShapeDtypeStruct((rows, width), low),
            jax.ShapeDtypeStruct((each, width), jnp.float32),
        ],
        scratch_shapes=[
            pltpu.VMEM((count, part, own), low), pltpu.VMEM((reps - 1, count, part, own), low),
            pltpu.VMEM((count, part, own), low), pltpu.VMEM((part, 3 * width), low),
            pltpu.VMEM((halves, part, width), low), pltpu.VMEM((reps - 1, halves, part, width), low),
            pltpu.VMEM((frames, part, width), low), pltpu.VMEM((part, width), low),
            pltpu.VMEM((2, each, width), low), pltpu.VMEM((3, each, width), low),
            pltpu.VMEM((4, HEADER, width), low),
            dma((2 + count + halves,)), dma((count + halves, reps - 1)), dma((count + halves, reps - 1)),
            dma((count + halves,)), dma((count + frames,)), dma((2, reps - 1)), dma((2, reps - 1)), dma((3,)), dma((3,)),
            dma((1,)), dma((4,)),
        ],
        cost_estimate=pl.CostEstimate(flops=70_000_000_000, bytes_accessed=20_000_000, transcendentals=0),
        compiler_params=pltpu.CompilerParams(collective_id=5, has_side_effects=True, vmem_limit_bytes=40 << 20),
        name="reduce_weights",
    )(grad_in, grad_out, tokens)


def rms_scale(values):
    return lax.rsqrt(jnp.mean(values * values, axis=-1, keepdims=True) + EPS)


def norm_back(grad_out, values, inv_scale, gain):
    scaled_grad = grad_out * gain
    inner = jnp.mean(scaled_grad * values, axis=-1, keepdims=True)
    return inv_scale * scaled_grad - values * inv_scale**3 * inner


def pad_heads(values, dim):
    shaped = values.reshape(values.shape[:-1] + (-1, dim))
    shaped = jnp.pad(shaped, [(0, 0)] * (shaped.ndim - 1) + [(0, LANES - dim)])
    return shaped.reshape(values.shape[:-1] + (-1,))


def cut_heads(values, dim):
    shaped = values.reshape(values.shape[:-1] + (-1, LANES))[..., :dim]
    return shaped.reshape(values.shape[:-1] + (-1,))


def on_device(
    inputs, segment_ids, valid_mask, input_weight, output_weight, conv_kernel, head_mix, first_gain, second_gain,
    group_gain, gate_weight, up_weight, down_weight, cotangent,
):
    tokens, width = inputs.shape[1:]
    heads, taps, span = conv_kernel.shape
    dim = width // heads
    scale = dim ** (-0.5)
    count = lax.axis_size("seq")
    team = FRAME // tokens
    own_heads = heads // team
    own_width = own_heads * dim
    own_pairs = own_heads // 2
    groups = [[g * team + i for i in range(team)] for g in range(count // team)]
    seq_rank = lax.axis_index("seq")
    place = seq_rank % team
    frame_first = (seq_rank // team) * FRAME
    row_first = seq_rank * tokens
    contract_rows = (((0,), (0,)), ((), ()))

    resid_in = inputs[0].astype(jnp.float32)
    grad_out = cotangent[0].astype(jnp.float32)
    row_valid = lax.dynamic_slice_in_dim(valid_mask[0], row_first, tokens).astype(jnp.float32)[:, None]
    ahead = lambda values: jnp.pad(values, (HEADER, 0))
    codes = make_codes(
        lax.dynamic_slice_in_dim(ahead(segment_ids[0]), frame_first, FRAME + HEADER),
        lax.dynamic_slice_in_dim(ahead(valid_mask[0]), frame_first, FRAME + HEADER),
    )
    own_kernel = lax.dynamic_slice_in_dim(conv_kernel, place * own_heads, own_heads)
    own_mix = lax.dynamic_slice_in_dim(head_mix, place * own_pairs, own_pairs).reshape(own_pairs, 4)
    own_gain = pad_heads(lax.dynamic_slice_in_dim(group_gain, place * own_width, own_width)[None], dim)
    toep, toep_split = split_toeplitz(toeplitz(own_kernel, scale))

    reps = lax.axis_size("rep")
    direct = team == 4 and (width // count) % (16 * reps) == 0
    first_scale = rms_scale(resid_in)
    normed_in = (resid_in * first_scale * first_gain).astype(jnp.bfloat16)
    if direct:
        own_input, normed_frame = gather_weight(input_weight, normed_in, reps, count)
    else:
        full_input = lax.all_gather(input_weight, "seq", axis=0, tiled=True)
        own_input = lax.dynamic_slice_in_dim(full_input.reshape(width, 3, width), place * own_width, own_width, axis=2)
        own_input = own_input.reshape(width, 3 * own_width)
        normed_frame = lax.all_gather(normed_in, "seq", axis=0, tiled=True, axis_index_groups=groups)
        ends = lax.all_gather(normed_in[tokens - HEADER :], "seq", axis=0)
        last = jnp.maximum(seq_rank // team * team - 1, 0)
        end = jnp.where(frame_first > 0, lax.dynamic_index_in_dim(ends, last, keepdims=False), 0)
        lead = jnp.zeros((EDGE - HEADER, width), jnp.bfloat16)
        normed_frame = jnp.concatenate([lead, end, normed_frame, jnp.zeros((EDGE, width), jnp.bfloat16)], axis=0)
    dmlp = (row_valid * grad_out).astype(jnp.bfloat16)
    own_input, output_weight, dmlp = lax.optimization_barrier((own_input, output_weight, dmlp))
    full_output = lax.all_gather(output_weight, "seq", axis=0, tiled=True)
    own_input = pad_heads(own_input, dim)
    proj = jnp.dot(normed_frame, own_input, preferred_element_type=jnp.float32).astype(jnp.bfloat16)
    dmlp_all = lax.all_gather(dmlp, "seq", axis=0, tiled=True)
    normed_own, att, prob = attention_forward(proj, toep_split, codes, own_gain, own_mix, dim, taps)
    normed_own, full_output = lax.optimization_barrier((normed_own, full_output))
    normed_own = cut_heads(normed_own, dim)

    def to_rows(values):
        moved = lax.all_to_all(
            values.reshape(team, tokens, own_width), "seq", 0, 0, tiled=True, axis_index_groups=groups
        )
        return moved.transpose(1, 0, 2).reshape(tokens, width)

    normed = frame_swap(normed_own) if direct else to_rows(normed_own)
    branch = jnp.dot(normed, full_output, preferred_element_type=jnp.float32)
    resid = resid_in + row_valid * branch
    second_scale = rms_scale(resid)
    normed_mid = (resid * second_scale * second_gain).astype(jnp.bfloat16)
    normed_mid, dmlp_all = lax.optimization_barrier((normed_mid, dmlp_all))
    inputs_all = lax.all_gather(normed_mid, "seq", axis=0, tiled=True)
    gate = jnp.dot(inputs_all, gate_weight, preferred_element_type=jnp.float32)
    up_proj = jnp.dot(inputs_all, up_weight, preferred_element_type=jnp.float32)
    dhidden = jnp.dot(dmlp_all, down_weight.T, preferred_element_type=jnp.float32)
    sigmoid_gate = jax.nn.sigmoid(gate)
    gate_grad = (dhidden * up_proj * sigmoid_gate * (1.0 + gate * (1.0 - sigmoid_gate))).astype(jnp.bfloat16)
    up_grad = (dhidden * gate * sigmoid_gate).astype(jnp.bfloat16)
    hidden = (jax.nn.silu(gate) * up_proj).astype(jnp.bfloat16)
    dmid_part = (
        jnp.dot(gate_grad, gate_weight.T, preferred_element_type=jnp.float32)
        + jnp.dot(up_grad, up_weight.T, preferred_element_type=jnp.float32)
    ).astype(jnp.bfloat16)
    gate_grad, up_grad, hidden, dmid_part = lax.optimization_barrier((gate_grad, up_grad, hidden, dmid_part))
    dmid_low = lax.psum_scatter(dmid_part, "seq", scatter_dimension=0, tiled=True)
    mlp_part = jnp.dot(hidden, down_weight, preferred_element_type=jnp.float32).astype(jnp.bfloat16)
    mlp_grads = [
        lax.dot_general(left, right, contract_rows, preferred_element_type=jnp.float32).astype(jnp.bfloat16)
        for left, right in ((inputs_all, gate_grad), (inputs_all, up_grad), (hidden, dmlp_all))
    ]
    dmid_low, mlp_part, mlp_grads = lax.optimization_barrier((dmid_low, mlp_part, mlp_grads))
    mlp_low = lax.psum_scatter(mlp_part, "seq", scatter_dimension=0, tiled=True)
    mlp_grads = [lax.psum(value, "rep") for value in mlp_grads]
    dmid = dmid_low.astype(jnp.float32)
    second_part = jnp.sum(dmid * resid * second_scale, axis=0)
    dresid = grad_out + norm_back(dmid, resid, second_scale, second_gain)
    dbranch = (row_valid * dresid).astype(jnp.bfloat16)
    if direct:
        dbranch_frame = frame_gather(dbranch)
    else:
        dbranch_frame = lax.all_gather(dbranch, "seq", axis=0, tiled=True, axis_index_groups=groups)
    own_output = lax.dynamic_slice_in_dim(full_output, place * own_width, own_width, axis=0)
    dnormed_own = lax.dot_general(dbranch_frame, own_output, NT, preferred_element_type=jnp.float32)
    own_output_grad = lax.dot_general(normed_own, dbranch_frame, contract_rows, preferred_element_type=jnp.float32)
    dq, dk, dv, dtoep, dmix, dgain = attention_backward(
        proj, toep, codes, prob, att, pad_heads(dnormed_own, dim), own_gain, own_mix, dim, taps
    )
    dproj = jnp.concatenate([dq, dk, dv], axis=1)
    own_input_grad = lax.dot_general(normed_frame, dproj, contract_rows, preferred_element_type=jnp.float32)
    own_input_grad = cut_heads(own_input_grad.astype(jnp.bfloat16), dim)
    own_output_grad = own_output_grad.astype(jnp.bfloat16)
    dnormin_part = lax.dot_general(dproj, own_input, NT, preferred_element_type=jnp.float32).astype(jnp.bfloat16)
    if direct:
        grad_input_w, grad_output_w, dnormin = reduce_weights(own_input_grad, own_output_grad, dnormin_part, reps, count)
    else:
        dnormin = lax.psum_scatter(
            dnormin_part[EDGE : EDGE + FRAME], "seq", scatter_dimension=0, tiled=True, axis_index_groups=groups
        ).astype(jnp.float32)
        starts = lax.all_gather(dnormin_part[EDGE - HEADER : EDGE], "seq", axis=0).astype(jnp.float32)
        later = lax.dynamic_slice_in_dim(
            jnp.pad(starts, ((0, team), (0, 0), (0, 0))), (seq_rank // team + 1) * team, team
        ).sum(axis=0)
        later = jnp.where(place == team - 1, later, 0.0)
        dnormin = dnormin + jnp.pad(later, ((tokens - HEADER, 0), (0, 0)))
        pieces = lax.all_to_all(own_input_grad.reshape(count, width // count, 3 * own_width), "seq", 0, 0, tiled=True)
        pieces = pieces.reshape(count // team, team, width // count, 3, own_width).astype(jnp.float32).sum(axis=0)
        grad_input_w = pieces.transpose(1, 2, 0, 3).reshape(width // count, 3 * width)
        spots = jnp.zeros((width, width), jnp.bfloat16)
        spots = lax.dynamic_update_slice_in_dim(spots, own_output_grad, place * own_width, 0)
        grad_output_w = lax.psum_scatter(spots, "seq", scatter_dimension=0, tiled=True)
        grad_input_w, grad_output_w = [
            lax.psum(value.astype(jnp.bfloat16), "rep") for value in (grad_input_w, grad_output_w)
        ]
    dnormin, mlp_low, mlp_grads = lax.optimization_barrier((dnormin, mlp_low, mlp_grads))
    result = resid + row_valid * mlp_low.astype(jnp.float32)
    first_part = jnp.sum(dnormin * resid_in * first_scale, axis=0)
    grad_in = dresid + norm_back(dnormin, resid_in, first_scale, first_gain)

    def spread(values, size):
        empty = jnp.zeros((size,) + values.shape[1:], jnp.float32)
        return lax.dynamic_update_slice_in_dim(empty, values, place * values.shape[0], 0)

    kernel_part = spread(toeplitz_grad(dtoep, taps, span, scale), heads)
    mix_part = spread(jnp.sum(dmix[:, :4], axis=-1).reshape(own_pairs, 2, 2), heads // 2)
    group_part = spread(cut_heads(dgain, dim)[0], width)
    parts = (kernel_part, mix_part, first_part, second_part, group_part)
    if direct:
        flat = small_sum(jnp.concatenate([value.reshape(-1) for value in parts]), reps, count)
        summed, start = [], 0
        for value in parts:
            summed.append(flat[start : start + value.size].reshape(value.shape))
            start += value.size
    else:
        summed = lax.psum(parts, ("rep", "seq"))
    grad_kernel, grad_mix, grad_first, grad_second, grad_group = summed
    grads = [value.astype(jnp.float32) for value in (grad_input_w, grad_output_w, *mlp_grads)]
    return (
        result.astype(jnp.bfloat16)[None], grad_in.astype(jnp.bfloat16)[None], grads[0], grads[1], grad_kernel,
        grad_mix, grad_first, grad_second, grad_group, grads[2], grads[3], grads[4],
    )


def solution(mesh):
    in_specs = (
        P("rep", "seq", None), P("rep", None), P("rep", None), P("seq", None), P("seq", None), P(), P(), P(), P(), P(),
        P(None, "seq"), P(None, "seq"), P("seq", None), P("rep", "seq", None),
    )
    out_specs = (
        P("rep", "seq", None), P("rep", "seq", None), P("seq", None), P("seq", None), P(), P(), P(), P(), P(),
        P(None, "seq"), P(None, "seq"), P("seq", None),
    )
    return jax.shard_map(on_device, mesh=mesh, in_specs=in_specs, out_specs=out_specs, check_vma=False)
```

time: 4040 us -> 682 us (0.17)
  other arithmetic: 2010 us -> 56.1 us
  local copies, waits for them, and re-layouts: 852 us -> 56.3 us
  waiting for transfers between devices: 815 us -> 94.3 us
  Pallas kernels: 0 us -> 351 us
  matrix products: 225 us -> 96.7 us
  blocking collectives: 41.8 us -> 0 us
    mul x25 -> x1, other arithmetic: 1010 us -> 0.1 us  [toeplitz(): weight = jnp.repeat(kernel[:, :, b] * scale, LANES, axis=1)[:, None, :]]
    another operation x596 -> x3, local copies, waits for them, and re-layouts: 691 us -> 1 us  [the longest x1 0.83 us: toeplitz_grad(): return jnp.stack(cols, axis=-1)]
    reduce_sum x60 -> x14, other arithmetic: 643 us -> 12.9 us  [the longest x11 7.25 us: toeplitz_grad(): cols.append(jnp.sum(part.reshape(heads, taps, LANES), axis=-1) * scale)]
    pallas_call x0 -> x7, Pallas kernels: none -> 351 us  [the longest x1 97.7 us: reduce_weights(): pl.pallas_call(functools.partial(reduce_kernel, reps, count), in_specs=[h...]
    reduce_max x8 -> x0, other arithmetic: 277 us -> none  [attend_group(): peak = jnp.max(jnp.where(allowed, conv, -1e+30), axis=-1, keepdims=True)]
    reduce_scatter x4 -> x2, waiting for transfers between devices: 282 us -> 39.2 us  [the longest x1 39.2 us: on_device(): lax.psum_scatter(dmid_part, 'seq', scatter_dimension=0, tiled=True)]
    ppermute x8 -> x0, waiting for transfers between devices: 147 us -> none  [from_behind(): return lax.ppermute(x, axis, pairs)]
    all_gather x2 -> x1, waiting for transfers between devices: 128 us -> 0.01 us  [on_device(): full_output = lax.all_gather(output_weight, 'seq', axis=0, tiled=True)]
  transfers between devices with their start and end apart: 17 -> 6, of which waited for: 12 -> 2; matrix products, arithmetic and copies ran while one was open for 74% -> 20% of each run, Pallas kernels for 0% -> 39%
where the time goes in v1:
time: 682 us; the launch traced here: 670 us
  Pallas kernels  351 us (51%)
  matrix products  96.7 us (14%)
  waiting for transfers between devices  94.3 us (14%)
  local copies, waits for them, and re-layouts  56.3 us (8%)
  other arithmetic  56.1 us (8%)
  between operations  15.3 us (2%)
    pallas_call x1, Pallas kernels, reduce_weights(): pl.pallas_call(functools.partial(reduce_kernel, reps, count), in_specs=[h...  97.7 us
    pallas_call x1, Pallas kernels, attention_backward(): pl.pallas_call(functools.partial(backward_kernel, dim, taps), grid=(pairs...  71.3 us
    pallas_call x1, Pallas kernels, attention_forward(): pl.pallas_call(functools.partial(forward_kernel, dim, taps), grid=(pairs,...  66.3 us
    all_gather x1, waiting for transfers between devices, on_device(): inputs_all = lax.all_gather(normed_mid, 'seq', axis=0, tiled=True)  54.3 us
    pallas_call x1, Pallas kernels, gather_weight(): pl.pallas_call(functools.partial(gather_kernel, reps, count), in_specs=[p...  52.2 us
    reduce_scatter x1, waiting for transfers between devices, on_device(): lax.psum_scatter(dmid_part, 'seq', scatter_dimension=0, tiled=True)  39.2 us
    pallas_call x1, Pallas kernels, frame_gather(): pl.pallas_call(frame_gather_kernel, in_specs=[pl.BlockSpec(memory_space=p...  26.5 us
    pallas_call x1, Pallas kernels, frame_swap(): pl.pallas_call(frame_swap_kernel, in_specs=[pl.BlockSpec(memory_space=pl....  23.5 us
  transfers between devices with their start and end apart: 6, of which 2 were waited for; matrix products, arithmetic and copies ran while one was open for 20% of the time, Pallas kernels for 39%

profile of v1, /device:TPU:25, one launch (start us, length us, event | category | flops | bytes accessed | tf_op | source)
XLA Modules:
  0.0 670.3 jit_solution(17219749791187321898)
XLA Ops:
  15.2 52.2 %gather_weight.1 = (bf16[1536,1152]{1,0:T(8,128)(2,1)}, bf16[1152,1536]{1,0:T(8,128)(2,1)}) custom-call(bf16[192,4608]{1,0:T(8,128)(2,1)} %w_ref.1, bf16[256,1536]{1,0:T(8,128)(2,1)} %fusion.21.x_ref, bf16[64,1536]{1,0:T(8,128)(2,1)} %broadcast_in_dim.194.z_ref), custom_call_target="tpu_custom_call" | custom-call | flops 40000000000 | bytes 20000000 | tf_op jit(solution)/shard_map/gather_weight/pallas_call | solution.py:580
  71.7 5.8 copy.41
  87.3 7.1 %convolution_convert_fusion.3.q_ref.k_ref.v_ref = bf16[1152,1536]{1,0:T(8,128)(2,1)} fusion(bf16[1152,1536]{1,0:T(8,128)(2,1)S(1)} %copy-done.65, bf16[1536,1536]{0,1:T(8,128)(2,1)S(1)} %bitcast.158), kind=kOutput, calls=%fused_computation.4 | convolution fusion | flops 5437587456 | bytes 11796480 | tf_op jit(solution)/shard_map/dot_general | solution.py:1033
  94.7 66.3 %attend.1 = (bf16[1024,512]{1,0:T(8,128)(2,1)S(1)}, f32[1024,512]{1,0:T(8,128)S(1)}, f32[4,1024,1024]{2,1,0:T(8,128)}) custom-call(bf16[1152,1536]{1,0:T(8,128)(2,1)} %convolution_convert_fusion.3.q_ref.k_ref.v_ref, bf16[1152,1536]{1,0:T(8,128)(2,1)} %convolution_convert_fusion.3.q_ref.k_ref.v_ref, ...), custom_call_target="tpu_custom_call" | custom-call | flops 60000002048 | bytes 40000000 | tf_op jit(solution)/shard_map/attend/pallas_call | solution.py:311
  166.8 23.5 %frame_swap.1 = bf16[256,1536]{1,0:T(8,128)(2,1)} custom-call(bf16[1024,384]{1,0:T(8,128)(2,1)} %copy.55.h_ref), custom_call_target="tpu_custom_call" | custom-call | flops 10000000000 | bytes 2000000 | tf_op jit(solution)/shard_map/frame_swap/pallas_call | solution.py:687
  196.5 8.6 %fusion.44 = f32[2048,512]{1,0:T(8,128)} fusion(bf16[2048,1536]{1,0:T(8,128)(2,1)} %all-gather.6.cloned.1.call-done, bf16[512,1536]{1,0:T(8,128)(2,1)} %param.26), kind=kOutput, calls=%fused_computation.150 | convolution fusion | flops 3221225472 | bytes 12058624 | tf_op jit(solution)/shard_map/dot_general | solution.py:1054
  205.1 54.3 %all-gather.8.cloned.1.call-done = bf16[2048,1536]{1,0:T(8,128)(2,1)} async-done(((bf16[256,1536]{1,0:T(8,128)(2,1)}), bf16[2048,1536]{1,0:T(8,128)(2,1)}) %all-gather.8.cloned.1.call-update) | async-done | bytes 6291472 | tf_op jit(solution)/shard_map/all_gather | solution.py:1051
  259.5 6.1 fusion.45
  265.8 6.9 %multiply_convert_fusion = (bf16[2048,512]{1,0:T(8,128)(2,1)}, bf16[2048,512]{1,0:T(8,128)(2,1)}, bf16[2048,512]{1,0:T(8,128)(2,1)}) fusion(f32[2048,512]{1,0:T(8,128)S(1)} %fusion.45, f32[2048,512]{1,0:T(8,128)S(1)} %copy-done.64, bf16[2048,1536]{1,0:T(8,128)(2,1)S(1)} %copy-done.59, bf16[1536,512]{1,0:T(8,128)(2,1)S(1)} %copy-done), kind=kOutput, calls=%fused_computation.8 | convolution fusion | flops 3238002688 | bytes 22544384 | tf_op jit(solution)/shard_map/dot_general | solution.py:1053
  272.7 5.2 fusion.46
  277.9 7.5 %add_convert_fusion = bf16[2048,1536]{1,0:T(8,128)(2,1)} fusion(f32[2048,1536]{1,0:T(8,128)S(1)} %fusion.46, bf16[2048,512]{1,0:T(8,128)(2,1)} %get-tuple-element.62, bf16[1536,512]{1,0:T(8,128)(2,1)S(1)} %copy-done), kind=kOutput, calls=%fused_computation | convolution fusion | flops 3227516928 | bytes 22544384 | tf_op jit(solution)/shard_map/dot_general | solution.py:1061
  286.8 6.9 %convolution_convert_fusion.2 = bf16[2048,1536]{1,0:T(8,128)(2,1)} fusion(bf16[2048,512]{1,0:T(8,128)(2,1)} %get-tuple-element.60, bf16[512,1536]{1,0:T(8,128)(2,1)S(1)} %copy-done.61), kind=kOutput, calls=%fused_computation.3 | convolution fusion | flops 3224371200 | bytes 9961472 | tf_op jit(solution)/shard_map/dot_general | solution.py:1065
  293.7 8.2 %convolution_convert_fusion.4 = bf16[512,1536]{1,0:T(8,128)(2,1)} fusion(bf16[2048,512]{1,0:T(8,128)(2,1)} %get-tuple-element.60, bf16[2048,1536]{1,0:T(8,128)(2,1)} %all-gather.6.cloned.1.call-done), kind=kOutput, calls=%fused_computation.43 | convolution fusion | flops 3222011904 | bytes 9961472 | tf_op jit(solution)/shard_map/dot_general | solution.py:1067
  301.9 7.7 %convolution_convert_fusion.5 = bf16[1536,512]{1,0:T(8,128)(2,1)} fusion(bf16[2048,1536]{1,0:T(8,128)(2,1)} %all-gather.8.cloned.1.call-done, bf16[2048,512]{1,0:T(8,128)(2,1)S(1)} %copy-done.63), kind=kOutput, calls=%fused_computation.44 | convolution fusion | flops 3222011904 | bytes 9961472 | tf_op jit(solution)/shard_map/dot_general | solution.py:1067
  309.6 4.6 convolution_convert_fusion.6
  314.2 39.2 %reduce-scatter.3.cloned.1.call-done = bf16[256,1536]{1,0:T(8,128)(2,1)} async-done(((bf16[2048,1536]{1,0:T(8,128)(2,1)}), bf16[256,1536]{1,0:T(8,128)(2,1)}) %reduce-scatter.3.cloned.1.call-update) | async-done | bytes 786448 | tf_op jit(solution)/shard_map/reduce_scatter | solution.py:1064
  358.1 26.5 %frame_gather.1 = bf16[1024,1536]{1,0:T(8,128)(2,1)} custom-call(bf16[256,1536]{1,0:T(8,128)(2,1)} %multiply_convert_fusion.3.x_ref), custom_call_target="tpu_custom_call" | custom-call | flops 20000000000 | bytes 8000000 | tf_op jit(solution)/shard_map/frame_gather/pallas_call | solution.py:644
  384.7 4.8 fusion.29
  395.9 71.3 %attend_back.1 = (bf16[1152,512]{1,0:T(8,128)(2,1)S(1)}, bf16[1152,512]{1,0:T(8,128)(2,1)S(1)}, bf16[1152,512]{1,0:T(8,128)(2,1)S(1)}, f32[4,256,768]{2,1,0:T(8,...) custom-call(bf16[1152,1536]{1,0:T(8,128)(2,1)} %convolution_convert_fusion.3.q_ref.k_ref.v_ref, ...), custom_call_target="tpu_custom_call" | custom-call | flops 70000001024 | bytes 40000000 | tf_op jit(solution)/shard_map/attend_back/pallas_call | solution.py:356
  468.4 5.0 select_reduce_fusion
  505.9 6.8 %convolution_convert_fusion.1 = bf16[1536,1536]{0,1:T(8,128)(2,1)S(1)} fusion(bf16[1152,1536]{1,0:T(8,128)(2,1)S(1)} %copy-done.66, bf16[1152,1536]{1,0:T(8,128)(2,1)S(1)} %constant_dynamic-update-slice_fusion), kind=kOutput, calls=%fused_computation.2 | convolution fusion | flops 5438177280 | bytes 11796480 | tf_op jit(solution)/shard_map/dot_general | solution.py:1088
  520.7 8.4 %convolution_convert_fusion.dn_ref = bf16[1152,1536]{1,0:T(8,128)(2,1)S(1)} fusion(bf16[1152,1536]{1,0:T(8,128)(2,1)S(1)} %copy-done.26, bf16[1536,1536]{0,1:T(8,128)(2,1)} %bitcast.159), kind=kOutput, calls=%fused_computation.1 | convolution fusion | flops 5437587456 | bytes 11796480 | tf_op jit(solution)/shard_map/dot_general | solution.py:1091
  529.1 97.7 %reduce_weights.1 = (bf16[192,4608]{1,0:T(8,128)(2,1)S(1)}, bf16[192,1536]{1,0:T(8,128)(2,1)S(1)}, f32[256,1536]{1,0:T(8,128)S(1)}) custom-call(bf16[1536,1152]{1,0:T(8,128)(2,1)S(1)} %copy-done.2, bf16[384,1536]{1,0:T(8,128)(2,1)S(1)} %convolution_convert_fusion.7.go_ref, bf16[1152,1536]{1,0:T(8,128)(2,1)S(1)} %convolution_convert_fusion.dn_ref), custom_call_target="tpu_custom_call" | custom-call | flops 70000001024 | bytes 20000000 | tf_op jit(solution)/shard_map/reduce_weights/pallas_call | solution.py:933
  631.7 13.1 %small_sum.1 = f32[48,128]{1,0:T(8,128)} custom-call(f32[48,128]{1,0:T(8,128)} %pad_bitcast_fusion.v_ref), custom_call_target="tpu_custom_call" | custom-call | tf_op jit(solution)/shard_map/small_sum/pallas_call | solution.py:738
  (289 shorter events, 111.3 us)
Async XLA Ops:
  7.2 258.4 %copy-start = (bf16[1536,512]{1,0:T(8,128)(2,1)S(1)}, bf16[1536,512]{1,0:T(8,128)(2,1)}, u32[]{:S(2)}) copy-start(bf16[1536,512]{1,0:T(8,128)(2,1)} %param.25) | copy-start | bytes 4718596
  7.2 156.0 %all-gather.4.cloned.1.call-start = ((), (), s32[]{:S(2)}) async-start(), calls=%async_computation.2 | async-start | bytes 5308416 | tf_op jit(solution)/shard_map/all_gather | solution.py:1031
  10.0 345.5 %copy-start.44 = (f32[1,256]{1,0:T(1,128)}, f32[1,256]{1,0:T(1,128)S(1)}, u32[]{:S(2)}) copy-start(f32[1,256]{1,0:T(1,128)S(1)} %fusion.41) | copy-start | bytes 3076
  15.2 53.0 %copy-start.32 = (f32[16,6,11]{0,1,2:T(8,128)S(1)}, f32[16,6,11]{0,1,2:T(8,128)}, u32[]{:S(2)}) copy-start(f32[16,6,11]{0,1,2:T(8,128)} %param.19) | copy-start | bytes 12676
  15.2 55.0 %copy-start.39 = (s32[1,2048]{1,0:T(1,128)S(1)}, s32[1,2048]{1,0:T(1,128)}, u32[]{:S(2)}) copy-start(s32[1,2048]{1,0:T(1,128)} %param.15) | copy-start | bytes 24580
  15.2 55.0 %copy-start.46 = (s32[1,2048]{1,0:T(1,128)S(1)}, s32[1,2048]{1,0:T(1,128)}, u32[]{:S(2)}) copy-start(s32[1,2048]{1,0:T(1,128)} %param.16) | copy-start | bytes 24580
  15.2 55.2 %copy-start.58 = (f32[8,2,2]{0,2,1:T(2,128)S(1)}, f32[8,2,2]{0,2,1:T(2,128)}, u32[]{:S(2)}) copy-start(f32[8,2,2]{0,2,1:T(2,128)} %param.20) | copy-start | bytes 388
  67.4 128.5 %all-gather.6.cloned.1.call-start = ((), (), s32[]{:S(2)}) async-start(), calls=%async_computation.3 | async-start | bytes 7077888 | tf_op jit(solution)/shard_map/all_gather | solution.py:1034
  68.1 191.3 %all-gather.8.cloned.1.call-start = ((), (), s32[]{:S(2)}) async-start(), calls=%async_computation.4 | async-start | bytes 7077888 | tf_op jit(solution)/shard_map/all_gather | solution.py:1051
  70.5 9.6 %copy-start.55 = (pred[768]{0:T(1024)(128)(4,1)}, pred[768]{0:T(1024)(128)(4,1)S(1)}, u32[]{:S(2)}) copy-start(pred[768]{0:T(1024)(128)(4,1)S(1)} %fusion.40) | copy-start | bytes 2308
  71.5 23.2 %copy-start.9 = (f32[2,4]{1,0:T(2,128)}, f32[2,4]{1,0:T(2,128)S(1)}, u32[]{:S(2)}) copy-start(f32[2,4]{1,0:T(2,128)S(1)} %copy.61.mix_ref) | copy-start | bytes 100
  80.0 14.5 %copy-start.20 = (bf16[1536,12,128]{0,2,1:T(8,128)(2,1)}, bf16[1536,12,128]{0,2,1:T(8,128)(2,1)S(1)}, u32[]{:S(2)}) copy-start(bf16[1536,12,128]{0,2,1:T(8,128)(2,1)S(1)} %pad.30) | copy-start | bytes 14155780
  194.6 160.9 %copy-start.12 = (f32[256,1536]{1,0:T(8,128)}, f32[256,1536]{1,0:T(8,128)S(1)}, u32[]{:S(2)}) copy-start(f32[256,1536]{1,0:T(8,128)S(1)} %get-tuple-element.140) | copy-start | bytes 4718596
  194.6 160.9 %copy-start.40 = (f32[256]{0:T(256)}, f32[256]{0:T(256)S(1)}, u32[]{:S(2)}) copy-start(f32[256]{0:T(256)S(1)} %get-tuple-element.138) | copy-start | bytes 3076
  194.7 160.9 %copy-start.47 = (f32[256]{0:T(256)}, f32[256]{0:T(256)S(1)}, u32[]{:S(2)}) copy-start(f32[256]{0:T(256)S(1)} %get-tuple-element.137) | copy-start | bytes 3076
  196.0 157.4 %reduce-scatter.3.cloned.1.call-start = ((), (), s32[]{:S(2)}) async-start(), calls=%async_computation.5 | async-start | bytes 7077888 | tf_op jit(solution)/shard_map/reduce_scatter | solution.py:1064
  285.4 345.0 %all-reduce.11.cloned.1.call-start = ((), (), s32[]{:S(2)}) async-start(), calls=%async_computation.7 | async-start | bytes 9437184 | tf_op jit(solution)/shard_map/psum | solution.py:1072
  293.7 15.9 %slice-start = ((s8[6291456]{0:T(1024)(128)(4,1)}), s8[4194304]{0:T(1024)(128)(4,1)S(1)}, s32[]{:S(2)}) async-start(s8[6291456]{0:T(1024)(128)(4,1)} %bitcast.188), calls=%async_computation.8 | async-start | bytes 8388608
  309.6 46.0 %copy-start.16 = (bf16[1,256,1536]{2,1,0:T(8,128)(2,1)S(1)}, bf16[1,256,1536]{2,1,0:T(8,128)(2,1)}, u32[]{:S(2)}) copy-start(bf16[1,256,1536]{2,1,0:T(8,128)(2,1)} %param.27) | copy-start | bytes 2359300
  355.5 29.2 %copy-start.49 = (f32[256]{0:T(256)}, f32[256]{0:T(256)S(1)}, u32[]{:S(2)}) copy-start(f32[256]{0:T(256)S(1)} %broadcast_multiply_fusion.1) | copy-start | bytes 3076
  393.3 237.1 %reduce-scatter.5.cloned.1.call-start = ((), (), s32[]{:S(2)}) async-start(), calls=%async_computation.6 | async-start | bytes 7077888 | tf_op jit(solution)/shard_map/reduce_scatter | solution.py:1071
  395.9 72.5 %copy-start.34 = (s32[768]{0:T(1024)S(1)}, s32[768]{0:T(1024)}, u32[]{:S(2)}) copy-start(s32[768]{0:T(1024)} %copy-done.33) | copy-start | bytes 9220
  395.9 72.5 %copy-start.36 = (s32[768]{0:T(1024)S(1)}, s32[768]{0:T(1024)}, u32[]{:S(2)}) copy-start(s32[768]{0:T(1024)} %copy-done.35) | copy-start | bytes 9220
  395.9 72.5 %copy-start.56 = (pred[768]{0:T(1024)(128)(4,1)S(1)}, pred[768]{0:T(1024)(128)(4,1)}, u32[]{:S(2)}) copy-start(pred[768]{0:T(1024)(128)(4,1)} %copy-done.55) | copy-start | bytes 2308
  (51 other events, 180.5 us)
Sparse Core Ops, SparseCore 0:
  67.5 50.6 all-gather.3
  120.4 69.1 all-gather.5
  196.1 63.3 all-gather.7
  285.5 67.8 reduce-scatter.2
  393.4 114.2 all-reduce.10
  509.8 101.7 reduce-scatter.4

commit v2 on v1

--- a/solution.py
+++ b/solution.py
@@ -45,17 +45,9 @@
     return high, jnp.concatenate([high, high, low], axis=1)
 
 
-def toeplitz_grad(grads, taps, span, scale):
-    heads = grads.shape[0]
-    shape = grads.shape
-    lane = lax.broadcasted_iota(jnp.int32, shape, 2)
-    tap = lax.broadcasted_iota(jnp.int32, shape, 1)
-    diff = lane % LANES + EDGE + span // 2 - tap
-    cols = []
-    for b in range(span):
-        part = jnp.sum(jnp.where(diff == b, grads, 0.0), axis=1)
-        cols.append(jnp.sum(part.reshape(heads, taps, LANES), axis=-1) * scale)
-    return jnp.stack(cols, axis=-1)
+def tap_grads(sums, taps, span, scale):
+    shaped = sums.reshape(sums.shape[0], 16, taps, LANES).sum(axis=-1)
+    return shaped[:, :span].transpose(0, 2, 1) * scale
 
 
 def lane_mask(dim):
@@ -97,10 +89,13 @@
 
     lax.fori_loop(0, 2 * step + 3, logits, 0)
     mx_ref[...] = jnp.full(mx_ref.shape, NEG, jnp.float32)
-    blocks = 2 * step + 2
 
     def convolve(c, carry):
-        at = pl.multiple_of(c * LANES, LANES)
+        for n in range(2):
+            convolve_block(pl.multiple_of((2 * c + n) * LANES, LANES))
+        return carry
+
+    def convolve_block(at):
         keep = (codes[HEADER:] == colc_ref[:, pl.ds(at, LANES)]) & (at + lane[HEADER:] <= ipos[HEADER:])
         for h in range(2):
             high = lm_ref[h, :, pl.ds(at, 2 * LANES)]
@@ -111,23 +106,25 @@
             conv = jnp.where(keep, conv, NEG)
             cv_ref[h, :, pl.ds(at, LANES)] = conv
             mx_ref[h] = jnp.maximum(mx_ref[h], conv)
-        return carry
-
-    lax.fori_loop(0, blocks, convolve, 0)
+
+    lax.fori_loop(0, step + 1, convolve, 0)
     sm_ref[...] = jnp.zeros(sm_ref.shape, jnp.float32)
     for h in range(2):
         peak = jnp.max(mx_ref[h], axis=-1, keepdims=True)
         mx_ref[h] = jnp.where(live, jnp.broadcast_to(peak, (ROWS, LANES)), 0.0)
 
     def exponents(c, carry):
-        at = pl.multiple_of(c * LANES, LANES)
         for h in range(2):
-            value = jnp.exp(cv_ref[h, :, pl.ds(at, LANES)] - mx_ref[h])
-            cv_ref[h, :, pl.ds(at, LANES)] = value
-            sm_ref[h] = sm_ref[h] + value
+            total = sm_ref[h]
+            for n in range(2):
+                at = pl.multiple_of((2 * c + n) * LANES, LANES)
+                value = jnp.exp(cv_ref[h, :, pl.ds(at, LANES)] - mx_ref[h])
+                cv_ref[h, :, pl.ds(at, LANES)] = value
+                total = total + value
+            sm_ref[h] = total
         return carry
 
-    lax.fori_loop(0, blocks, exponents, 0)
+    lax.fori_loop(0, step + 1, exponents, 0)
     for h in range(2):
         total = jnp.sum(sm_ref[h], axis=-1, keepdims=True)
         total = jnp.where(live, jnp.broadcast_to(total, (ROWS, LANES)), 1.0)
@@ -137,16 +134,21 @@
     mix = [[mix_ref[pair, 2 * g + h] for h in range(2)] for g in range(2)]
 
     def mixing(c, carry):
-        at = pl.multiple_of(c * LANES, LANES)
-        prob = [cv_ref[h, :, pl.ds(at, LANES)] * sm_ref[h] for h in range(2)]
+        at = pl.multiple_of(c * 2 * LANES, 2 * LANES)
+        mixed = [[], []]
+        for n in range(2):
+            spot = pl.ds(pl.multiple_of(at + n * LANES, LANES), LANES)
+            prob = [cv_ref[h, :, spot] * sm_ref[h] for h in range(2)]
+            for g in range(2):
+                prob_ref[g, :, spot] = prob[g].astype(prob_ref.dtype)
+                mixed[g].append((mix[g][0] * prob[0] + mix[g][1] * prob[1]).astype(jnp.bfloat16))
         for g in range(2):
             cols = slice(g * LANES, (g + 1) * LANES)
-            prob_ref[g, :, pl.ds(at, LANES)] = prob[g].astype(prob_ref.dtype)
-            mixed = (mix[g][0] * prob[0] + mix[g][1] * prob[1]).astype(jnp.bfloat16)
-            acc_ref[g] += dot(mixed, v_ref[pl.ds(at + EDGE, LANES), cols])
+            value = v_ref[pl.ds(pl.multiple_of(at + EDGE, 16), 2 * LANES), cols]
+            acc_ref[g] += dot(jnp.concatenate(mixed[g], axis=1), value)
         return carry
 
-    lax.fori_loop(0, blocks, mixing, 0)
+    lax.fori_loop(0, step + 1, mixing, 0)
     for g in range(2):
         att = acc_ref[g]
         att_ref[:, g * LANES : (g + 1) * LANES] = att
@@ -156,9 +158,9 @@
 
 
 def backward_kernel(
-    dim, taps, q_ref, k_ref, v_ref, t_ref, rowc_ref, colp_ref, colt_ref, rowt_ref, prob_ref, att_ref, dn_ref,
-    gain_ref, mix_ref, dq_ref, dk_ref, dv_ref, g_ref, dmix_ref, dgain_ref,
-    dp_ref, dc_ref, dl_ref, lt_ref, dkt_ref, dvt_ref, datt_ref, dattt_ref, qt_ref, rs_ref, dqa_ref, dm_ref, ahead_ref,
+    dim, taps, span, q_ref, k_ref, v_ref, t_ref, rowc_ref, colp_ref, colt_ref, rowt_ref, prob_ref, att_ref, dn_ref,
+    gain_ref, mix_ref, dq_ref, dk_ref, dv_ref, taps_ref, dmix_ref, dgain_ref,
+    dp_ref, dc_ref, dl_ref, lt_ref, dkt_ref, dvt_ref, datt_ref, dattt_ref, qt_ref, rs_ref, dqa_ref, dm_ref, ahead_ref, g_ref,
 ):
     pair = pl.program_id(0)
     turn = pl.program_id(1)
@@ -207,7 +209,11 @@
     dm_ref[...] = jnp.zeros(dm_ref.shape, jnp.float32)
 
     def probs(c, carry):
-        at = pl.multiple_of(c * LANES, LANES)
+        for n in range(2):
+            probs_block(pl.multiple_of((2 * c + n) * LANES, LANES))
+        return carry
+
+    def probs_block(at):
         prob = [prob_ref[h, :, pl.ds(at, LANES)].astype(jnp.float32) for h in range(2)]
         dmixed = []
         for g in range(2):
@@ -222,9 +228,8 @@
             dprob = mix[0][h] * dmixed[0] + mix[1][h] * dmixed[1]
             dp_ref[h, :, pl.ds(at, LANES)] = dprob
             rs_ref[h] += prob[h] * dprob
-        return carry
-
-    lax.fori_loop(0, blocks, probs, 0)
+
+    lax.fori_loop(0, step + 1, probs, 0)
     for h in range(2):
         rs_ref[h] = jnp.broadcast_to(jnp.sum(rs_ref[h], axis=-1, keepdims=True), (ROWS, LANES))
     for n in range(4):
@@ -247,7 +252,11 @@
     lax.fori_loop(0, blocks + 1, transposed_logits, 0)
 
     def convolve(c, carry):
-        at = pl.multiple_of(c * LANES, LANES)
+        for n in range(2):
+            convolve_block(pl.multiple_of((2 * c + n) * LANES, LANES))
+        return carry
+
+    def convolve_block(at):
         for h in range(2):
             prob = prob_ref[h, :, pl.ds(at, LANES)].astype(jnp.float32)
             dc_ref[h, :ROWS, pl.ds(at, LANES)] = prob * (dp_ref[h, :, pl.ds(at, LANES)] - rs_ref[h])
@@ -256,9 +265,8 @@
             )
             g_ref[h] += dot(lt_ref[h, pl.ds(at, 2 * LANES), :], shifted)
             dl_ref[h, :, pl.ds(at, 2 * LANES)] += dot(shifted, t_ref[h], NT)
-        return carry
-
-    lax.fori_loop(0, blocks, convolve, 0)
+
+    lax.fori_loop(0, step + 1, convolve, 0)
     dqa_ref[...] = jnp.zeros(dqa_ref.shape, jnp.float32)
 
     def logits(c, carry):
@@ -299,6 +307,17 @@
             dkt_ref[h, :, : 2 * LANES] += dot(query.astype(jnp.float32).T.astype(jnp.bfloat16), dl)
             dk_ref[:, cols] = dkt_ref[h].T.astype(jnp.bfloat16)
             dv_ref[pl.ds(EDGE, dvt_ref.shape[2]), cols] = dvt_ref[h].T.astype(jnp.bfloat16)
+        shape = (2 * LANES, taps * LANES)
+        lanes = lax.broadcasted_iota(jnp.int32, shape, 1) & (LANES - 1)
+        diff = lanes + (EDGE + span // 2) - lax.broadcasted_iota(jnp.int32, shape, 0)
+
+        def diagonals(b, carry):
+            for h in range(2):
+                part = jnp.where(diff == b, g_ref[h], 0.0)
+                taps_ref[h, pl.ds(b, 1), :] = jnp.sum(part, axis=0, keepdims=True)
+            return carry
+
+        lax.fori_loop(0, span, diagonals, 0)
 
 
 def attention_forward(proj, toep, codes, gain, mix, dim, taps):
@@ -339,13 +358,13 @@
             pltpu.VMEM((2, ROWS, LANES), jnp.float32),
             pltpu.VMEM((2, ROWS, LANES), jnp.float32),
         ],
-        cost_estimate=pl.CostEstimate(flops=60_000_000_000, bytes_accessed=40_000_000, transcendentals=0),
+        cost_estimate=pl.CostEstimate(flops=10_000_000_000, bytes_accessed=40_000_000, transcendentals=0),
         compiler_params=pltpu.CompilerParams(vmem_limit_bytes=48 << 20),
         name="attend",
     )(proj, proj, proj, toep, codes["row"], codes["colp"], codes["col"], gain, mix)
 
 
-def attention_backward(proj, toep, codes, prob, att, dnormed, gain, mix, dim, taps):
+def attention_backward(proj, toep, codes, prob, att, dnormed, gain, mix, dim, taps, span):
     tall = proj.shape[0]
     frame = tall - 2 * EDGE
     pairs = mix.shape[0]
@@ -354,7 +373,7 @@
     wide = pairs * 2 * LANES
     back = lambda r: steps - 1 - r
     return pl.pallas_call(
-        functools.partial(backward_kernel, dim, taps),
+        functools.partial(backward_kernel, dim, taps, span),
         grid=(pairs, steps),
         in_specs=[
             whole(0), whole(1), whole(2),
@@ -373,7 +392,7 @@
             pl.BlockSpec((tall, 2 * LANES), lambda p, r: (0, p)),
             pl.BlockSpec((tall, 2 * LANES), lambda p, r: (0, p)),
             pl.BlockSpec((tall, 2 * LANES), lambda p, r: (0, p)),
-            pl.BlockSpec((2, 2 * LANES, taps * LANES), lambda p, r: (p, 0, 0)),
+            pl.BlockSpec((2, 16, taps * LANES), lambda p, r: (p, 0, 0)),
             pl.BlockSpec((1, 8, LANES), lambda p, r: (p, 0, 0)),
             pl.BlockSpec((1, 2 * LANES), lambda p, r: (0, p)),
         ],
@@ -381,7 +400,7 @@
             jax.ShapeDtypeStruct((tall, wide), jnp.bfloat16),
             jax.ShapeDtypeStruct((tall, wide), jnp.bfloat16),
             jax.ShapeDtypeStruct((tall, wide), jnp.bfloat16),
-            jax.ShapeDtypeStruct((2 * pairs, 2 * LANES, taps * LANES), jnp.float32),
+            jax.ShapeDtypeStruct((2 * pairs, 16, taps * LANES), jnp.float32),
             jax.ShapeDtypeStruct((pairs, 8, LANES), jnp.float32),
             jax.ShapeDtypeStruct((1, wide), jnp.float32),
         ],
@@ -399,8 +418,9 @@
             pltpu.VMEM((2, ROWS, LANES), jnp.float32),
             pltpu.VMEM((4, ROWS, LANES), jnp.float32),
             pltpu.VMEM((2 * HEADER, LANES), jnp.float32),
+            pltpu.VMEM((2, 2 * LANES, taps * LANES), jnp.float32),
         ],
-        cost_estimate=pl.CostEstimate(flops=70_000_000_000, bytes_accessed=40_000_000, transcendentals=0),
+        cost_estimate=pl.CostEstimate(flops=10_000_000_000, bytes_accessed=40_000_000, transcendentals=0),
         compiler_params=pltpu.CompilerParams(vmem_limit_bytes=48 << 20),
         name="attend_back",
     )(proj, proj, proj, toep, codes["row"], codes["colp"], codes["colt"], codes["rowt"], prob, att, dnormed, gain, mix)
@@ -422,6 +442,7 @@
 
 
 MESH = pl.DeviceIdType.MESH
+TOKENS_AFTER = 2
 
 
 def meet(peers):
@@ -486,15 +507,6 @@
         )
         copy.start()
         waits.append(copy)
-    partner = (chip ^ 1) * 2 + core
-    for half in range(2):
-        mine = x_ref.at[pl.ds(half * (tokens // 2), tokens // 2), :]
-        copy = send(mine, token_rows(me, half), tok_send.at[0, half], tok_recv.at[0, half], at(rep, partner))
-        copy.start()
-        waits.append(copy)
-        copy = send(mine, token_rows(me, half), tok_send.at[1, half], tok_recv.at[1, half], at(rep, sibling))
-        copy.start()
-        waits.append(copy)
     local = [
         pltpu.make_async_copy(source(0, rows, me, t), target(spot(me, 0), rows, t), own_sem.at[t]) for t in range(3)
     ]
@@ -508,6 +520,17 @@
     ))
     for copy in local:
         copy.start()
+    def send_tokens():
+        partner = (chip ^ 1) * 2 + core
+        for half in range(2):
+            mine = x_ref.at[pl.ds(half * (tokens // 2), tokens // 2), :]
+            copy = send(mine, token_rows(me, half), tok_send.at[0, half], tok_recv.at[0, half], at(rep, partner))
+            copy.start()
+            waits.append(copy)
+            copy = send(mine, token_rows(me, half), tok_send.at[1, half], tok_recv.at[1, half], at(rep, sibling))
+            copy.start()
+            waits.append(copy)
+
     head = f_ref.at[pl.ds(lead, HEADER), :]
     fill = pltpu.make_async_copy(z_ref.at[pl.ds(0, HEADER), :], head, own_sem.at[6])
     sends_on = (place == 3) & (me < count - 4)
@@ -516,17 +539,20 @@
              at(rep, lax.rem(me + 1 + v, count)))
         for v in range(4)
     ]
-
-    @pl.when(sends_on)
-    def _():
-        for copy in after:
-            copy.start()
-
-    @pl.when(me < 4)
-    def _():
-        fill.start()
-
+    partner = (chip ^ 1) * 2 + core
     for n, who in enumerate(far_ids):
+        if n == min(TOKENS_AFTER, len(far_ids) - 1):
+            send_tokens()
+
+            @pl.when(sends_on)
+            def _():
+                for copy in after:
+                    copy.start()
+
+            @pl.when(me < 4)
+            def _():
+                fill.start()
+
         for t in range(3):
             got = target(spot(who, rep), part, t)
             send(got, got, far_send.at[n, t], far_recv.at[who, t], at(rep, who)).wait_recv()
@@ -589,7 +615,7 @@
             dma((7,)), dma((3,)), dma((3,)), dma((far, 3)), dma((count, 3)), dma((far, reps - 1)), dma((far, reps - 1)),
             dma((3, 2)), dma((3, 2)), dma((4,)), dma((1,)),
         ],
-        cost_estimate=pl.CostEstimate(flops=40_000_000_000, bytes_accessed=20_000_000, transcendentals=0),
+        cost_estimate=pl.CostEstimate(flops=2_000_000_000, bytes_accessed=20_000_000, transcendentals=0),
         compiler_params=pltpu.CompilerParams(collective_id=1, has_side_effects=True),
         name="gather_weight",
     )(weight, tokens, jnp.zeros((EDGE, tokens.shape[1]), tokens.dtype))
@@ -647,7 +673,7 @@
         out_specs=pl.BlockSpec(memory_space=pl.ANY),
         out_shape=jax.ShapeDtypeStruct((values.shape[0] * 4, values.shape[1]), values.dtype),
         scratch_shapes=[dma((1,)), dma((3, 2)), dma((3, 2))],
-        cost_estimate=pl.CostEstimate(flops=20_000_000_000, bytes_accessed=8_000_000, transcendentals=0),
+        cost_estimate=pl.CostEstimate(flops=2_000_000_000, bytes_accessed=8_000_000, transcendentals=0),
         compiler_params=pltpu.CompilerParams(collective_id=2, has_side_effects=True),
         name="frame_gather",
     )(values)
@@ -690,72 +716,17 @@
         out_specs=pl.BlockSpec(memory_space=pl.ANY),
         out_shape=jax.ShapeDtypeStruct((values.shape[0] // 4, values.shape[1] * 4), values.dtype),
         scratch_shapes=[dma((1,)), dma((3,)), dma((3,))],
-        cost_estimate=pl.CostEstimate(flops=10_000_000_000, bytes_accessed=2_000_000, transcendentals=0),
+        cost_estimate=pl.CostEstimate(flops=2_000_000_000, bytes_accessed=2_000_000, transcendentals=0),
         compiler_params=pltpu.CompilerParams(collective_id=3, has_side_effects=True),
         name="frame_swap",
     )(values)
 
 
-def small_sum_kernel(reps, count, v_ref, o_ref, one_ref, two_ref, sum_ref, send1, recv1, send2, recv2):
-    rep = lax.axis_index("rep")
-    me = lax.axis_index("seq")
-    rep_ids = [(rep + k) % reps for k in range(1, reps)]
-    seq_ids = [(me + k) % count for k in range(1, count)]
-    meet([(r, me) for r in rep_ids] + [(rep, s) for s in seq_ids])
-    waits = []
-    for m, r in enumerate(rep_ids):
-        copy = send(v_ref, one_ref.at[rep], send1.at[m], recv1.at[rep], (r, me))
-        copy.start()
-        waits.append(copy)
-    one_ref[rep] = v_ref[...]
-    for m, r in enumerate(rep_ids):
-        send(v_ref, one_ref.at[r], send1.at[m], recv1.at[r], (r, me)).wait_recv()
-    total = one_ref[0]
-    for r in range(1, reps):
-        total = total + one_ref[r]
-    sum_ref[...] = total
-    for m, s in enumerate(seq_ids):
-        copy = send(sum_ref, two_ref.at[me], send2.at[m], recv2.at[me], (rep, s))
-        copy.start()
-        waits.append(copy)
-    two_ref[me] = total
-    for m, s in enumerate(seq_ids):
-        send(sum_ref, two_ref.at[s], send2.at[m], recv2.at[s], (rep, s)).wait_recv()
-    total = two_ref[0]
-    for s in range(1, count):
-        total = total + two_ref[s]
-    o_ref[...] = total
-    for copy in waits:
-        copy.wait_send()
-
-
-def small_sum(values, reps, count):
-    size = values.shape[0]
-    rows = -(-size // (8 * LANES)) * 8
-    shaped = jnp.pad(values, (0, rows * LANES - size)).reshape(rows, LANES)
-    dma = pltpu.SemaphoreType.DMA
-    vmem = pl.BlockSpec(memory_space=pltpu.VMEM)
-    out = pl.pallas_call(
-        functools.partial(small_sum_kernel, reps, count),
-        in_specs=[vmem],
-        out_specs=vmem,
-        out_shape=jax.ShapeDtypeStruct(shaped.shape, jnp.float32),
-        scratch_shapes=[
-            pltpu.VMEM((reps, rows, LANES), jnp.float32), pltpu.VMEM((count, rows, LANES), jnp.float32),
-            pltpu.VMEM((rows, LANES), jnp.float32),
-            dma((reps - 1,)), dma((reps,)), dma((count - 1,)), dma((count,)),
-        ],
-        compiler_params=pltpu.CompilerParams(collective_id=4, has_side_effects=True),
-        name="small_sum",
-    )(shaped)
-    return out.reshape(-1)[:size]
-
-
 def reduce_kernel(
-    reps, count, gi_ref, go_ref, dn_ref, oi_ref, oo_ref, od_ref,
-    li_ref, ri_ref, zi_ref, qi_ref, lo_ref, ro_ref, zo_ref, qo_ref, ld_ref, bd_ref, hd_ref,
-    load_sem, one_send, one_recv, two_send, two_recv, three_send, three_recv, tok_send, tok_recv,
-    head_send, head_recv,
+    reps, count, gi_ref, go_ref, dn_ref, xs_ref, sv_ref, oi_ref, oo_ref, od_ref, so_ref,
+    li_ref, ri_ref, rb_ref, zi_ref, qi_ref, lo_ref, ro_ref, rc_ref, zo_ref, qo_ref, ld_ref, bd_ref, hd_ref,
+    load_sem, one_send, one_recv, on_send, on_recv, near_send, near_recv, past_send, past_recv, two_send, two_recv, three_send, three_recv, tok_send, tok_recv,
+    head_send, head_recv, vec_ref, one_ref, two_ref, sum_ref, small_one, small_got, small_two, small_end,
 ):
     rep = lax.axis_index("rep")
     me = lax.axis_index("seq")
@@ -765,9 +736,10 @@
     partner = (chip ^ 1) * 2 + core
     rep_ids = [(rep + k) % reps for k in range(1, reps)]
     seq_ids = [(me + k) % count for k in range(1, count)]
-    part = li_ref.shape[1]
+    part = li_ref.shape[2]
     rows = part * reps
     halves = lo_ref.shape[0]
+    frames = count // 4
     cols = gi_ref.shape[1] // 3
     width = cols * 4
     tokens = od_ref.shape[0]
@@ -806,15 +778,17 @@
     for copy in loads:
         copy.start()
     order = seq_ids + [me]
-    for h in range(halves):
-        for m, r in enumerate(rep_ids):
-            push(quarter(go_ref, h, r), ro_ref.at[m, h], one_send.at[count + h, m], one_recv.at[count + h, m], (r, me))
-    for n, who in enumerate(order):
-        for m, r in enumerate(rep_ids):
-            push(quarter(gi_ref, who, r), ri_ref.at[m, n], one_send.at[n, m], one_recv.at[n, m], (r, me))
-    own = [pltpu.make_async_copy(quarter(gi_ref, who, rep), li_ref.at[n], load_sem.at[2 + n]) for n, who in enumerate(order)]
-    own += [
-        pltpu.make_async_copy(quarter(go_ref, h, rep), lo_ref.at[h], load_sem.at[2 + count + h]) for h in range(halves)
+    near = [rep ^ 1, rep ^ 2]
+    past = [rep ^ 2, rep ^ 1]
+    blocks = [(go_ref, h, lo_ref.at[h], ro_ref.at[h], rc_ref.at[h]) for h in range(halves)]
+    blocks += [(gi_ref, who, li_ref.at[n], ri_ref.at[n], rb_ref.at[n]) for n, who in enumerate(order)]
+    for n, (grad, row, _, got, _) in enumerate(blocks):
+        for m, r in enumerate((near[n % 2], rep ^ 3)):
+            push(quarter(grad, row, r), got.at[m], one_send.at[n, m], one_recv.at[n, m], (near[n % 2], me))
+    own = [
+        pltpu.make_async_copy(quarter(grad, row, r), held.at[m], load_sem.at[2 + 2 * n + m])
+        for n, (grad, row, held, _, _) in enumerate(blocks)
+        for m, r in enumerate((rep, past[n % 2]))
     ]
     for copy in own:
         copy.start()
@@ -825,34 +799,46 @@
     ld_ref[0] = (ld_ref[0].astype(wide) + bd_ref[0].astype(wide)).astype(jnp.bfloat16)
     push(ld_ref.at[0], bd_ref.at[2], tok_send.at[2], tok_recv.at[2], (rep, partner))
 
-    def over_reps(local_ref, rest_ref, n, sems):
-        total = local_ref[n].astype(wide)
-        for m in range(reps - 1):
-            arrived(rest_ref.at[m, n], one_send.at[sems, m], one_recv.at[sems, m])
-            total = total + rest_ref[m, n].astype(wide)
-        local_ref[n] = total.astype(jnp.bfloat16)
-
-    frames = count // 4
-    for h in range(halves):
-        own[count + h].wait()
-        over_reps(lo_ref, ro_ref, h, count + h)
-        owner = place * halves + h
-
-        @pl.when(owner == me)
-        def _():
-            zo_ref[me // 4] = lo_ref[h]
-
-        @pl.when(owner != me)
-        def _():
-            send(lo_ref.at[h], zo_ref.at[me // 4], two_send.at[count + h], two_recv.at[count + me // 4], (rep, owner)).start()
-
-    for n, who in enumerate(order):
-        own[n].wait()
-        over_reps(li_ref, ri_ref, n, n)
-        if n < count - 1:
-            push(li_ref.at[n], zi_ref.at[me], two_send.at[n], two_recv.at[me], (rep, who))
+    def pass_on(n):
+        _, _, held, got, last = blocks[n]
+        own[2 * n + 1].wait()
+        arrived(got.at[1], one_send.at[n, 1], one_recv.at[n, 1])
+        held[1] = (held[1].astype(wide) + got[1].astype(wide)).astype(jnp.bfloat16)
+        push(held.at[1], last, on_send.at[n], on_recv.at[n], (past[n % 2], me))
+
+    def finish(n):
+        _, _, held, got, last = blocks[n]
+        own[2 * n].wait()
+        arrived(got.at[0], one_send.at[n, 0], one_recv.at[n, 0])
+        arrived(last, on_send.at[n], on_recv.at[n])
+        held[0] = (held[0].astype(wide) + got[0].astype(wide) + last[...].astype(wide)).astype(jnp.bfloat16)
+        if n < halves:
+            owner = place * halves + n
+
+            @pl.when(owner == me)
+            def _():
+                zo_ref[me // 4] = lo_ref[n, 0]
+
+            @pl.when(owner != me)
+            def _():
+                shipped(n).start()
+        elif n < halves + count - 1:
+            k = n - halves
+            push(li_ref.at[k, 0], zi_ref.at[me], two_send.at[k], two_recv.at[me], (rep, order[k]))
         else:
-            zi_ref[me] = li_ref[n]
+            zi_ref[me] = li_ref[count - 1, 0]
+
+    def shipped(h):
+        return send(
+            lo_ref.at[h, 0], zo_ref.at[me // 4], two_send.at[count + h], two_recv.at[count + me // 4],
+            (rep, place * halves + h),
+        )
+
+    for n in range(len(blocks) + 2):
+        if n < len(blocks):
+            pass_on(n)
+        if n >= 2:
+            finish(n - 2)
 
     loads[1].wait()
     arrived(bd_ref.at[1], tok_send.at[1], tok_recv.at[1])
@@ -871,6 +857,15 @@
     def _():
         ahead.wait_send()
 
+    gain_rows = width // LANES
+    first = jnp.sum(od_ref[...] * xs_ref[...], axis=0, keepdims=True)
+    vec_ref[...] = sv_ref[...]
+    for k in range(gain_rows):
+        vec_ref[k : k + 1, :] = first[:, k * LANES : (k + 1) * LANES]
+    for m, r in enumerate(rep_ids):
+        push(vec_ref, one_ref.at[rep], small_one.at[m], small_got.at[rep], (r, me))
+    one_ref[rep] = vec_ref[...]
+
     for f in range(frames):
         source = f * 4 + me // halves
 
@@ -884,6 +879,15 @@
     qo_ref[...] = total.astype(jnp.bfloat16)
     for m, r in enumerate(rep_ids):
         push(qo_ref, oo_ref.at[pl.ds(pl.multiple_of(rep * part, 16), part), :], three_send.at[0, m], three_recv.at[0, m], (r, me))
+    for m, r in enumerate(rep_ids):
+        arrived(one_ref.at[r], small_one.at[m], small_got.at[r])
+    total = one_ref[0]
+    for r in range(1, reps):
+        total = total + one_ref[r]
+    sum_ref[...] = total
+    two_ref[me] = total
+    for m, s in enumerate(seq_ids):
+        push(sum_ref, two_ref.at[me], small_two.at[m], small_end.at[me], (rep, s))
     for n, who in enumerate(seq_ids):
         arrived(zi_ref.at[who], two_send.at[n], two_recv.at[who])
     for u in range(4):
@@ -894,8 +898,19 @@
             qi_ref[:, t * width + u * cols : t * width + (u + 1) * cols] = total[:, t * cols : (t + 1) * cols].astype(
                 jnp.bfloat16
             )
-    for m, r in enumerate(rep_ids):
-        push(qi_ref, oi_ref.at[pl.ds(pl.multiple_of(rep * part, 16), part), :], three_send.at[1, m], three_recv.at[1, m], (r, me))
+    wing = 3 * width // 2
+
+    def shard(r, k):
+        return oi_ref.at[pl.ds(pl.multiple_of(r * part, 16), part), pl.ds(k * wing, wing)]
+
+    for k in range(2):
+        mine = qi_ref.at[:, pl.ds(k * wing, wing)]
+        push(mine, shard(rep, k), near_send.at[k], near_recv.at[k], (near[k], me))
+        push(mine, shard(rep, k), past_send.at[k, 0], past_recv.at[k, 0], (past[k], me))
+    for k in range(2):
+        got = shard(near[k], k)
+        arrived(got, near_send.at[k], near_recv.at[k])
+        push(got, got, past_send.at[k, 1], past_recv.at[k, 1], (past[k], me))
     final = [
         pltpu.make_async_copy(qo_ref, oo_ref.at[pl.ds(pl.multiple_of(rep * part, 16), part), :], load_sem.at[0]),
         pltpu.make_async_copy(qi_ref, oi_ref.at[pl.ds(pl.multiple_of(rep * part, 16), part), :], load_sem.at[1]),
@@ -907,19 +922,27 @@
 
         @pl.when(owner != me)
         def _():
-            send(lo_ref.at[h], zo_ref.at[me // 4], two_send.at[count + h], two_recv.at[count + me // 4], (rep, owner)).wait_send()
-
+            shipped(h).wait_send()
+
+    for m, s in enumerate(seq_ids):
+        arrived(two_ref.at[s], small_two.at[m], small_end.at[s])
+    total = two_ref[0]
+    for s in range(1, count):
+        total = total + two_ref[s]
+    so_ref[...] = total
     for copy in final:
         copy.wait()
     for m in range(reps - 1):
         r = (rep + reps - 1 - m) % reps
-        for n, ref in ((0, oo_ref), (1, oi_ref)):
-            arrived(ref.at[pl.ds(pl.multiple_of(r * part, 16), part), :], three_send.at[n, m], three_recv.at[n, m])
+        arrived(oo_ref.at[pl.ds(pl.multiple_of(r * part, 16), part), :], three_send.at[0, m], three_recv.at[0, m])
+    for k in range(2):
+        arrived(shard(past[k], k), past_send.at[k, 0], past_recv.at[k, 0])
+        arrived(shard(rep ^ 3, k), past_send.at[k, 1], past_recv.at[k, 1])
     for copy in waits:
         copy.wait_send()
 
 
-def reduce_weights(grad_in, grad_out, tokens, reps, count):
+def reduce_weights(grad_in, grad_out, tokens, scaled, small, reps, count):
     width = grad_out.shape[1]
     own = grad_in.shape[1]
     rows = width // count
@@ -930,30 +953,39 @@
     dma = pltpu.SemaphoreType.DMA
     low = jnp.bfloat16
     hbm = pl.BlockSpec(memory_space=pl.ANY)
+    vmem = pl.BlockSpec(memory_space=pltpu.VMEM)
+    lines = small.shape[0]
     return pl.pallas_call(
         functools.partial(reduce_kernel, reps, count),
-        in_specs=[hbm] * 3,
-        out_specs=[hbm, hbm, pl.BlockSpec(memory_space=pltpu.VMEM)],
+        in_specs=[hbm] * 3 + [vmem] * 2,
+        out_specs=[hbm, hbm, vmem, vmem],
         out_shape=[
             jax.ShapeDtypeStruct((rows, 3 * width), low),
             jax.ShapeDtypeStruct((rows, width), low),
             jax.ShapeDtypeStruct((each, width), jnp.float32),
+            jax.ShapeDtypeStruct((lines, LANES), jnp.float32),
         ],
         scratch_shapes=[
-            pltpu.VMEM((count, part, own), low), pltpu.VMEM((reps - 1, count, part, own), low),
-            pltpu.VMEM((count, part, own), low), pltpu.VMEM((part, 3 * width), low),
-            pltpu.VMEM((halves, part, width), low), pltpu.VMEM((reps - 1, halves, part, width), low),
+            pltpu.VMEM((count, 2, part, own), low), pltpu.VMEM((count, 2, part, own), low),
+            pltpu.VMEM((count, part, own), low), pltpu.VMEM((count, part, own), low), pltpu.VMEM((part, 3 * width), low),
+            pltpu.VMEM((halves, 2, part, width), low), pltpu.VMEM((halves, 2, part, width), low),
+            pltpu.VMEM((halves, part, width), low),
             pltpu.VMEM((frames, part, width), low), pltpu.VMEM((part, width), low),
             pltpu.VMEM((2, each, width), low), pltpu.VMEM((3, each, width), low),
             pltpu.VMEM((4, HEADER, width), low),
-            dma((2 + count + halves,)), dma((count + halves, reps - 1)), dma((count + halves, reps - 1)),
-            dma((count + halves,)), dma((count + frames,)), dma((2, reps - 1)), dma((2, reps - 1)), dma((3,)), dma((3,)),
+            dma((2 + 2 * (count + halves),)), dma((count + halves, 2)), dma((count + halves, 2)), dma((count + halves,)),
+            dma((count + halves,)),
+            dma((2,)), dma((2,)), dma((2, 2)), dma((2, 2)),
+            dma((count + halves,)), dma((count + frames,)), dma((1, reps - 1)), dma((1, reps - 1)), dma((3,)), dma((3,)),
             dma((1,)), dma((4,)),
+            pltpu.VMEM((lines, LANES), jnp.float32), pltpu.VMEM((reps, lines, LANES), jnp.float32),
+            pltpu.VMEM((count, lines, LANES), jnp.float32), pltpu.VMEM((lines, LANES), jnp.float32),
+            dma((reps - 1,)), dma((reps,)), dma((count - 1,)), dma((count,)),
         ],
-        cost_estimate=pl.CostEstimate(flops=70_000_000_000, bytes_accessed=20_000_000, transcendentals=0),
+        cost_estimate=pl.CostEstimate(flops=2_000_000_000, bytes_accessed=20_000_000, transcendentals=0),
         compiler_params=pltpu.CompilerParams(collective_id=5, has_side_effects=True, vmem_limit_bytes=40 << 20),
         name="reduce_weights",
-    )(grad_in, grad_out, tokens)
+    )(grad_in, grad_out, tokens, scaled, small)
 
 
 def rms_scale(values):
@@ -1011,7 +1043,7 @@
     toep, toep_split = split_toeplitz(toeplitz(own_kernel, scale))
 
     reps = lax.axis_size("rep")
-    direct = team == 4 and (width // count) % (16 * reps) == 0
+    direct = team == 4 and reps == 4 and (width // count) % (16 * reps) == 0
     first_scale = rms_scale(resid_in)
     normed_in = (resid_in * first_scale * first_gain).astype(jnp.bfloat16)
     if direct:
@@ -1081,16 +1113,34 @@
     own_output = lax.dynamic_slice_in_dim(full_output, place * own_width, own_width, axis=0)
     dnormed_own = lax.dot_general(dbranch_frame, own_output, NT, preferred_element_type=jnp.float32)
     own_output_grad = lax.dot_general(normed_own, dbranch_frame, contract_rows, preferred_element_type=jnp.float32)
+    own_output_grad = own_output_grad.astype(jnp.bfloat16)
     dq, dk, dv, dtoep, dmix, dgain = attention_backward(
-        proj, toep, codes, prob, att, pad_heads(dnormed_own, dim), own_gain, own_mix, dim, taps
+        proj, toep, codes, prob, att, pad_heads(dnormed_own, dim), own_gain, own_mix, dim, taps, span
     )
     dproj = jnp.concatenate([dq, dk, dv], axis=1)
     own_input_grad = lax.dot_general(normed_frame, dproj, contract_rows, preferred_element_type=jnp.float32)
     own_input_grad = cut_heads(own_input_grad.astype(jnp.bfloat16), dim)
-    own_output_grad = own_output_grad.astype(jnp.bfloat16)
     dnormin_part = lax.dot_general(dproj, own_input, NT, preferred_element_type=jnp.float32).astype(jnp.bfloat16)
+    def spread(values, size):
+        empty = jnp.zeros((size,) + values.shape[1:], jnp.float32)
+        return lax.dynamic_update_slice_in_dim(empty, values, place * values.shape[0], 0)
+
+    kernel_part = spread(tap_grads(dtoep, taps, span, scale), heads)
+    mix_part = spread(jnp.sum(dmix[:, :4], axis=-1).reshape(own_pairs, 2, 2), heads // 2)
+    group_part = spread(cut_heads(dgain, dim)[0], width)
+    parts = (kernel_part, mix_part, second_part, group_part)
     if direct:
-        grad_input_w, grad_output_w, dnormin = reduce_weights(own_input_grad, own_output_grad, dnormin_part, reps, count)
+        flat = jnp.concatenate([jnp.zeros((width,), jnp.float32)] + [value.reshape(-1) for value in parts])
+        size = -(-flat.shape[0] // (8 * LANES)) * 8 * LANES
+        small = jnp.pad(flat, (0, size - flat.shape[0])).reshape(-1, LANES)
+        grad_input_w, grad_output_w, dnormin, small = reduce_weights(
+            own_input_grad, own_output_grad, dnormin_part, resid_in * first_scale, small, reps, count
+        )
+        flat = small.reshape(-1)
+        grad_first, others, start = flat[:width], [], width
+        for value in parts:
+            others.append(flat[start : start + value.size].reshape(value.shape))
+            start += value.size
     else:
         dnormin = lax.psum_scatter(
             dnormin_part[EDGE : EDGE + FRAME], "seq", scatter_dimension=0, tiled=True, axis_index_groups=groups
@@ -1112,26 +1162,12 @@
         ]
     dnormin, mlp_low, mlp_grads = lax.optimization_barrier((dnormin, mlp_low, mlp_grads))
     result = resid + row_valid * mlp_low.astype(jnp.float32)
-    first_part = jnp.sum(dnormin * resid_in * first_scale, axis=0)
+    if not direct:
+        first_part = jnp.sum(dnormin * resid_in * first_scale, axis=0)
+        grad_first, others = lax.psum((first_part, parts), ("rep", "seq"))
     grad_in = dresid + norm_back(dnormin, resid_in, first_scale, first_gain)
 
-    def spread(values, size):
-        empty = jnp.zeros((size,) + values.shape[1:], jnp.float32)
-        return lax.dynamic_update_slice_in_dim(empty, values, place * values.shape[0], 0)
-
-    kernel_part = spread(toeplitz_grad(dtoep, taps, span, scale), heads)
-    mix_part = spread(jnp.sum(dmix[:, :4], axis=-1).reshape(own_pairs, 2, 2), heads // 2)
-    group_part = spread(cut_heads(dgain, dim)[0], width)
-    parts = (kernel_part, mix_part, first_part, second_part, group_part)
-    if direct:
-        flat = small_sum(jnp.concatenate([value.reshape(-1) for value in parts]), reps, count)
-        summed, start = [], 0
-        for value in parts:
-            summed.append(flat[start : start + value.size].reshape(value.shape))
-            start += value.size
-    else:
-        summed = lax.psum(parts, ("rep", "seq"))
-    grad_kernel, grad_mix, grad_first, grad_second, grad_group = summed
+    grad_kernel, grad_mix, grad_second, grad_group = others
     grads = [value.astype(jnp.float32) for value in (grad_input_w, grad_output_w, *mlp_grads)]
     return (
         result.astype(jnp.bfloat16)[None], grad_in.astype(jnp.bfloat16)[None], grads[0], grads[1], grad_kernel,

time: 682 us -> 639 us (0.937)
  Pallas kernels: 351 us -> 326 us
  other arithmetic: 56.1 us -> 36 us
    pallas_call x2 -> x1, Pallas kernels: 84.4 us -> 68.3 us  [attention_backward(): pl.pallas_call(functools.partial(backward_kernel, dim, taps, span), grid=...]
    reduce_sum x13 -> x2, other arithmetic: 12.8 us -> 2 us  [the longest x1 1.71 us: tap_grads(): shaped = sums.reshape(sums.shape[0], 16, taps, LANES).sum(axis=-1)]
    unnamed x11 -> x1, other arithmetic: 9.77 us -> 0.01 us
    pallas_call x1, Pallas kernels: 97.7 us -> 89.1 us  [reduce_weights(): pl.pallas_call(functools.partial(reduce_kernel, reps, count), in_specs=[h...]
    unnamed x155 -> x137, local copies, waits for them, and re-layouts: 16.4 us -> 15.9 us
  transfers between devices with their start and end apart: 6 -> 6, of which waited for: 2 -> 2; matrix products, arithmetic and copies ran while one was open for 20% -> 21% of each run, Pallas kernels for 39% -> 44%
where the time goes in v2:
time: 639 us; the launch traced here: 627 us
  Pallas kernels  326 us (51%)
  matrix products  97 us (15%)
  waiting for transfers between devices  94.7 us (15%)
  local copies, waits for them, and re-layouts  58 us (9%)
  other arithmetic  36 us (6%)
  between operations  15.3 us (2%)
    pallas_call x1, Pallas kernels, reduce_weights(): pl.pallas_call(functools.partial(reduce_kernel, reps, count), in_specs=[h...  89.1 us
    pallas_call x1, Pallas kernels, attention_backward(): pl.pallas_call(functools.partial(backward_kernel, dim, taps, span), grid=...  68.3 us
    pallas_call x1, Pallas kernels, attention_forward(): pl.pallas_call(functools.partial(forward_kernel, dim, taps), grid=(pairs,...  62.5 us
    all_gather x1, waiting for transfers between devices, on_device(): inputs_all = lax.all_gather(normed_mid, 'seq', axis=0, tiled=True)  54.3 us
    pallas_call x1, Pallas kernels, gather_weight(): pl.pallas_call(functools.partial(gather_kernel, reps, count), in_specs=[p...  52.1 us
    reduce_scatter x1, waiting for transfers between devices, on_device(): lax.psum_scatter(dmid_part, 'seq', scatter_dimension=0, tiled=True)  39.1 us
    pallas_call x1, Pallas kernels, frame_swap(): pl.pallas_call(frame_swap_kernel, in_specs=[pl.BlockSpec(memory_space=pl....  27 us
    pallas_call x1, Pallas kernels, frame_gather(): pl.pallas_call(frame_gather_kernel, in_specs=[pl.BlockSpec(memory_space=p...  26.5 us
  transfers between devices with their start and end apart: 6, of which 2 were waited for; matrix products, arithmetic and copies ran while one was open for 21% of the time, Pallas kernels for 44%

profile of v2, /device:TPU:25, one launch (start us, length us, event | category | flops | bytes accessed | tf_op | source)
XLA Modules:
  0.0 627.4 jit_solution(6489114550434901800)
XLA Ops:
  15.7 52.1 %gather_weight.1 = (bf16[1536,1152]{1,0:T(8,128)(2,1)}, bf16[1152,1536]{1,0:T(8,128)(2,1)}) custom-call(bf16[192,4608]{1,0:T(8,128)(2,1)} %w_ref.1, bf16[256,1536]{1,0:T(8,128)(2,1)} %get-tuple-element.121.x_ref, bf16[64,1536]{1,0:T(8,128)(2,1)} %broadcast_in_dim.179.z_ref), custom_call_target="tpu_custom_call" | custom-call | flops 2000000000 | bytes 20000000 | tf_op jit(solution)/shard_map/gather_weight/pallas_call | solution.py:606
  71.3 5.8 copy.60
  88.0 7.1 %convolution_convert_fusion.3.q_ref.k_ref.v_ref = bf16[1152,1536]{1,0:T(8,128)(2,1)} fusion(bf16[1152,1536]{1,0:T(8,128)(2,1)S(1)} %copy-done.54, bf16[1536,1536]{0,1:T(8,128)(2,1)S(1)} %bitcast.143), kind=kOutput, calls=%fused_computation.4 | convolution fusion | flops 5437587456 | bytes 11796480 | tf_op jit(solution)/shard_map/dot_general | solution.py:1065
  95.3 62.5 %attend.1 = (bf16[1024,512]{1,0:T(8,128)(2,1)S(1)}, f32[1024,512]{1,0:T(8,128)S(1)}, f32[4,1024,1024]{2,1,0:T(8,128)}) custom-call(bf16[1152,1536]{1,0:T(8,128)(2,1)} %convolution_convert_fusion.3.q_ref.k_ref.v_ref, bf16[1152,1536]{1,0:T(8,128)(2,1)} %convolution_convert_fusion.3.q_ref.k_ref.v_ref, ...), custom_call_target="tpu_custom_call" | custom-call | flops 10000000000 | bytes 40000000 | tf_op jit(solution)/shard_map/attend/pallas_call | solution.py:330
  163.7 27.0 %frame_swap.1 = bf16[256,1536]{1,0:T(8,128)(2,1)} custom-call(bf16[1024,384]{1,0:T(8,128)(2,1)} %copy.74.h_ref), custom_call_target="tpu_custom_call" | custom-call | flops 2000000000 | bytes 2000000 | tf_op jit(solution)/shard_map/frame_swap/pallas_call | solution.py:713
  190.7 4.3 multiply_reduce_fusion
  196.9 8.7 %fusion.41 = f32[2048,512]{1,0:T(8,128)} fusion(bf16[2048,1536]{1,0:T(8,128)(2,1)} %all-gather.6.cloned.1.call-done, bf16[512,1536]{1,0:T(8,128)(2,1)} %param.26), kind=kOutput, calls=%fused_computation.127 | convolution fusion | flops 3221225472 | bytes 12058624 | tf_op jit(solution)/shard_map/dot_general | solution.py:1086
  205.6 54.3 %all-gather.8.cloned.1.call-done = bf16[2048,1536]{1,0:T(8,128)(2,1)} async-done(((bf16[256,1536]{1,0:T(8,128)(2,1)}), bf16[2048,1536]{1,0:T(8,128)(2,1)}) %all-gather.8.cloned.1.call-update) | async-done | bytes 6291472 | tf_op jit(solution)/shard_map/all_gather | solution.py:1083
  259.9 6.1 fusion.42
  266.2 6.8 %multiply_convert_fusion = (bf16[2048,512]{1,0:T(8,128)(2,1)}, bf16[2048,512]{1,0:T(8,128)(2,1)}, bf16[2048,512]{1,0:T(8,128)(2,1)}) fusion(f32[2048,512]{1,0:T(8,128)S(1)} %fusion.42, f32[2048,512]{1,0:T(8,128)S(1)} %copy-done.57, bf16[2048,1536]{1,0:T(8,128)(2,1)S(1)} %copy-done.50, bf16[1536,512]{1,0:T(8,128)(2,1)S(1)} %copy-done), kind=kOutput, calls=%fused_computation.8 | convolution fusion | flops 3238002688 | bytes 22544384 | tf_op jit(solution)/shard_map/dot_general | solution.py:1085
  273.1 5.2 fusion.43
  278.3 7.4 %add_convert_fusion = bf16[2048,1536]{1,0:T(8,128)(2,1)} fusion(f32[2048,1536]{1,0:T(8,128)S(1)} %fusion.43, bf16[2048,512]{1,0:T(8,128)(2,1)} %get-tuple-element.63, bf16[1536,512]{1,0:T(8,128)(2,1)S(1)} %copy-done), kind=kOutput, calls=%fused_computation | convolution fusion | flops 3227516928 | bytes 22544384 | tf_op jit(solution)/shard_map/dot_general | solution.py:1093
  287.1 7.0 %convolution_convert_fusion.2 = bf16[2048,1536]{1,0:T(8,128)(2,1)} fusion(bf16[2048,512]{1,0:T(8,128)(2,1)} %get-tuple-element.61, bf16[512,1536]{1,0:T(8,128)(2,1)S(1)} %copy-done.52), kind=kOutput, calls=%fused_computation.3 | convolution fusion | flops 3224371200 | bytes 9961472 | tf_op jit(solution)/shard_map/dot_general | solution.py:1097
  294.1 8.2 %convolution_convert_fusion.4 = bf16[512,1536]{1,0:T(8,128)(2,1)} fusion(bf16[2048,512]{1,0:T(8,128)(2,1)} %get-tuple-element.61, bf16[2048,1536]{1,0:T(8,128)(2,1)} %all-gather.6.cloned.1.call-done), kind=kOutput, calls=%fused_computation.31 | convolution fusion | flops 3222011904 | bytes 9961472 | tf_op jit(solution)/shard_map/dot_general | solution.py:1099
  302.3 7.6 %convolution_convert_fusion.5 = bf16[1536,512]{1,0:T(8,128)(2,1)} fusion(bf16[2048,1536]{1,0:T(8,128)(2,1)} %all-gather.8.cloned.1.call-done, bf16[2048,512]{1,0:T(8,128)(2,1)S(1)} %copy-done.56), kind=kOutput, calls=%fused_computation.32 | convolution fusion | flops 3222011904 | bytes 9961472 | tf_op jit(solution)/shard_map/dot_general | solution.py:1099
  310.0 4.6 convolution_convert_fusion.6
  314.5 39.1 %reduce-scatter.3.cloned.1.call-done = bf16[256,1536]{1,0:T(8,128)(2,1)} async-done(((bf16[2048,1536]{1,0:T(8,128)(2,1)}), bf16[256,1536]{1,0:T(8,128)(2,1)}) %reduce-scatter.3.cloned.1.call-update) | async-done | bytes 786448 | tf_op jit(solution)/shard_map/reduce_scatter | solution.py:1096
  357.5 26.5 %frame_gather.1 = bf16[1024,1536]{1,0:T(8,128)(2,1)} custom-call(bf16[256,1536]{1,0:T(8,128)(2,1)} %multiply_convert_fusion.3.x_ref), custom_call_target="tpu_custom_call" | custom-call | flops 2000000000 | bytes 8000000 | tf_op jit(solution)/shard_map/frame_gather/pallas_call | solution.py:670
  384.0 4.8 fusion.25
  393.1 68.3 %attend_back.1 = (bf16[1152,512]{1,0:T(8,128)(2,1)S(1)}, bf16[1152,512]{1,0:T(8,128)(2,1)S(1)}, bf16[1152,512]{1,0:T(8,128)(2,1)S(1)}, f32[4,16,768]{2,1,0:T(8,1...) custom-call(bf16[1152,1536]{1,0:T(8,128)(2,1)} %convolution_convert_fusion.3.q_ref.k_ref.v_ref, ...), custom_call_target="tpu_custom_call" | custom-call | flops 10000000000 | bytes 40000000 | tf_op jit(solution)/shard_map/attend_back/pallas_call | solution.py:375
  477.2 6.8 %convolution_convert_fusion.1 = bf16[1536,1536]{0,1:T(8,128)(2,1)S(1)} fusion(bf16[1152,1536]{1,0:T(8,128)(2,1)S(1)} %copy-done.55, bf16[1152,1536]{1,0:T(8,128)(2,1)S(1)} %constant_dynamic-update-slice_fusion), kind=kOutput, calls=%fused_computation.2 | convolution fusion | flops 5438177280 | bytes 11796480 | tf_op jit(solution)/shard_map/dot_general | solution.py:1121
  486.0 4.4 copy.77.gi_ref
  498.9 8.6 %convolution_convert_fusion.dn_ref = bf16[1152,1536]{1,0:T(8,128)(2,1)S(1)} fusion(bf16[1152,1536]{1,0:T(8,128)(2,1)S(1)} %copy-done.30, bf16[1536,1536]{0,1:T(8,128)(2,1)} %bitcast.144), kind=kOutput, calls=%fused_computation.1 | convolution fusion | flops 5437587456 | bytes 11796480 | tf_op jit(solution)/shard_map/dot_general | solution.py:1123
  507.5 89.1 %reduce_weights.1 = (bf16[192,4608]{1,0:T(8,128)(2,1)S(1)}, bf16[192,1536]{1,0:T(8,128)(2,1)S(1)}, f32[256,1536]{1,0:T(8,128)S(1)}, f32[48,128]{1,0:T(8,128)S(1)}) custom-call(bf16[1536,1152]{1,0:T(8,128)(2,1)S(1)} %copy.77.gi_ref, bf16[384,1536]{1,0:T(8,128)(2,1)S(1)} %convolution_convert_fusion.7.go_ref, ...), custom_call_target="tpu_custom_call" | custom-call | flops 2000000000 | bytes 20000000 | tf_op jit(solution)/shard_map/reduce_weights/pallas_call | solution.py:958
  (241 shorter events, 89.7 us)
Async XLA Ops:
  7.2 258.8 %copy-start = (bf16[1536,512]{1,0:T(8,128)(2,1)S(1)}, bf16[1536,512]{1,0:T(8,128)(2,1)}, u32[]{:S(2)}) copy-start(bf16[1536,512]{1,0:T(8,128)(2,1)} %param.25) | copy-start | bytes 4718596
  7.2 152.8 %all-gather.4.cloned.1.call-start = ((), (), s32[]{:S(2)}) async-start(), calls=%async_computation.2 | async-start | bytes 5308416 | tf_op jit(solution)/shard_map/all_gather | solution.py:1063
  10.0 346.0 %copy-start.39 = (f32[1,256]{1,0:T(1,128)}, f32[1,256]{1,0:T(1,128)S(1)}, u32[]{:S(2)}) copy-start(f32[1,256]{1,0:T(1,128)S(1)} %fusion.38) | copy-start | bytes 3076
  15.7 53.0 %copy-start.34 = (f32[16,6,11]{0,1,2:T(8,128)S(1)}, f32[16,6,11]{0,1,2:T(8,128)}, u32[]{:S(2)}) copy-start(f32[16,6,11]{0,1,2:T(8,128)} %param.19) | copy-start | bytes 12676
  15.7 54.2 %copy-start.36 = (s32[1,2048]{1,0:T(1,128)S(1)}, s32[1,2048]{1,0:T(1,128)}, u32[]{:S(2)}) copy-start(s32[1,2048]{1,0:T(1,128)} %param.15) | copy-start | bytes 24580
  15.7 54.2 %copy-start.41 = (s32[1,2048]{1,0:T(1,128)S(1)}, s32[1,2048]{1,0:T(1,128)}, u32[]{:S(2)}) copy-start(s32[1,2048]{1,0:T(1,128)} %param.16) | copy-start | bytes 24580
  15.7 55.3 %copy-start.49 = (f32[8,2,2]{0,2,1:T(2,128)S(1)}, f32[8,2,2]{0,2,1:T(2,128)}, u32[]{:S(2)}) copy-start(f32[8,2,2]{0,2,1:T(2,128)} %param.20) | copy-start | bytes 388
  67.9 128.5 %all-gather.6.cloned.1.call-start = ((), (), s32[]{:S(2)}) async-start(), calls=%async_computation.3 | async-start | bytes 7077888 | tf_op jit(solution)/shard_map/all_gather | solution.py:1066
  68.6 191.3 %all-gather.8.cloned.1.call-start = ((), (), s32[]{:S(2)}) async-start(), calls=%async_computation.4 | async-start | bytes 7077888 | tf_op jit(solution)/shard_map/all_gather | solution.py:1083
  71.2 24.2 %copy-start.13 = (f32[2,4]{1,0:T(2,128)}, f32[2,4]{1,0:T(2,128)S(1)}, u32[]{:S(2)}) copy-start(f32[2,4]{1,0:T(2,128)S(1)} %copy.80.mix_ref) | copy-start | bytes 100
  195.0 161.0 %copy-start.16 = (f32[256,1536]{1,0:T(8,128)}, f32[256,1536]{1,0:T(8,128)S(1)}, u32[]{:S(2)}) copy-start(f32[256,1536]{1,0:T(8,128)S(1)} %get-tuple-element.142) | copy-start | bytes 4718596
  195.1 161.0 %copy-start.37 = (f32[256]{0:T(256)}, f32[256]{0:T(256)S(1)}, u32[]{:S(2)}) copy-start(f32[256]{0:T(256)S(1)} %get-tuple-element.140) | copy-start | bytes 3076
  195.1 161.0 %copy-start.44 = (f32[256]{0:T(256)}, f32[256]{0:T(256)S(1)}, u32[]{:S(2)}) copy-start(f32[256]{0:T(256)S(1)} %get-tuple-element.139) | copy-start | bytes 3076
  196.4 157.3 %reduce-scatter.3.cloned.1.call-start = ((), (), s32[]{:S(2)}) async-start(), calls=%async_computation.5 | async-start | bytes 7077888 | tf_op jit(solution)/shard_map/reduce_scatter | solution.py:1096
  285.7 322.5 %all-reduce.11.cloned.1.call-start = ((), (), s32[]{:S(2)}) async-start(), calls=%async_computation.7 | async-start | bytes 9437184 | tf_op jit(solution)/shard_map/psum | solution.py:1104
  294.1 8.3 %copy-start.56 = (bf16[2048,512]{1,0:T(8,128)(2,1)S(1)}, bf16[2048,512]{1,0:T(8,128)(2,1)}, u32[]{:S(2)}) copy-start(bf16[2048,512]{1,0:T(8,128)(2,1)} %get-tuple-element.63) | copy-start | bytes 6291460
  294.1 15.9 %slice-start = ((s8[6291456]{0:T(1024)(128)(4,1)}), s8[4194304]{0:T(1024)(128)(4,1)S(1)}, s32[]{:S(2)}) async-start(s8[6291456]{0:T(1024)(128)(4,1)} %bitcast.171), calls=%async_computation.8 | async-start | bytes 8388608
  302.3 7.6 %slice-start.1 = ((s8[6291456]{0:T(1024)(128)(4,1)}), s8[2097152]{0:T(1024)(128)(4,1)S(1)}, s32[]{:S(2)}) async-start(s8[6291456]{0:T(1024)(128)(4,1)} %bitcast.171), calls=%async_computation.9 | async-start | bytes 4194304
  302.3 7.6 %copy-start.53 = (bf16[2048,512]{1,0:T(8,128)(2,1)S(1)}, bf16[2048,512]{1,0:T(8,128)(2,1)}, u32[]{:S(2)}) copy-start(bf16[2048,512]{1,0:T(8,128)(2,1)} %get-tuple-element.62) | copy-start | bytes 6291460
  353.7 254.5 %reduce-scatter.5.cloned.1.call-start = ((), (), s32[]{:S(2)}) async-start(), calls=%async_computation.6 | async-start | bytes 7077888 | tf_op jit(solution)/shard_map/reduce_scatter | solution.py:1103
  356.0 28.0 %copy-start.46 = (f32[256]{0:T(256)}, f32[256]{0:T(256)S(1)}, u32[]{:S(2)}) copy-start(f32[256]{0:T(256)S(1)} %broadcast_multiply_fusion.1) | copy-start | bytes 3076
  486.0 7.0 %copy-start.35 = (f32[1536]{0:T(1024)S(1)}, f32[1536]{0:T(1024)}, u32[]{:S(2)}) copy-start(f32[1536]{0:T(1024)} %get-tuple-element.108) | copy-start | bytes 18436
  498.8 8.7 %copy-start.4 = (f32[256,1536]{1,0:T(8,128)S(1)}, f32[256,1536]{1,0:T(8,128)}, u32[]{:S(2)}) copy-start(f32[256,1536]{1,0:T(8,128)} %get-tuple-element.120.xs_ref) | copy-start | bytes 4718596
  608.3 7.9 %copy-start.33 = (f32[1536]{0:T(1024)S(1)}, f32[1536]{0:T(1024)}, u32[]{:S(2)}) copy-start(f32[1536]{0:T(1024)} %param.21) | copy-start | bytes 18436
  (42 other events, 136.5 us)
Sparse Core Ops, SparseCore 0:
  68.0 50.5 all-gather.3
  120.8 70.1 all-gather.5
  196.5 63.3 all-gather.7
  285.8 67.8 reduce-scatter.2
  357.8 114.4 all-reduce.10
  474.5 93.1 reduce-scatter.4

commit v3 on v2

--- a/solution.py
+++ b/solution.py
@@ -62,11 +62,40 @@
     return centred * inv, inv
 
 
+def widen(sources, targets, dim, pairs):
+    pair = pl.program_id(0)
+    for source, target in zip(sources, targets):
+        for h in range(2):
+            target[:, h * LANES + dim : (h + 1) * LANES] = jnp.zeros((target.shape[0], LANES - dim), target.dtype)
+        for p in range(pairs):
+
+            @pl.when(pair == p)
+            def _():
+                for h in range(2):
+                    left = (2 * p + h) * dim
+                    target[:, h * LANES : h * LANES + dim] = source[:, left : left + dim]
+
+
+def place_head(target, rows, left, h, value, dim, pairs):
+    pair = pl.program_id(0)
+    for p in range(pairs):
+
+        @pl.when(pair == p)
+        def _():
+            at = left + (2 * p + h) * dim
+            target[rows, at : at + dim] = value[:, :dim].astype(target.dtype)
+
+
 def forward_kernel(
-    dim, taps, q_ref, k_ref, v_ref, t_ref, rowc_ref, colp_ref, colc_ref, gain_ref, mix_ref,
-    normed_ref, att_ref, prob_ref, lm_ref, lo_ref, p_ref, cv_ref, mx_ref, sm_ref, acc_ref,
+    dim, taps, pairs, qs_ref, ks_ref, vs_ref, t_ref, rowc_ref, colp_ref, colc_ref, gain_ref, mix_ref,
+    normed_ref, att_ref, prob_ref, lm_ref, lo_ref, p_ref, cv_ref, mx_ref, sm_ref, acc_ref, q_ref, k_ref, v_ref,
 ):
     step = pl.program_id(1)
+
+    @pl.when(step == 0)
+    def _():
+        widen((qs_ref, ks_ref, vs_ref), (q_ref, k_ref, v_ref), dim, pairs)
+
     first = step * ROWS
     top = pl.multiple_of(first + EDGE - HEADER, 16)
     tall = ROWS + HEADER
@@ -154,13 +183,13 @@
         att_ref[:, g * LANES : (g + 1) * LANES] = att
         unit, _ = group_stats(att, dim)
         normed = unit * gain_ref[0:1, g * LANES : (g + 1) * LANES]
-        normed_ref[:, g * LANES : (g + 1) * LANES] = normed.astype(jnp.bfloat16)
+        place_head(normed_ref, pl.ds(pl.multiple_of(first, ROWS), ROWS), 0, g, normed, dim, pairs)
 
 
 def backward_kernel(
-    dim, taps, span, q_ref, k_ref, v_ref, t_ref, rowc_ref, colp_ref, colt_ref, rowt_ref, prob_ref, att_ref, dn_ref,
-    gain_ref, mix_ref, dq_ref, dk_ref, dv_ref, taps_ref, dmix_ref, dgain_ref,
-    dp_ref, dc_ref, dl_ref, lt_ref, dkt_ref, dvt_ref, datt_ref, dattt_ref, qt_ref, rs_ref, dqa_ref, dm_ref, ahead_ref, g_ref,
+    dim, taps, span, pairs, qs_ref, ks_ref, vs_ref, t_ref, rowc_ref, colp_ref, colt_ref, rowt_ref, prob_ref, att_ref, dns_ref,
+    gain_ref, mix_ref, dproj_ref, taps_ref, dmix_ref, dgain_ref,
+    dp_ref, dc_ref, dl_ref, lt_ref, dkt_ref, dvt_ref, datt_ref, dattt_ref, qt_ref, rs_ref, dqa_ref, dm_ref, ahead_ref, g_ref, q_ref, k_ref, v_ref, dn_ref,
 ):
     pair = pl.program_id(0)
     turn = pl.program_id(1)
@@ -181,9 +210,14 @@
         g_ref[...] = jnp.zeros(g_ref.shape, jnp.float32)
         dmix_ref[...] = jnp.zeros(dmix_ref.shape, jnp.float32)
         dgain_ref[...] = jnp.zeros(dgain_ref.shape, jnp.float32)
-        for ref in (dq_ref, dv_ref):
-            ref[:EDGE, :] = jnp.zeros((EDGE, 2 * LANES), jnp.bfloat16)
-            ref[ref.shape[0] - EDGE :, :] = jnp.zeros((EDGE, 2 * LANES), jnp.bfloat16)
+        widen((qs_ref, ks_ref, vs_ref), (q_ref, k_ref, v_ref), dim, pairs)
+
+        @pl.when(pair == 0)
+        def _():
+            for rows in (slice(0, EDGE), slice(dproj_ref.shape[0] - EDGE, dproj_ref.shape[0])):
+                dproj_ref[rows, :] = jnp.zeros((EDGE, dproj_ref.shape[1]), jnp.bfloat16)
+
+    widen((dns_ref,), (dn_ref,), dim, pairs)
 
     @pl.when(turn > 0)
     def _():
@@ -281,7 +315,7 @@
 
     lax.fori_loop(0, blocks + 1, logits, 0)
     for h in range(2):
-        dq_ref[pl.ds(own, ROWS), h * LANES : (h + 1) * LANES] = dqa_ref[h].astype(jnp.bfloat16)
+        place_head(dproj_ref, pl.ds(own, ROWS), 0, h, dqa_ref[h], dim, pairs)
 
     @pl.when(step == 0)
     def _():
@@ -303,10 +337,12 @@
             raw = jnp.where(keep, dot(query, near, NT), 0.0)
             g_ref[h] += dot(raw.T.astype(jnp.bfloat16), shifted)
             dl = jnp.where(keep, dot(shifted, t_ref[h], NT), 0.0).astype(jnp.bfloat16)
-            dq_ref[head, cols] = dot(dl, near).astype(jnp.bfloat16)
+            place_head(dproj_ref, head, 0, h, dot(dl, near), dim, pairs)
             dkt_ref[h, :, : 2 * LANES] += dot(query.astype(jnp.float32).T.astype(jnp.bfloat16), dl)
-            dk_ref[:, cols] = dkt_ref[h].T.astype(jnp.bfloat16)
-            dv_ref[pl.ds(EDGE, dvt_ref.shape[2]), cols] = dvt_ref[h].T.astype(jnp.bfloat16)
+            every = slice(0, dkt_ref.shape[2])
+            place_head(dproj_ref, every, 2 * pairs * dim, h, dkt_ref[h].T, dim, pairs)
+            inner = slice(EDGE, EDGE + dvt_ref.shape[2])
+            place_head(dproj_ref, inner, 4 * pairs * dim, h, dvt_ref[h].T, dim, pairs)
         shape = (2 * LANES, taps * LANES)
         lanes = lax.broadcasted_iota(jnp.int32, shape, 1) & (LANES - 1)
         diff = lanes + (EDGE + span // 2) - lax.broadcasted_iota(jnp.int32, shape, 0)
@@ -325,10 +361,10 @@
     frame = tall - 2 * EDGE
     pairs = mix.shape[0]
     steps = frame // ROWS
-    whole = lambda off: pl.BlockSpec((tall, 2 * LANES), lambda p, r: (0, off * pairs + p))
+    whole = lambda off: pl.BlockSpec((tall, 2 * pairs * dim), lambda p, r: (0, off))
     wide = pairs * 2 * LANES
     return pl.pallas_call(
-        functools.partial(forward_kernel, dim, taps),
+        functools.partial(forward_kernel, dim, taps, mix.shape[0]),
         grid=(pairs, steps),
         in_specs=[
             whole(0), whole(1), whole(2),
@@ -340,12 +376,12 @@
             pl.BlockSpec(memory_space=pltpu.SMEM),
         ],
         out_specs=[
-            pl.BlockSpec((ROWS, 2 * LANES), lambda p, r: (r, p)),
+            pl.BlockSpec((frame, 2 * pairs * dim), lambda p, r: (0, 0)),
             pl.BlockSpec((ROWS, 2 * LANES), lambda p, r: (r, p)),
             pl.BlockSpec((2, ROWS, frame), lambda p, r: (p, r, 0)),
         ],
         out_shape=[
-            jax.ShapeDtypeStruct((frame, wide), jnp.bfloat16),
+            jax.ShapeDtypeStruct((frame, 2 * pairs * dim), jnp.bfloat16),
             jax.ShapeDtypeStruct((frame, wide), jnp.float32),
             jax.ShapeDtypeStruct((2 * pairs, frame, frame), PROB),
         ],
@@ -357,6 +393,9 @@
             pltpu.VMEM((2, ROWS, LANES), jnp.float32),
             pltpu.VMEM((2, ROWS, LANES), jnp.float32),
             pltpu.VMEM((2, ROWS, LANES), jnp.float32),
+            pltpu.VMEM((tall, 2 * LANES), jnp.bfloat16),
+            pltpu.VMEM((tall, 2 * LANES), jnp.bfloat16),
+            pltpu.VMEM((tall, 2 * LANES), jnp.bfloat16),
         ],
         cost_estimate=pl.CostEstimate(flops=10_000_000_000, bytes_accessed=40_000_000, transcendentals=0),
         compiler_params=pltpu.CompilerParams(vmem_limit_bytes=48 << 20),
@@ -369,11 +408,11 @@
     frame = tall - 2 * EDGE
     pairs = mix.shape[0]
     steps = frame // ROWS
-    whole = lambda off: pl.BlockSpec((tall, 2 * LANES), lambda p, r: (0, off * pairs + p))
+    whole = lambda off: pl.BlockSpec((tall, 2 * pairs * dim), lambda p, r: (0, off))
     wide = pairs * 2 * LANES
     back = lambda r: steps - 1 - r
     return pl.pallas_call(
-        functools.partial(backward_kernel, dim, taps, span),
+        functools.partial(backward_kernel, dim, taps, span, mix.shape[0]),
         grid=(pairs, steps),
         in_specs=[
             whole(0), whole(1), whole(2),
@@ -384,22 +423,18 @@
             pl.BlockSpec((1, frame), lambda p, r: (0, 0)),
             pl.BlockSpec((2, ROWS, frame), lambda p, r: (p, back(r), 0)),
             pl.BlockSpec((ROWS, 2 * LANES), lambda p, r: (back(r), p)),
-            pl.BlockSpec((ROWS, 2 * LANES), lambda p, r: (back(r), p)),
+            pl.BlockSpec((ROWS, 2 * pairs * dim), lambda p, r: (back(r), 0)),
             pl.BlockSpec((1, 2 * LANES), lambda p, r: (0, p)),
             pl.BlockSpec(memory_space=pltpu.SMEM),
         ],
         out_specs=[
-            pl.BlockSpec((tall, 2 * LANES), lambda p, r: (0, p)),
-            pl.BlockSpec((tall, 2 * LANES), lambda p, r: (0, p)),
-            pl.BlockSpec((tall, 2 * LANES), lambda p, r: (0, p)),
+            pl.BlockSpec((tall, 6 * pairs * dim), lambda p, r: (0, 0)),
             pl.BlockSpec((2, 16, taps * LANES), lambda p, r: (p, 0, 0)),
             pl.BlockSpec((1, 8, LANES), lambda p, r: (p, 0, 0)),
             pl.BlockSpec((1, 2 * LANES), lambda p, r: (0, p)),
         ],
         out_shape=[
-            jax.ShapeDtypeStruct((tall, wide), jnp.bfloat16),
-            jax.ShapeDtypeStruct((tall, wide), jnp.bfloat16),
-            jax.ShapeDtypeStruct((tall, wide), jnp.bfloat16),
+            jax.ShapeDtypeStruct((tall, 6 * pairs * dim), jnp.bfloat16),
             jax.ShapeDtypeStruct((2 * pairs, 16, taps * LANES), jnp.float32),
             jax.ShapeDtypeStruct((pairs, 8, LANES), jnp.float32),
             jax.ShapeDtypeStruct((1, wide), jnp.float32),
@@ -419,6 +454,10 @@
             pltpu.VMEM((4, ROWS, LANES), jnp.float32),
             pltpu.VMEM((2 * HEADER, LANES), jnp.float32),
             pltpu.VMEM((2, 2 * LANES, taps * LANES), jnp.float32),
+            pltpu.VMEM((tall, 2 * LANES), jnp.bfloat16),
+            pltpu.VMEM((tall, 2 * LANES), jnp.bfloat16),
+            pltpu.VMEM((tall, 2 * LANES), jnp.bfloat16),
+            pltpu.VMEM((ROWS, 2 * LANES), jnp.float32),
         ],
         cost_estimate=pl.CostEstimate(flops=10_000_000_000, bytes_accessed=40_000_000, transcendentals=0),
         compiler_params=pltpu.CompilerParams(vmem_limit_bytes=48 << 20),
@@ -988,6 +1027,91 @@
     )(grad_in, grad_out, tokens, scaled, small)
 
 
+def rep_sum_kernel(
+    g_refs, o_ref, held, got, last, load_sem, one_send, one_recv, on_send, on_recv
+):
+    rep = lax.axis_index("rep")
+    me = lax.axis_index("seq")
+    near = [rep ^ 1, rep ^ 2]
+    past = [rep ^ 2, rep ^ 1]
+    meet([(r, me) for r in near])
+    waits = []
+
+    def push(src, dst, send_sem, recv_sem, peer):
+        copy = send(src, dst, send_sem, recv_sem, peer)
+        copy.start()
+        waits.append(copy)
+
+    def arrived(dst, send_sem, recv_sem):
+        send(dst, dst, send_sem, recv_sem, (near[0], me)).wait_recv()
+
+    blocks = [(k, s) for k in range(3) for s in range(2)]
+
+    def rows(n, r):
+        k, s = blocks[n]
+        size = last[k].shape[1]
+        return g_refs[k].at[pl.ds(pl.multiple_of(r * 2 * size + s * size, 16), size), :]
+
+    for n, (k, s) in enumerate(blocks):
+        for m, r in enumerate((near[s], rep ^ 3)):
+            push(rows(n, r), got[k].at[s, m], one_send.at[n, m], one_recv.at[n, m], (near[s], me))
+    own = [
+        pltpu.make_async_copy(rows(n, r), held[k].at[s, m], load_sem.at[2 * n + m])
+        for n, (k, s) in enumerate(blocks)
+        for m, r in enumerate((rep, past[s]))
+    ]
+    for copy in own:
+        copy.start()
+    wide = jnp.float32
+    for n in range(len(blocks) + 2):
+        if n < len(blocks):
+            k, s = blocks[n]
+            own[2 * n + 1].wait()
+            arrived(got[k].at[s, 1], one_send.at[n, 1], one_recv.at[n, 1])
+            held[k][s, 1] = (held[k][s, 1].astype(wide) + got[k][s, 1].astype(wide)).astype(jnp.bfloat16)
+            push(held[k].at[s, 1], last[k].at[s], on_send.at[n], on_recv.at[n], (past[s], me))
+        if n >= 2:
+            k, s = blocks[n - 2]
+            size = last[k].shape[1]
+            own[2 * n - 4].wait()
+            arrived(got[k].at[s, 0], one_send.at[n - 2, 0], one_recv.at[n - 2, 0])
+            arrived(last[k].at[s], on_send.at[n - 2], on_recv.at[n - 2])
+            total = held[k][s, 0].astype(wide) + got[k][s, 0].astype(wide) + last[k][s].astype(wide)
+            total = total.astype(jnp.bfloat16)
+            lanes = last[0].shape[2]
+            if k < 2:
+                o_ref[s * size : (s + 1) * size, k * lanes : (k + 1) * lanes] = total
+            else:
+                for j in range(total.shape[1] // lanes):
+                    first = (2 * j + s) * size
+                    o_ref[first : first + size, 2 * lanes :] = total[:, j * lanes : (j + 1) * lanes]
+    for copy in waits:
+        copy.wait_send()
+
+
+def rep_sum(arrays):
+    dma = pltpu.SemaphoreType.DMA
+    shapes = [(value.shape[0] // 4, value.shape[1]) for value in arrays]
+    low = jnp.bfloat16
+
+    def body(*refs):
+        rep_sum_kernel(refs[:3], refs[3], refs[4:7], refs[7:10], refs[10:13], *refs[13:])
+
+    return pl.pallas_call(
+        body,
+        in_specs=[pl.BlockSpec(memory_space=pl.ANY)] * 3,
+        out_specs=pl.BlockSpec(memory_space=pltpu.VMEM),
+        out_shape=jax.ShapeDtypeStruct((shapes[0][0], 3 * shapes[0][1]), low),
+        scratch_shapes=[pltpu.VMEM((2, 2, rows // 2, cols), low) for rows, cols in shapes]
+        + [pltpu.VMEM((2, 2, rows // 2, cols), low) for rows, cols in shapes]
+        + [pltpu.VMEM((2, rows // 2, cols), low) for rows, cols in shapes]
+        + [dma((12,)), dma((6, 2)), dma((6, 2)), dma((6,)), dma((6,))],
+        cost_estimate=pl.CostEstimate(flops=2_000_000_000, bytes_accessed=20_000_000, transcendentals=0),
+        compiler_params=pltpu.CompilerParams(collective_id=6, has_side_effects=True, vmem_limit_bytes=32 << 20),
+        name="rep_sum",
+    )(*arrays)
+
+
 def rms_scale(values):
     return lax.rsqrt(jnp.mean(values * values, axis=-1, keepdims=True) + EPS)
 
@@ -1043,7 +1167,7 @@
     toep, toep_split = split_toeplitz(toeplitz(own_kernel, scale))
 
     reps = lax.axis_size("rep")
-    direct = team == 4 and reps == 4 and (width // count) % (16 * reps) == 0
+    direct = team == 4 and reps == 4 and down_weight.shape[0] * 3 == width and (width // count) % (16 * reps) == 0
     first_scale = rms_scale(resid_in)
     normed_in = (resid_in * first_scale * first_gain).astype(jnp.bfloat16)
     if direct:
@@ -1061,12 +1185,10 @@
     dmlp = (row_valid * grad_out).astype(jnp.bfloat16)
     own_input, output_weight, dmlp = lax.optimization_barrier((own_input, output_weight, dmlp))
     full_output = lax.all_gather(output_weight, "seq", axis=0, tiled=True)
-    own_input = pad_heads(own_input, dim)
     proj = jnp.dot(normed_frame, own_input, preferred_element_type=jnp.float32).astype(jnp.bfloat16)
     dmlp_all = lax.all_gather(dmlp, "seq", axis=0, tiled=True)
     normed_own, att, prob = attention_forward(proj, toep_split, codes, own_gain, own_mix, dim, taps)
     normed_own, full_output = lax.optimization_barrier((normed_own, full_output))
-    normed_own = cut_heads(normed_own, dim)
 
     def to_rows(values):
         moved = lax.all_to_all(
@@ -1099,9 +1221,14 @@
         lax.dot_general(left, right, contract_rows, preferred_element_type=jnp.float32).astype(jnp.bfloat16)
         for left, right in ((inputs_all, gate_grad), (inputs_all, up_grad), (hidden, dmlp_all))
     ]
+    if direct:
+        mlp_grads = rep_sum(mlp_grads)
     dmid_low, mlp_part, mlp_grads = lax.optimization_barrier((dmid_low, mlp_part, mlp_grads))
     mlp_low = lax.psum_scatter(mlp_part, "seq", scatter_dimension=0, tiled=True)
-    mlp_grads = [lax.psum(value, "rep") for value in mlp_grads]
+    if direct:
+        packed = lax.all_gather(mlp_grads, "rep", axis=0)
+    else:
+        mlp_grads = [lax.psum(value, "rep") for value in mlp_grads]
     dmid = dmid_low.astype(jnp.float32)
     second_part = jnp.sum(dmid * resid * second_scale, axis=0)
     dresid = grad_out + norm_back(dmid, resid, second_scale, second_gain)
@@ -1114,12 +1241,11 @@
     dnormed_own = lax.dot_general(dbranch_frame, own_output, NT, preferred_element_type=jnp.float32)
     own_output_grad = lax.dot_general(normed_own, dbranch_frame, contract_rows, preferred_element_type=jnp.float32)
     own_output_grad = own_output_grad.astype(jnp.bfloat16)
-    dq, dk, dv, dtoep, dmix, dgain = attention_backward(
-        proj, toep, codes, prob, att, pad_heads(dnormed_own, dim), own_gain, own_mix, dim, taps, span
+    dproj, dtoep, dmix, dgain = attention_backward(
+        proj, toep, codes, prob, att, dnormed_own, own_gain, own_mix, dim, taps, span
     )
-    dproj = jnp.concatenate([dq, dk, dv], axis=1)
     own_input_grad = lax.dot_general(normed_frame, dproj, contract_rows, preferred_element_type=jnp.float32)
-    own_input_grad = cut_heads(own_input_grad.astype(jnp.bfloat16), dim)
+    own_input_grad = own_input_grad.astype(jnp.bfloat16)
     dnormin_part = lax.dot_general(dproj, own_input, NT, preferred_element_type=jnp.float32).astype(jnp.bfloat16)
     def spread(values, size):
         empty = jnp.zeros((size,) + values.shape[1:], jnp.float32)
@@ -1160,7 +1286,11 @@
         grad_input_w, grad_output_w = [
             lax.psum(value.astype(jnp.bfloat16), "rep") for value in (grad_input_w, grad_output_w)
         ]
-    dnormin, mlp_low, mlp_grads = lax.optimization_barrier((dnormin, mlp_low, mlp_grads))
+    dnormin, mlp_low, mlp_sums = lax.optimization_barrier((dnormin, mlp_low, packed if direct else mlp_grads))
+    if direct:
+        packed = mlp_sums
+    else:
+        mlp_grads = mlp_sums
     result = resid + row_valid * mlp_low.astype(jnp.float32)
     if not direct:
         first_part = jnp.sum(dnormin * resid_in * first_scale, axis=0)
@@ -1168,6 +1298,13 @@
     grad_in = dresid + norm_back(dnormin, resid_in, first_scale, first_gain)
 
     grad_kernel, grad_mix, grad_second, grad_group = others
+    if direct:
+        units = down_weight.shape[0]
+        mlp_grads = [
+            packed[:, :, :units].reshape(width, units),
+            packed[:, :, units : 2 * units].reshape(width, units),
+            packed[:, :, 2 * units :].reshape(reps, 3, units // reps, units).transpose(0, 2, 1, 3).reshape(units, width),
+        ]
     grads = [value.astype(jnp.float32) for value in (grad_input_w, grad_output_w, *mlp_grads)]
     return (
         result.astype(jnp.bfloat16)[None], grad_in.astype(jnp.bfloat16)[None], grads[0], grads[1], grad_kernel,

time: 639 us -> 608 us (0.951)
  Pallas kernels: 326 us -> 381 us
  waiting for transfers between devices: 94.7 us -> 54.9 us
  local copies, waits for them, and re-layouts: 58 us -> 30 us
  matrix products: 97 us -> 87.6 us
    pallas_call x2 -> x3, Pallas kernels: 131 us -> 186 us  [the longest x1 77.3 us: attention_backward(): pl.pallas_call(functools.partial(backward_kernel, dim, taps, span, mix.sh...]
    reduce_scatter x1, waiting for transfers between devices: 39.1 us -> 0.01 us  [on_device(): lax.psum_scatter(dmid_part, 'seq', scatter_dimension=0, tiled=True)]
    reshape x4 -> x0, local copies, waits for them, and re-layouts: 8.98 us -> none  [the longest x2 5.55 us: cut_heads(): return shaped.reshape(values.shape[:-1] + (-1,))]
    unnamed x137 -> x94, local copies, waits for them, and re-layouts: 15.9 us -> 17.2 us
  transfers between devices with their start and end apart: 6 -> 6, of which waited for: 2 -> 1; matrix products, arithmetic and copies ran while one was open for 21% -> 15% of each run, Pallas kernels for 44% -> 55%
where the time goes in v3:
time: 608 us; the launch traced here: 600 us
  Pallas kernels  381 us (63%)
  matrix products  87.6 us (14%)
  waiting for transfers between devices  54.9 us (9%)
  local copies, waits for them, and re-layouts  30 us (5%)
  other arithmetic  29.9 us (5%)
  between operations  15.1 us (2%)
    pallas_call x1, Pallas kernels, reduce_weights(): pl.pallas_call(functools.partial(reduce_kernel, reps, count), in_specs=[h...  82.9 us
    pallas_call x1, Pallas kernels, attention_backward(): pl.pallas_call(functools.partial(backward_kernel, dim, taps, span, mix.sh...  77.3 us
    pallas_call x1, Pallas kernels, attention_forward(): pl.pallas_call(functools.partial(forward_kernel, dim, taps, mix.shape[0])...  66.2 us
    all_gather x1, waiting for transfers between devices, on_device(): inputs_all = lax.all_gather(normed_mid, 'seq', axis=0, tiled=True)  53.8 us
    pallas_call x1, Pallas kernels, gather_weight(): pl.pallas_call(functools.partial(gather_kernel, reps, count), in_specs=[p...  52.1 us
    pallas_call x1, Pallas kernels, rep_sum(): pl.pallas_call(body, in_specs=[pl.BlockSpec(memory_space=pl.ANY)] * 3, ou...  42.8 us
    pallas_call x1, Pallas kernels, frame_swap(): pl.pallas_call(frame_swap_kernel, in_specs=[pl.BlockSpec(memory_space=pl....  32.8 us
    pallas_call x1, Pallas kernels, frame_gather(): pl.pallas_call(frame_gather_kernel, in_specs=[pl.BlockSpec(memory_space=p...  27 us
  transfers between devices with their start and end apart: 6, of which 1 were waited for; matrix products, arithmetic and copies ran while one was open for 15% of the time, Pallas kernels for 55%

profile of v3, /device:TPU:25, one launch (start us, length us, event | category | flops | bytes accessed | tf_op | source)
XLA Modules:
  0.0 599.7 jit_solution(14350740697379435617)
XLA Ops:
  15.3 52.1 %gather_weight.1 = (bf16[1536,1152]{1,0:T(8,128)(2,1)}, bf16[1152,1536]{1,0:T(8,128)(2,1)}) custom-call(bf16[192,4608]{1,0:T(8,128)(2,1)} %w_ref.1, bf16[256,1536]{1,0:T(8,128)(2,1)} %get-tuple-element.121.x_ref, bf16[64,1536]{1,0:T(8,128)(2,1)} %broadcast_in_dim.179.z_ref), custom_call_target="tpu_custom_call" | custom-call | flops 2000000000 | bytes 20000000 | tf_op jit(solution)/shard_map/gather_weight/pallas_call | solution.py:645
  79.9 4.9 convolution_convert_fusion.3.qs_ref.ks_ref.vs_ref
  85.0 66.2 %attend.1 = (bf16[1024,384]{1,0:T(8,128)(2,1)S(1)}, f32[1024,512]{1,0:T(8,128)S(1)}, f32[4,1024,1024]{2,1,0:T(8,128)}) custom-call(bf16[1152,1152]{1,0:T(8,128)(2,1)S(1)} %convolution_convert_fusion.3.qs_ref.ks_ref.vs_ref, bf16[1152,1152]{1,0:T(8,128)(2,1)S(1)} %convolution_convert_fusion.3.qs_ref.ks_ref.vs_ref, ...), custom_call_target="tpu_custom_call" | custom-call | flops 10000000000 | bytes 40000000 | tf_op jit(solution)/shard_map/attend/pallas_call | solution.py:366
  155.7 32.8 %frame_swap.1 = bf16[256,1536]{1,0:T(8,128)(2,1)} custom-call(bf16[1024,384]{1,0:T(8,128)(2,1)} %copy-done.5), custom_call_target="tpu_custom_call" | custom-call | flops 2000000000 | bytes 2000000 | tf_op jit(solution)/shard_map/frame_swap/pallas_call | solution.py:752
  188.5 4.3 multiply_reduce_fusion
  195.4 8.6 %fusion.42 = f32[2048,512]{1,0:T(8,128)} fusion(bf16[2048,1536]{1,0:T(8,128)(2,1)} %all-gather.8.cloned.1.call-done, bf16[512,1536]{1,0:T(8,128)(2,1)} %param.26), kind=kOutput, calls=%fused_computation.127 | convolution fusion | flops 3221225472 | bytes 12058624 | tf_op jit(solution)/shard_map/dot_general | solution.py:1208
  204.0 53.8 %all-gather.10.cloned.1.call-done = bf16[2048,1536]{1,0:T(8,128)(2,1)} async-done(((bf16[256,1536]{1,0:T(8,128)(2,1)}), bf16[2048,1536]{1,0:T(8,128)(2,1)}) %all-gather.10.cloned.1.call-update) | async-done | bytes 6291472 | tf_op jit(solution)/shard_map/all_gather | solution.py:1205
  257.8 6.1 %fusion.43 = f32[2048,512]{1,0:T(8,128)S(1)} fusion(bf16[2048,1536]{1,0:T(8,128)(2,1)} %all-gather.10.cloned.1.call-done, bf16[1536,512]{1,0:T(8,128)(2,1)} %param.24), kind=kOutput, calls=%fused_computation.128 | convolution fusion | flops 3221225472 | bytes 12058624 | tf_op jit(solution)/shard_map/dot_general | solution.py:1206
  264.1 6.8 %multiply_convert_fusion = (bf16[2048,512]{1,0:T(8,128)(2,1)}, bf16[2048,512]{1,0:T(8,128)(2,1)}, bf16[2048,512]{1,0:T(8,128)(2,1)}) fusion(f32[2048,512]{1,0:T(8,128)S(1)} %fusion.43, f32[2048,512]{1,0:T(8,128)S(1)} %copy-done.36, bf16[2048,1536]{1,0:T(8,128)(2,1)S(1)} %copy-done.27, bf16[1536,512]{1,0:T(8,128)(2,1)S(1)} %copy-done), kind=kOutput, calls=%fused_computation.8 | convolution fusion | flops 3238002688 | bytes 22544384 | tf_op jit(solution)/shard_map/dot_general | solution.py:1207
  271.0 5.2 fusion.44
  276.2 7.6 %add_convert_fusion = bf16[2048,1536]{1,0:T(8,128)(2,1)} fusion(f32[2048,1536]{1,0:T(8,128)S(1)} %fusion.44, bf16[2048,512]{1,0:T(8,128)(2,1)} %get-tuple-element.57, bf16[1536,512]{1,0:T(8,128)(2,1)S(1)} %copy-done), kind=kOutput, calls=%fused_computation | convolution fusion | flops 3227516928 | bytes 22544384 | tf_op jit(solution)/shard_map/dot_general | solution.py:1215
  284.3 7.0 %convolution_convert_fusion.4.refs_2_ = bf16[512,1536]{1,0:T(8,128)(2,1)S(1)} fusion(bf16[2048,512]{1,0:T(8,128)(2,1)} %get-tuple-element.55, bf16[2048,1536]{1,0:T(8,128)(2,1)} %all-gather.8.cloned.1.call-done), kind=kOutput, calls=%fused_computation.32 | convolution fusion | flops 3222011904 | bytes 9961472 | tf_op jit(solution)/shard_map/dot_general | solution.py:1221
  291.3 6.5 %convolution_convert_fusion.5.refs_1_ = bf16[1536,512]{1,0:T(8,128)(2,1)S(1)} fusion(bf16[2048,1536]{1,0:T(8,128)(2,1)} %all-gather.10.cloned.1.call-done, bf16[2048,512]{1,0:T(8,128)(2,1)S(1)} %copy-done.34), kind=kOutput, calls=%fused_computation.33 | convolution fusion | flops 3222011904 | bytes 9961472 | tf_op jit(solution)/shard_map/dot_general | solution.py:1221
  297.9 3.6 convolution_convert_fusion.6.refs_0_
  301.5 42.8 %rep_sum.1 = bf16[384,1536]{1,0:T(8,128)(2,1)} custom-call(bf16[1536,512]{1,0:T(8,128)(2,1)S(1)} %convolution_convert_fusion.6.refs_0_, bf16[1536,512]{1,0:T(8,128)(2,1)S(1)} %convolution_convert_fusion.5.refs_1_, bf16[512,1536]{1,0:T(8,128)(2,1)S(1)} %convolution_convert_fusion.4.refs_2_), custom_call_target="tpu_custom_call" | custom-call | flops 2000000000 | bytes 20000000 | tf_op jit(solution)/shard_map/rep_sum/pallas_call | solution.py:1100
  344.3 8.2 %convolution_convert_fusion.2 = bf16[2048,1536]{1,0:T(8,128)(2,1)} fusion(bf16[2048,512]{1,0:T(8,128)(2,1)} %get-tuple-element.55, bf16[512,1536]{1,0:T(8,128)(2,1)} %param.26), kind=kOutput, calls=%fused_computation.3 | convolution fusion | flops 3224371200 | bytes 9961472 | tf_op jit(solution)/shard_map/dot_general | solution.py:1219
  358.0 27.0 %frame_gather.1 = bf16[1024,1536]{1,0:T(8,128)(2,1)} custom-call(bf16[256,1536]{1,0:T(8,128)(2,1)} %multiply_convert_fusion.3.x_ref), custom_call_target="tpu_custom_call" | custom-call | flops 2000000000 | bytes 8000000 | tf_op jit(solution)/shard_map/frame_gather/pallas_call | solution.py:709
  385.0 4.4 fusion.25.dns_ref
  389.6 77.3 %attend_back.1 = (bf16[1152,1152]{1,0:T(8,128)(2,1)}, f32[4,16,768]{2,1,0:T(8,128)S(1)}, f32[2,8,128]{2,1,0:T(8,128)S(1)}, f32[1,512]{1,0:T(1,128)S(1)}) custom-call(bf16[1152,1152]{1,0:T(8,128)(2,1)} %copy-done.7, bf16[1152,1152]{1,0:T(8,128)(2,1)} %copy-done.7, bf16[1152,1152]{1,0:T(8,128)(2,1)} %copy-done.7, ...), custom_call_target="tpu_custom_call" | custom-call | flops 10000000000 | bytes 40000000 | tf_op jit(solution)/shard_map/attend_back/pallas_call | solution.py:414
  468.0 3.5 convolution_convert_fusion.7.go_ref
  471.9 5.1 convolution_convert_fusion.dn_ref
  477.0 5.7 convolution_convert_fusion.1.gi_ref
  482.7 82.9 %reduce_weights.1 = (bf16[192,4608]{1,0:T(8,128)(2,1)S(1)}, bf16[192,1536]{1,0:T(8,128)(2,1)S(1)}, f32[256,1536]{1,0:T(8,128)S(1)}, f32[48,128]{1,0:T(8,128)S(1)}) custom-call(bf16[1536,1152]{1,0:T(8,128)(2,1)S(1)} %convolution_convert_fusion.1.gi_ref, bf16[384,1536]{1,0:T(8,128)(2,1)S(1)} %convolution_convert_fusion.7.go_ref, ...), custom_call_target="tpu_custom_call" | custom-call | flops 2000000000 | bytes 20000000 | tf_op jit(solution)/shard_map/reduce_weights/pallas_call | solution.py:997
  567.9 3.5 slice.95
  (190 shorter events, 58.6 us)
Async XLA Ops:
  7.2 256.7 %copy-start = (bf16[1536,512]{1,0:T(8,128)(2,1)S(1)}, bf16[1536,512]{1,0:T(8,128)(2,1)}, u32[]{:S(2)}) copy-start(bf16[1536,512]{1,0:T(8,128)(2,1)} %param.25) | copy-start | bytes 4718596
  7.2 5.1 copy-start.12
  7.2 148.5 %all-gather.6.cloned.1.call-start = ((), (), s32[]{:S(2)}) async-start(), calls=%async_computation.2 | async-start | bytes 5308416 | tf_op jit(solution)/shard_map/all_gather | solution.py:1187
  9.4 58.1 %copy-start.23 = (f32[256]{0:T(256)}, f32[256]{0:T(256)S(1)}, u32[]{:S(2)}) copy-start(f32[256]{0:T(256)S(1)} %get-tuple-element.138) | copy-start | bytes 3076
  15.3 53.0 %copy-start.20 = (f32[16,6,11]{0,1,2:T(8,128)S(1)}, f32[16,6,11]{0,1,2:T(8,128)}, u32[]{:S(2)}) copy-start(f32[16,6,11]{0,1,2:T(8,128)} %param.19) | copy-start | bytes 12676
  15.3 54.2 %copy-start.21 = (s32[1,2048]{1,0:T(1,128)S(1)}, s32[1,2048]{1,0:T(1,128)}, u32[]{:S(2)}) copy-start(s32[1,2048]{1,0:T(1,128)} %param.15) | copy-start | bytes 24580
  15.3 54.2 %copy-start.22 = (s32[1,2048]{1,0:T(1,128)S(1)}, s32[1,2048]{1,0:T(1,128)}, u32[]{:S(2)}) copy-start(s32[1,2048]{1,0:T(1,128)} %param.16) | copy-start | bytes 24580
  15.3 55.3 %copy-start.26 = (f32[8,2,2]{0,2,1:T(2,128)S(1)}, f32[8,2,2]{0,2,1:T(2,128)}, u32[]{:S(2)}) copy-start(f32[8,2,2]{0,2,1:T(2,128)} %param.20) | copy-start | bytes 388
  67.5 127.6 %all-gather.8.cloned.1.call-start = ((), (), s32[]{:S(2)}) async-start(), calls=%async_computation.3 | async-start | bytes 7077888 | tf_op jit(solution)/shard_map/all_gather | solution.py:1189
  68.3 189.5 %all-gather.10.cloned.1.call-start = ((), (), s32[]{:S(2)}) async-start(), calls=%async_computation.4 | async-start | bytes 7077888 | tf_op jit(solution)/shard_map/all_gather | solution.py:1205
  74.7 5.2 copy-start.32
  188.5 5.5 copy-start.18
  195.1 157.4 %reduce-scatter.3.cloned.1.call-start = ((), (), s32[]{:S(2)}) async-start(), calls=%async_computation.5 | async-start | bytes 7077888 | tf_op jit(solution)/shard_map/reduce_scatter | solution.py:1218
  257.8 6.1 %copy-start.27 = (bf16[2048,1536]{1,0:T(8,128)(2,1)S(1)}, bf16[2048,1536]{1,0:T(8,128)(2,1)}, u32[]{:S(2)}) copy-start(bf16[2048,1536]{1,0:T(8,128)(2,1)} %all-gather.10.cloned.1.call-done) | copy-start | bytes 18874372
  257.8 6.3 %copy-start.36 = (f32[2048,512]{1,0:T(8,128)S(1)}, f32[2048,512]{1,0:T(8,128)}, u32[]{:S(2)}) copy-start(f32[2048,512]{1,0:T(8,128)} %fusion.42) | copy-start | bytes 12582916
  264.1 6.9 %copy-start.28 = (bf16[1536,512]{1,0:T(8,128)(2,1)S(1)}, bf16[1536,512]{1,0:T(8,128)(2,1)}, u32[]{:S(2)}) copy-start(bf16[1536,512]{1,0:T(8,128)(2,1)} %param.24) | copy-start | bytes 4718596
  283.8 292.3 %all-gather.12.cloned.1.call-start = ((), (), s32[]{:S(2)}) async-start(), calls=%async_computation.7 | async-start | bytes 5898240 | tf_op jit(solution)/shard_map/all_gather | solution.py:1229
  284.2 7.0 %copy-start.34 = (bf16[2048,512]{1,0:T(8,128)(2,1)S(1)}, bf16[2048,512]{1,0:T(8,128)(2,1)}, u32[]{:S(2)}) copy-start(bf16[2048,512]{1,0:T(8,128)(2,1)} %get-tuple-element.57) | copy-start | bytes 6291460
  284.2 13.6 %slice-start = ((s8[6291456]{0:T(1024)(128)(4,1)}), s8[4194304]{0:T(1024)(128)(4,1)S(1)}, s32[]{:S(2)}) async-start(s8[6291456]{0:T(1024)(128)(4,1)} %bitcast.167), calls=%async_computation.8 | async-start | bytes 8388608
  291.3 6.6 %slice-start.1 = ((s8[6291456]{0:T(1024)(128)(4,1)}), s8[2097152]{0:T(1024)(128)(4,1)S(1)}, s32[]{:S(2)}) async-start(s8[6291456]{0:T(1024)(128)(4,1)} %bitcast.167), calls=%async_computation.9 | async-start | bytes 4194304
  291.3 6.6 %copy-start.29 = (bf16[2048,512]{1,0:T(8,128)(2,1)S(1)}, bf16[2048,512]{1,0:T(8,128)(2,1)}, u32[]{:S(2)}) copy-start(bf16[2048,512]{1,0:T(8,128)(2,1)} %get-tuple-element.56) | copy-start | bytes 6291460
  352.5 223.6 %reduce-scatter.5.cloned.1.call-start = ((), (), s32[]{:S(2)}) async-start(), calls=%async_computation.6 | async-start | bytes 7077888 | tf_op jit(solution)/shard_map/reduce_scatter | solution.py:1227
  389.6 78.4 %copy-start.6 = (bf16[1024,384]{1,0:T(8,128)(2,1)S(1)}, bf16[1024,384]{1,0:T(8,128)(2,1)}, u32[]{:S(2)}) copy-start(bf16[1024,384]{1,0:T(8,128)(2,1)} %copy-done.5) | copy-start | bytes 2359300
  477.0 5.8 copy-start.2
  (21 other events, 57.8 us)
Sparse Core Ops, SparseCore 0:
  67.6 50.5 all-gather.5
  120.4 71.8 all-gather.7
  195.2 62.5 all-gather.9
  283.9 67.8 reduce-scatter.2
  353.4 58.2 all-gather.11
  413.9 66.9 reduce-scatter.4

commit v4 on v3

--- a/solution.py
+++ b/solution.py
@@ -1256,17 +1256,17 @@
     group_part = spread(cut_heads(dgain, dim)[0], width)
     parts = (kernel_part, mix_part, second_part, group_part)
     if direct:
-        flat = jnp.concatenate([jnp.zeros((width,), jnp.float32)] + [value.reshape(-1) for value in parts])
-        size = -(-flat.shape[0] // (8 * LANES)) * 8 * LANES
-        small = jnp.pad(flat, (0, size - flat.shape[0])).reshape(-1, LANES)
+        lines = lambda value: jnp.pad(value.reshape(-1), (0, -value.size % LANES)).reshape(-1, LANES)
+        small = jnp.concatenate([jnp.zeros((width // LANES, LANES), jnp.float32)] + [lines(value) for value in parts])
+        small = jnp.pad(small, ((0, -small.shape[0] % 8), (0, 0)))
         grad_input_w, grad_output_w, dnormin, small = reduce_weights(
             own_input_grad, own_output_grad, dnormin_part, resid_in * first_scale, small, reps, count
         )
-        flat = small.reshape(-1)
-        grad_first, others, start = flat[:width], [], width
+        grad_first, others, start = small[: width // LANES].reshape(-1), [], width // LANES
         for value in parts:
-            others.append(flat[start : start + value.size].reshape(value.shape))
-            start += value.size
+            size = -(-value.size // LANES)
+            others.append(small[start : start + size].reshape(-1)[: value.size].reshape(value.shape))
+            start += size
     else:
         dnormin = lax.psum_scatter(
             dnormin_part[EDGE : EDGE + FRAME], "seq", scatter_dimension=0, tiled=True, axis_index_groups=groups

time: 608 us -> 603 us (level)
  transfers between devices with their start and end apart: 6 -> 6, of which waited for: 1 -> 1; matrix products, arithmetic and copies ran while one was open for 15% -> 14% of each run, Pallas kernels for 55% -> 55%
where the time goes in v4:
time: 603 us; the launch traced here: 595 us
  Pallas kernels  381 us (63%)
  matrix products  87.1 us (14%)
  waiting for transfers between devices  54.9 us (9%)
  other arithmetic  30 us (5%)
  local copies, waits for them, and re-layouts  25.4 us (4%)
  between operations  15.2 us (3%)
    pallas_call x1, Pallas kernels, reduce_weights(): pl.pallas_call(functools.partial(reduce_kernel, reps, count), in_specs=[h...  82.8 us
    pallas_call x1, Pallas kernels, attention_backward(): pl.pallas_call(functools.partial(backward_kernel, dim, taps, span, mix.sh...  77.6 us
    pallas_call x1, Pallas kernels, attention_forward(): pl.pallas_call(functools.partial(forward_kernel, dim, taps, mix.shape[0])...  66.2 us
    all_gather x1, waiting for transfers between devices, on_device(): inputs_all = lax.all_gather(normed_mid, 'seq', axis=0, tiled=True)  53.8 us
    pallas_call x1, Pallas kernels, gather_weight(): pl.pallas_call(functools.partial(gather_kernel, reps, count), in_specs=[p...  52.1 us
    pallas_call x1, Pallas kernels, rep_sum(): pl.pallas_call(body, in_specs=[pl.BlockSpec(memory_space=pl.ANY)] * 3, ou...  42.8 us
    pallas_call x1, Pallas kernels, frame_swap(): pl.pallas_call(frame_swap_kernel, in_specs=[pl.BlockSpec(memory_space=pl....  32.8 us
    pallas_call x1, Pallas kernels, frame_gather(): pl.pallas_call(frame_gather_kernel, in_specs=[pl.BlockSpec(memory_space=p...  27 us
  transfers between devices with their start and end apart: 6, of which 1 were waited for; matrix products, arithmetic and copies ran while one was open for 14% of the time, Pallas kernels for 55%

profile of v4, /device:TPU:25, one launch (start us, length us, event | category | flops | bytes accessed | tf_op | source)
XLA Modules:
  0.0 594.9 jit_solution(4920525067868603274)
XLA Ops:
  15.3 52.1 %gather_weight.1 = (bf16[1536,1152]{1,0:T(8,128)(2,1)}, bf16[1152,1536]{1,0:T(8,128)(2,1)}) custom-call(bf16[192,4608]{1,0:T(8,128)(2,1)} %w_ref.1, bf16[256,1536]{1,0:T(8,128)(2,1)} %get-tuple-element.133.x_ref, bf16[64,1536]{1,0:T(8,128)(2,1)} %broadcast_in_dim.185.z_ref), custom_call_target="tpu_custom_call" | custom-call | flops 2000000000 | bytes 20000000 | tf_op jit(solution)/shard_map/gather_weight/pallas_call | solution.py:645
  79.8 4.9 convolution_convert_fusion.3.qs_ref.ks_ref.vs_ref
  85.0 66.2 %attend.1 = (bf16[1024,384]{1,0:T(8,128)(2,1)S(1)}, f32[1024,512]{1,0:T(8,128)S(1)}, f32[4,1024,1024]{2,1,0:T(8,128)}) custom-call(bf16[1152,1152]{1,0:T(8,128)(2,1)S(1)} %convolution_convert_fusion.3.qs_ref.ks_ref.vs_ref, bf16[1152,1152]{1,0:T(8,128)(2,1)S(1)} %convolution_convert_fusion.3.qs_ref.ks_ref.vs_ref, ...), custom_call_target="tpu_custom_call" | custom-call | flops 10000000000 | bytes 40000000 | tf_op jit(solution)/shard_map/attend/pallas_call | solution.py:366
  155.7 32.8 %frame_swap.1 = bf16[256,1536]{1,0:T(8,128)(2,1)} custom-call(bf16[1024,384]{1,0:T(8,128)(2,1)} %copy-done.5), custom_call_target="tpu_custom_call" | custom-call | flops 2000000000 | bytes 2000000 | tf_op jit(solution)/shard_map/frame_swap/pallas_call | solution.py:752
  188.5 4.3 multiply_reduce_fusion
  195.3 8.7 %fusion.41 = f32[2048,512]{1,0:T(8,128)} fusion(bf16[2048,1536]{1,0:T(8,128)(2,1)} %all-gather.8.cloned.1.call-done, bf16[512,1536]{1,0:T(8,128)(2,1)} %param.26), kind=kOutput, calls=%fused_computation.131 | convolution fusion | flops 3221225472 | bytes 12058624 | tf_op jit(solution)/shard_map/dot_general | solution.py:1208
  204.0 53.8 %all-gather.10.cloned.1.call-done = bf16[2048,1536]{1,0:T(8,128)(2,1)} async-done(((bf16[256,1536]{1,0:T(8,128)(2,1)}), bf16[2048,1536]{1,0:T(8,128)(2,1)}) %all-gather.10.cloned.1.call-update) | async-done | bytes 6291472 | tf_op jit(solution)/shard_map/all_gather | solution.py:1205
  257.7 6.1 %fusion.42 = f32[2048,512]{1,0:T(8,128)S(1)} fusion(bf16[2048,1536]{1,0:T(8,128)(2,1)} %all-gather.10.cloned.1.call-done, bf16[1536,512]{1,0:T(8,128)(2,1)} %param.24), kind=kOutput, calls=%fused_computation.132 | convolution fusion | flops 3221225472 | bytes 12058624 | tf_op jit(solution)/shard_map/dot_general | solution.py:1206
  264.1 6.9 %multiply_convert_fusion = (bf16[2048,512]{1,0:T(8,128)(2,1)}, bf16[2048,512]{1,0:T(8,128)(2,1)}, bf16[2048,512]{1,0:T(8,128)(2,1)}) fusion(f32[2048,512]{1,0:T(8,128)S(1)} %fusion.42, f32[2048,512]{1,0:T(8,128)S(1)} %copy-done.36, bf16[2048,1536]{1,0:T(8,128)(2,1)S(1)} %copy-done.27, bf16[1536,512]{1,0:T(8,128)(2,1)S(1)} %copy-done), kind=kOutput, calls=%fused_computation.8 | convolution fusion | flops 3238002688 | bytes 22544384 | tf_op jit(solution)/shard_map/dot_general | solution.py:1207
  271.0 5.1 fusion.43
  276.0 7.2 %add_convert_fusion = bf16[2048,1536]{1,0:T(8,128)(2,1)} fusion(f32[2048,1536]{1,0:T(8,128)S(1)} %fusion.43, bf16[2048,512]{1,0:T(8,128)(2,1)} %get-tuple-element.57, bf16[1536,512]{1,0:T(8,128)(2,1)S(1)} %copy-done), kind=kOutput, calls=%fused_computation | convolution fusion | flops 3227516928 | bytes 22544384 | tf_op jit(solution)/shard_map/dot_general | solution.py:1215
  283.8 7.0 %convolution_convert_fusion.4.refs_2_ = bf16[512,1536]{1,0:T(8,128)(2,1)S(1)} fusion(bf16[2048,512]{1,0:T(8,128)(2,1)} %get-tuple-element.55, bf16[2048,1536]{1,0:T(8,128)(2,1)} %all-gather.8.cloned.1.call-done), kind=kOutput, calls=%fused_computation.32 | convolution fusion | flops 3222011904 | bytes 9961472 | tf_op jit(solution)/shard_map/dot_general | solution.py:1221
  290.8 6.5 %convolution_convert_fusion.5.refs_1_ = bf16[1536,512]{1,0:T(8,128)(2,1)S(1)} fusion(bf16[2048,1536]{1,0:T(8,128)(2,1)} %all-gather.10.cloned.1.call-done, bf16[2048,512]{1,0:T(8,128)(2,1)S(1)} %copy-done.34), kind=kOutput, calls=%fused_computation.33 | convolution fusion | flops 3222011904 | bytes 9961472 | tf_op jit(solution)/shard_map/dot_general | solution.py:1221
  297.4 3.5 convolution_convert_fusion.6.refs_0_
  300.9 42.8 %rep_sum.1 = bf16[384,1536]{1,0:T(8,128)(2,1)} custom-call(bf16[1536,512]{1,0:T(8,128)(2,1)S(1)} %convolution_convert_fusion.6.refs_0_, bf16[1536,512]{1,0:T(8,128)(2,1)S(1)} %convolution_convert_fusion.5.refs_1_, bf16[512,1536]{1,0:T(8,128)(2,1)S(1)} %convolution_convert_fusion.4.refs_2_), custom_call_target="tpu_custom_call" | custom-call | flops 2000000000 | bytes 20000000 | tf_op jit(solution)/shard_map/rep_sum/pallas_call | solution.py:1100
  343.7 8.2 %convolution_convert_fusion.2 = bf16[2048,1536]{1,0:T(8,128)(2,1)} fusion(bf16[2048,512]{1,0:T(8,128)(2,1)} %get-tuple-element.55, bf16[512,1536]{1,0:T(8,128)(2,1)} %param.26), kind=kOutput, calls=%fused_computation.3 | convolution fusion | flops 3224371200 | bytes 9961472 | tf_op jit(solution)/shard_map/dot_general | solution.py:1219
  357.4 27.0 %frame_gather.1 = bf16[1024,1536]{1,0:T(8,128)(2,1)} custom-call(bf16[256,1536]{1,0:T(8,128)(2,1)} %multiply_convert_fusion.3.x_ref), custom_call_target="tpu_custom_call" | custom-call | flops 2000000000 | bytes 8000000 | tf_op jit(solution)/shard_map/frame_gather/pallas_call | solution.py:709
  384.4 4.4 fusion.25.dns_ref
  389.0 77.6 %attend_back.1 = (bf16[1152,1152]{1,0:T(8,128)(2,1)}, f32[4,16,768]{2,1,0:T(8,128)S(1)}, f32[2,8,128]{2,1,0:T(8,128)S(1)}, f32[1,512]{1,0:T(1,128)S(1)}) custom-call(bf16[1152,1152]{1,0:T(8,128)(2,1)} %copy-done.7, bf16[1152,1152]{1,0:T(8,128)(2,1)} %copy-done.7, bf16[1152,1152]{1,0:T(8,128)(2,1)} %copy-done.7, ...), custom_call_target="tpu_custom_call" | custom-call | flops 10000000000 | bytes 40000000 | tf_op jit(solution)/shard_map/attend_back/pallas_call | solution.py:414
  468.2 3.5 convolution_convert_fusion.7.go_ref
  472.1 5.0 convolution_convert_fusion.dn_ref
  477.1 5.7 convolution_convert_fusion.1.gi_ref
  482.9 82.8 %reduce_weights.1 = (bf16[192,4608]{1,0:T(8,128)(2,1)S(1)}, bf16[192,1536]{1,0:T(8,128)(2,1)S(1)}, f32[256,1536]{1,0:T(8,128)S(1)}, f32[48,128]{1,0:T(8,128)S(1)}) custom-call(bf16[1536,1152]{1,0:T(8,128)(2,1)S(1)} %convolution_convert_fusion.1.gi_ref, bf16[384,1536]{1,0:T(8,128)(2,1)S(1)} %convolution_convert_fusion.7.go_ref, ...), custom_call_target="tpu_custom_call" | custom-call | flops 2000000000 | bytes 20000000 | tf_op jit(solution)/shard_map/reduce_weights/pallas_call | solution.py:997
  576.6 3.1 copy.102
  (191 shorter events, 54.5 us)
Async XLA Ops:
  7.2 256.7 %copy-start = (bf16[1536,512]{1,0:T(8,128)(2,1)S(1)}, bf16[1536,512]{1,0:T(8,128)(2,1)}, u32[]{:S(2)}) copy-start(bf16[1536,512]{1,0:T(8,128)(2,1)} %param.25) | copy-start | bytes 4718596
  7.2 148.5 %all-gather.6.cloned.1.call-start = ((), (), s32[]{:S(2)}) async-start(), calls=%async_computation.2 | async-start | bytes 5308416 | tf_op jit(solution)/shard_map/all_gather | solution.py:1187
  9.3 58.1 %copy-start.23 = (f32[256]{0:T(256)}, f32[256]{0:T(256)S(1)}, u32[]{:S(2)}) copy-start(f32[256]{0:T(256)S(1)} %get-tuple-element.151) | copy-start | bytes 3076
  15.3 53.0 %copy-start.20 = (f32[16,6,11]{0,1,2:T(8,128)S(1)}, f32[16,6,11]{0,1,2:T(8,128)}, u32[]{:S(2)}) copy-start(f32[16,6,11]{0,1,2:T(8,128)} %param.19) | copy-start | bytes 12676
  15.3 54.2 %copy-start.21 = (s32[1,2048]{1,0:T(1,128)S(1)}, s32[1,2048]{1,0:T(1,128)}, u32[]{:S(2)}) copy-start(s32[1,2048]{1,0:T(1,128)} %param.15) | copy-start | bytes 24580
  15.3 54.2 %copy-start.22 = (s32[1,2048]{1,0:T(1,128)S(1)}, s32[1,2048]{1,0:T(1,128)}, u32[]{:S(2)}) copy-start(s32[1,2048]{1,0:T(1,128)} %param.16) | copy-start | bytes 24580
  15.3 55.3 %copy-start.26 = (f32[8,2,2]{0,2,1:T(2,128)S(1)}, f32[8,2,2]{0,2,1:T(2,128)}, u32[]{:S(2)}) copy-start(f32[8,2,2]{0,2,1:T(2,128)} %param.20) | copy-start | bytes 388
  67.4 127.6 %all-gather.8.cloned.1.call-start = ((), (), s32[]{:S(2)}) async-start(), calls=%async_computation.3 | async-start | bytes 7077888 | tf_op jit(solution)/shard_map/all_gather | solution.py:1189
  68.2 189.5 %all-gather.10.cloned.1.call-start = ((), (), s32[]{:S(2)}) async-start(), calls=%async_computation.4 | async-start | bytes 7077888 | tf_op jit(solution)/shard_map/all_gather | solution.py:1205
  74.7 5.2 copy-start.32
  188.5 5.5 copy-start.18
  195.0 156.8 %reduce-scatter.3.cloned.1.call-start = ((), (), s32[]{:S(2)}) async-start(), calls=%async_computation.5 | async-start | bytes 7077888 | tf_op jit(solution)/shard_map/reduce_scatter | solution.py:1218
  257.7 6.1 %copy-start.27 = (bf16[2048,1536]{1,0:T(8,128)(2,1)S(1)}, bf16[2048,1536]{1,0:T(8,128)(2,1)}, u32[]{:S(2)}) copy-start(bf16[2048,1536]{1,0:T(8,128)(2,1)} %all-gather.10.cloned.1.call-done) | copy-start | bytes 18874372
  257.7 6.3 %copy-start.36 = (f32[2048,512]{1,0:T(8,128)S(1)}, f32[2048,512]{1,0:T(8,128)}, u32[]{:S(2)}) copy-start(f32[2048,512]{1,0:T(8,128)} %fusion.41) | copy-start | bytes 12582916
  264.1 6.9 %copy-start.28 = (bf16[1536,512]{1,0:T(8,128)(2,1)S(1)}, bf16[1536,512]{1,0:T(8,128)(2,1)}, u32[]{:S(2)}) copy-start(bf16[1536,512]{1,0:T(8,128)(2,1)} %param.24) | copy-start | bytes 4718596
  283.3 288.1 %all-gather.12.cloned.1.call-start = ((), (), s32[]{:S(2)}) async-start(), calls=%async_computation.7 | async-start | bytes 5898240 | tf_op jit(solution)/shard_map/all_gather | solution.py:1229
  283.7 7.0 %copy-start.34 = (bf16[2048,512]{1,0:T(8,128)(2,1)S(1)}, bf16[2048,512]{1,0:T(8,128)(2,1)}, u32[]{:S(2)}) copy-start(bf16[2048,512]{1,0:T(8,128)(2,1)} %get-tuple-element.57) | copy-start | bytes 6291460
  283.7 13.6 %slice-start = ((s8[6291456]{0:T(1024)(128)(4,1)}), s8[4194304]{0:T(1024)(128)(4,1)S(1)}, s32[]{:S(2)}) async-start(s8[6291456]{0:T(1024)(128)(4,1)} %bitcast.178), calls=%async_computation.8 | async-start | bytes 8388608
  290.8 6.6 %slice-start.1 = ((s8[6291456]{0:T(1024)(128)(4,1)}), s8[2097152]{0:T(1024)(128)(4,1)S(1)}, s32[]{:S(2)}) async-start(s8[6291456]{0:T(1024)(128)(4,1)} %bitcast.178), calls=%async_computation.9 | async-start | bytes 4194304
  290.8 6.6 %copy-start.29 = (bf16[2048,512]{1,0:T(8,128)(2,1)S(1)}, bf16[2048,512]{1,0:T(8,128)(2,1)}, u32[]{:S(2)}) copy-start(bf16[2048,512]{1,0:T(8,128)(2,1)} %get-tuple-element.56) | copy-start | bytes 6291460
  351.9 219.4 %reduce-scatter.5.cloned.1.call-start = ((), (), s32[]{:S(2)}) async-start(), calls=%async_computation.6 | async-start | bytes 7077888 | tf_op jit(solution)/shard_map/reduce_scatter | solution.py:1227
  389.0 79.1 %copy-start.6 = (bf16[1024,384]{1,0:T(8,128)(2,1)S(1)}, bf16[1024,384]{1,0:T(8,128)(2,1)}, u32[]{:S(2)}) copy-start(bf16[1024,384]{1,0:T(8,128)(2,1)} %copy-done.5) | copy-start | bytes 2359300
  472.1 5.1 copy-start.31
  477.1 5.7 copy-start.2
  (21 other events, 58.0 us)
Sparse Core Ops, SparseCore 0:
  67.6 50.5 all-gather.5
  120.4 71.8 all-gather.7
  195.2 62.5 all-gather.9
  283.4 67.8 reduce-scatter.2
  352.9 58.2 all-gather.11
  413.4 66.9 reduce-scatter.4
